TPU v7x, 256 devices: a whole 4x4x8 slice. The times are simulated.
256 devices in a mesh: row: 16 (over z, core), col: 16 (over x, y).
Axes of the slice: x: 4, y: 4, z: 8, core: 2. Of those that a mesh axis runs over, the one named last changes fastest.
Arguments:
- cost_tiles: float32 [16, 16, 64, 128, 128], P('row', 'col'), may hold values from 0 to 66
- tile_rows: int32 [16, 16, 64], P('row', 'col'), may hold values from 0 to 127, as said below
- tile_cols: int32 [16, 16, 64], P('row', 'col'), may hold values from 0 to 127
- tile_count: int32 [16, 16], P('row', 'col'), may hold values from 16 to 64, as said below
- source_logmass: float32 [262144], P('row'), may hold values from -3 to 0
- target_logmass: float32 [262144], P('col'), may hold values from -103 to -100
- target_init: float32 [262144], P('col'), may hold values from -2 to 14
Outputs:
- source_potential: float32 [262144], P('row')
- target_potential: float32 [262144], P('col')
Inputs may be any that keep to these rules, and one draw needn't show every extreme that they name: Among the first tile_count slots of a device all (tile_rows, tile_cols) pairs differ; every source block of a row shard appears in such a slot of some device of that shard, and every target block of a col shard likewise. Slots at tile_count or later hold pairs to be ignored. `tile_count`: some device has all 64 slots in use in every draw.
All inputs are finite; a program needn't handle non-finite values.
Results may differ from a plain program's by a relative error of at most 0.00019.
Values sent between devices are 32-bit elements; how exact they have to be, the bound alone decides.
No kernel may reach another device: no remote copies, remote signals or barrier semaphores. Data moves between devices by JAX's collectives and lax.ppermute only.
A program may use at most 64 MiB of HBM per device.

v0:
```python
import jax
import jax.numpy as jnp
from jax import lax
from jax.sharding import PartitionSpec as P

ITERS = 2


EPS = 0.1


def copy_for_each(shard, axis):
    peers = lax.axis_size(axis)
    return lax.all_to_all(
        jnp.broadcast_to(shard[None], (peers, *shard.shape)), axis, 0, 0, tiled=True
    )


def of_everyone(shard, axis):
    everything = copy_for_each(shard, axis)
    return jnp.max(everything, axis=0)


def cut_along(shard, dim, peers):
    before, after = (shard.shape[:dim], shard.shape[dim + 1 :])
    return jnp.moveaxis(shard.reshape(*before, peers, -1, *after), dim, 0)


def sent_and_summed(shard, axis, dim):
    peers = lax.axis_size(axis)
    parts = lax.all_to_all(cut_along(shard, dim, peers), axis, 0, 0, tiled=True)
    return jnp.sum(parts, axis=0)


def in_order(parts, dim):
    shape = list(parts.shape[1:])
    shape[dim] *= parts.shape[0]
    return jnp.moveaxis(parts, 0, dim).reshape(shape)


def gathered_copies(shard, axis, dim):
    parts = copy_for_each(shard, axis)
    return in_order(parts, dim)


def block_stats(cost, pot_blocks, gather_ids, seg_ids, valid, nseg, rows_side):
    red = 2 if rows_side else 1
    part = pot_blocks[gather_ids]
    if rows_side:
        scores = (part[:, None, :] - cost) / EPS
    else:
        scores = (part[:, :, None] - cost) / EPS
    tmax = jnp.where(valid[:, None], jnp.max(scores, axis=red), -jnp.inf)
    onehot = (seg_ids[:, None] == jnp.arange(nseg)[None, :]) & valid[:, None]
    peak = jnp.max(jnp.where(onehot.T[:, :, None], tmax[None, :, :], -jnp.inf), axis=1)
    shift = jnp.where(valid[:, None], peak[seg_ids], 0.0)
    if rows_side:
        expo = jnp.exp(scores - shift[:, :, None])
    else:
        expo = jnp.exp(scores - shift[:, None, :])
    tsum = jnp.where(valid[:, None], jnp.sum(expo, axis=red), 0.0)
    mass = jnp.dot(
        onehot.astype(jnp.float32).T,
        tsum,
        precision=lax.Precision.HIGHEST,
        preferred_element_type=jnp.float32,
    )
    return (peak, mass)


def local_stats(cost, pot, gather_ids, seg_ids, count, nseg, rows_side):
    pot_blocks = pot.reshape(-1, cost.shape[-1])
    slots = cost.shape[0]
    valid = jnp.arange(slots) < count
    return block_stats(cost, pot_blocks, gather_ids, seg_ids, valid, nseg, rows_side)


def finish_source(peak, mass, logmass):
    top = of_everyone(peak, "col")
    scaled = mass * jnp.exp(peak - top)
    share = sent_and_summed(scaled.reshape(-1), "col", 0)
    width = share.shape[0]
    start = lax.axis_index("col") * width
    top_share = lax.dynamic_slice_in_dim(top.reshape(-1), start, width, 0)
    mass_share = lax.dynamic_slice_in_dim(logmass, start, width, 0)
    piece = EPS * mass_share - EPS * (top_share + jnp.log(share))
    return gathered_copies(piece, "col", 0)


def finish_target(peak, mass, logmass):
    top = of_everyone(peak, "row")
    scaled = mass * jnp.exp(peak - top)
    share = sent_and_summed(scaled.reshape(-1), "row", 0)
    width = share.shape[0]
    start = lax.axis_index("row") * width
    top_share = lax.dynamic_slice_in_dim(top.reshape(-1), start, width, 0)
    mass_share = lax.dynamic_slice_in_dim(logmass, start, width, 0)
    piece = EPS * mass_share - EPS * (top_share + jnp.log(share))
    return lax.all_gather(piece, "row", axis=0, tiled=True)


def local(
    cost_tiles, tile_rows, tile_cols, tile_count, source_logmass, target_logmass, target_init
):
    width = cost_tiles.shape[-1]
    cost = cost_tiles.reshape(cost_tiles.shape[2], width, width)
    rows = tile_rows.reshape(-1)
    cols = tile_cols.reshape(-1)
    count = tile_count.reshape(())
    src_blocks = source_logmass.shape[0] // width
    tgt_blocks = target_logmass.shape[0] // width
    target_potential = target_init
    source_potential = source_logmass
    for step in range(ITERS):
        peak, mass = local_stats(cost, target_potential, cols, rows, count, src_blocks, True)
        source_potential = finish_source(peak, mass, source_logmass)
        peak, mass = local_stats(cost, source_potential, rows, cols, count, tgt_blocks, False)
        target_potential = finish_target(peak, mass, target_logmass)
    return (source_potential, target_potential)


def solution(mesh):
    return jax.shard_map(
        local,
        mesh=mesh,
        in_specs=(
            P("row", "col", None, None, None),
            P("row", "col", None),
            P("row", "col", None),
            P("row", "col"),
            P("row"),
            P("col"),
            P("col"),
        ),
        out_specs=(P("row"), P("col")),
        check_vma=False,
    )
```

profile of v0, /device:TPU:1, one launch (start us, length us, event | category | flops | bytes accessed | tf_op | source)
XLA Modules:
  0.0 249.2 jit_solution(4396380979940419612)
XLA Ops:
  2.6 3.3 %fusion.7 = f32[64,128]{1,0:T(8,128)S(1)} fusion(f32[1,1,64,128,128]{4,3,2,1,0:T(8,128)} %param.7, f32[64,128]{1,0:T(8,128)S(1)} %gather_fusion), kind=kLoop, calls=%fused_computation.27 | loop fusion | flops 3137536 | bytes 4259840 | tf_op jit(solution)/shard_map/reduce_max | solution.py:53
  6.1 1.6 select_reduce_fusion.3
  7.7 1.1 broadcast_in_dim.190
  8.8 7.6 %all-to-all-start = ((f32[16,128,128]{2,1,0:T(8,128)}), f32[16,128,128]{2,1,0:T(8,128)S(1)}, u32[]{:S(2)}, u32[]{:S(2)}) async-start(f32[16,128,128]{2,1,0:T(8,128)} %broadcast_in_dim.190), calls=%async_computation | async-start | bytes 2097152 | tf_op jit(solution)/shard_map/all_to_all | solution.py:14
  17.1 4.0 %exponential_reduce_fusion.3 = f32[64,128]{1,0:T(8,128)S(1)} fusion(f32[1,1,64,128,128]{4,3,2,1,0:T(8,128)} %param.7, f32[64,128]{1,0:T(8,128)S(1)} %broadcast_select_fusion.3, f32[64,128]{1,0:T(8,128)S(1)} %gather_fusion), kind=kLoop, calls=%fused_computation.22 | loop fusion | flops 4186112 | bytes 4292608 | tf_op jit(solution)/shard_map/reduce_sum | solution.py:61
  21.1 11.0 %all-to-all-done = f32[16,128,128]{2,1,0:T(8,128)S(1)} async-done(((f32[16,128,128]{2,1,0:T(8,128)}), f32[16,128,128]{2,1,0:T(8,128)S(1)}, u32[]{:S(2)}, u32[]{:S(2)}) %all-to-all-start) | async-done | bytes 1048608 | tf_op jit(solution)/shard_map/all_to_all | solution.py:14
  33.1 3.9 %all-to-all-start.1 = ((f32[16,1,1024]{2,1,0:T(1,128)}), f32[16,1,1024]{2,1,0:T(1,128)S(1)}, u32[]{:S(2)}, u32[]{:S(2)}) async-start(f32[16,1,1024]{2,1,0:T(1,128)} %bitcast.10), calls=%async_computation.1 | async-start | bytes 131072 | tf_op jit(solution)/shard_map/all_to_all | solution.py:31
  37.0 6.5 %all-to-all-done.1 = f32[16,1,1024]{2,1,0:T(1,128)S(1)} async-done(((f32[16,1,1024]{2,1,0:T(1,128)}), f32[16,1,1024]{2,1,0:T(1,128)S(1)}, u32[]{:S(2)}, u32[]{:S(2)}) %all-to-all-start.1) | async-done | bytes 65568 | tf_op jit(solution)/shard_map/all_to_all | solution.py:31
  44.3 9.5 %all_to_all.68 = f32[16,1,1024]{2,1,0:T(1,128)S(1)} all-to-all(f32[16,1,1024]{2,1,0:T(1,128)S(1)} %broadcast_in_dim.192), channel_id=1, replica_groups=mesh['row'=16,'col'=16] {'col'}, dimensions={0} | all-to-all | bytes 131072 | tf_op jit(solution)/shard_map/all_to_all | solution.py:14
  54.4 2.8 %fusion.6 = f32[64,128]{1,0:T(8,128)S(1)} fusion(f32[1,1,64,128,128]{4,3,2,1,0:T(8,128)} %param.7, f32[64,128]{1,0:T(8,128)S(1)} %gather_fusion.2), kind=kLoop, calls=%fused_computation.26 | loop fusion | flops 3137536 | bytes 4259840 | tf_op jit(solution)/shard_map/reduce_max | solution.py:53
  57.3 1.6 select_reduce_fusion.2
  60.0 13.7 %all-to-all-start.3 = ((f32[16,128,128]{2,1,0:T(8,128)}), f32[16,128,128]{2,1,0:T(8,128)S(1)}, u32[]{:S(2)}, u32[]{:S(2)}) async-start(f32[16,128,128]{2,1,0:T(8,128)} %broadcast_in_dim.194), calls=%async_computation.3 | async-start | bytes 2097152 | tf_op jit(solution)/shard_map/all_to_all | solution.py:14
  74.3 2.9 %exponential_reduce_fusion.2 = f32[64,128]{1,0:T(8,128)S(1)} fusion(f32[1,1,64,128,128]{4,3,2,1,0:T(8,128)} %param.7, f32[64,128]{1,0:T(8,128)S(1)} %broadcast_select_fusion.2, f32[64,128]{1,0:T(8,128)S(1)} %gather_fusion.2), kind=kLoop, calls=%fused_computation.20 | loop fusion | flops 4186112 | bytes 4292608 | tf_op jit(solution)/shard_map/reduce_sum | solution.py:61
  77.3 24.4 %all-to-all-done.3 = f32[16,128,128]{2,1,0:T(8,128)S(1)} async-done(((f32[16,128,128]{2,1,0:T(8,128)}), f32[16,128,128]{2,1,0:T(8,128)S(1)}, u32[]{:S(2)}, u32[]{:S(2)}) %all-to-all-start.3) | async-done | bytes 1048608 | tf_op jit(solution)/shard_map/all_to_all | solution.py:14
  102.7 3.4 %all-to-all-start.4 = ((f32[16,1,1024]{2,1,0:T(1,128)}), f32[16,1,1024]{2,1,0:T(1,128)S(1)}, u32[]{:S(2)}, u32[]{:S(2)}) async-start(f32[16,1,1024]{2,1,0:T(1,128)} %bitcast.13), calls=%async_computation.4 | async-start | bytes 131072 | tf_op jit(solution)/shard_map/all_to_all | solution.py:31
  106.1 7.8 %all-to-all-done.4 = f32[16,1,1024]{2,1,0:T(1,128)S(1)} async-done(((f32[16,1,1024]{2,1,0:T(1,128)}), f32[16,1,1024]{2,1,0:T(1,128)S(1)}, u32[]{:S(2)}, u32[]{:S(2)}) %all-to-all-start.4) | async-done | bytes 65568 | tf_op jit(solution)/shard_map/all_to_all | solution.py:31
  114.6 14.9 %all_gather.6 = f32[16384]{0:T(1024)S(1)} all-gather(f32[1024]{0:T(1024)S(1)} %multiply_subtract_fusion.2), channel_id=1, replica_groups=mesh['row'=16,'col'=16] {'row'}, dimensions={0}, use_global_device_ids=true | all-gather | bytes 69632 | tf_op jit(solution)/shard_map/all_gather | solution.py:99
  130.1 3.3 %fusion.5 = f32[64,128]{1,0:T(8,128)S(1)} fusion(f32[1,1,64,128,128]{4,3,2,1,0:T(8,128)} %param.7, f32[64,128]{1,0:T(8,128)S(1)} %gather_fusion.4), kind=kLoop, calls=%fused_computation.25 | loop fusion | flops 3137536 | bytes 4259840 | tf_op jit(solution)/shard_map/reduce_max | solution.py:53
  133.5 1.6 select_reduce_fusion.1
  136.2 3.7 %all-to-all-start.5 = ((f32[16,128,128]{2,1,0:T(8,128)}), f32[16,128,128]{2,1,0:T(8,128)S(1)}, u32[]{:S(2)}, u32[]{:S(2)}) async-start(f32[16,128,128]{2,1,0:T(8,128)} %broadcast_in_dim.196), calls=%async_computation.5 | async-start | bytes 2097152 | tf_op jit(solution)/shard_map/all_to_all | solution.py:14
  140.6 4.0 %exponential_reduce_fusion.1 = f32[64,128]{1,0:T(8,128)S(1)} fusion(f32[1,1,64,128,128]{4,3,2,1,0:T(8,128)} %param.7, f32[64,128]{1,0:T(8,128)S(1)} %broadcast_select_fusion.1, f32[64,128]{1,0:T(8,128)S(1)} %gather_fusion.4), kind=kLoop, calls=%fused_computation.18 | loop fusion | flops 4186112 | bytes 4292608 | tf_op jit(solution)/shard_map/reduce_sum | solution.py:61
  144.5 12.5 %all-to-all-done.5 = f32[16,128,128]{2,1,0:T(8,128)S(1)} async-done(((f32[16,128,128]{2,1,0:T(8,128)}), f32[16,128,128]{2,1,0:T(8,128)S(1)}, u32[]{:S(2)}, u32[]{:S(2)}) %all-to-all-start.5) | async-done | bytes 1048608 | tf_op jit(solution)/shard_map/all_to_all | solution.py:14
  157.4 9.8 %all_to_all.69 = f32[16,1,1024]{2,1,0:T(1,128)S(1)} all-to-all(f32[16,1,1024]{2,1,0:T(1,128)S(1)} %bitcast.63), channel_id=1, replica_groups=mesh['row'=16,'col'=16] {'col'}, dimensions={0} | all-to-all | bytes 131072 | tf_op jit(solution)/shard_map/all_to_all | solution.py:31
  168.0 9.8 %all_to_all.70 = f32[16,1,1024]{2,1,0:T(1,128)S(1)} all-to-all(f32[16,1,1024]{2,1,0:T(1,128)S(1)} %broadcast_in_dim.197), channel_id=1, replica_groups=mesh['row'=16,'col'=16] {'col'}, dimensions={0} | all-to-all | bytes 131072 | tf_op jit(solution)/shard_map/all_to_all | solution.py:14
  178.4 2.8 %fusion.4 = f32[64,128]{1,0:T(8,128)S(1)} fusion(f32[1,1,64,128,128]{4,3,2,1,0:T(8,128)} %param.7, f32[64,128]{1,0:T(8,128)S(1)} %gather_fusion.6), kind=kLoop, calls=%fused_computation.24 | loop fusion | flops 3137536 | bytes 4259840 | tf_op jit(solution)/shard_map/reduce_max | solution.py:53
  181.3 1.6 select_reduce_fusion
  184.0 8.1 %all-to-all-start.8 = ((f32[16,128,128]{2,1,0:T(8,128)}), f32[16,128,128]{2,1,0:T(8,128)S(1)}, u32[]{:S(2)}, u32[]{:S(2)}) async-start(f32[16,128,128]{2,1,0:T(8,128)} %broadcast_in_dim.199), calls=%async_computation.8 | async-start | bytes 2097152 | tf_op jit(solution)/shard_map/all_to_all | solution.py:14
  192.8 2.9 %exponential_reduce_fusion = f32[64,128]{1,0:T(8,128)S(1)} fusion(f32[1,1,64,128,128]{4,3,2,1,0:T(8,128)} %param.7, f32[64,128]{1,0:T(8,128)S(1)} %broadcast_select_fusion, f32[64,128]{1,0:T(8,128)S(1)} %gather_fusion.6), kind=kLoop, calls=%fused_computation.16 | loop fusion | flops 4186112 | bytes 4292608 | tf_op jit(solution)/shard_map/reduce_sum | solution.py:61
  195.7 24.4 %all-to-all-done.8 = f32[16,128,128]{2,1,0:T(8,128)S(1)} async-done(((f32[16,128,128]{2,1,0:T(8,128)}), f32[16,128,128]{2,1,0:T(8,128)S(1)}, u32[]{:S(2)}, u32[]{:S(2)}) %all-to-all-start.8) | async-done | bytes 1048608 | tf_op jit(solution)/shard_map/all_to_all | solution.py:14
  221.1 3.4 %all-to-all-start.9 = ((f32[16,1,1024]{2,1,0:T(1,128)}), f32[16,1,1024]{2,1,0:T(1,128)S(1)}, u32[]{:S(2)}, u32[]{:S(2)}) async-start(f32[16,1,1024]{2,1,0:T(1,128)} %bitcast.20), calls=%async_computation.9 | async-start | bytes 131072 | tf_op jit(solution)/shard_map/all_to_all | solution.py:31
  224.5 7.8 %all-to-all-done.9 = f32[16,1,1024]{2,1,0:T(1,128)S(1)} async-done(((f32[16,1,1024]{2,1,0:T(1,128)}), f32[16,1,1024]{2,1,0:T(1,128)S(1)}, u32[]{:S(2)}, u32[]{:S(2)}) %all-to-all-start.9) | async-done | bytes 65568 | tf_op jit(solution)/shard_map/all_to_all | solution.py:31
  233.1 14.9 %all_gather.7 = f32[16384]{0:T(1024)S(1)} all-gather(f32[1024]{0:T(1024)S(1)} %multiply_subtract_fusion), channel_id=1, replica_groups=mesh['row'=16,'col'=16] {'row'}, dimensions={0}, use_global_device_ids=true | all-gather | bytes 69632 | tf_op jit(solution)/shard_map/all_gather | solution.py:99
  (51 shorter events, 17.2 us)
Async XLA Ops:
  0.6 1.4 copy-start
  0.6 5.4 %copy-start.2 = (s32[1,1,64]{2,1,0:T(1,128)S(1)}, s32[1,1,64]{2,1,0:T(1,128)}, u32[]{:S(2)}) copy-start(s32[1,1,64]{2,1,0:T(1,128)} %param.9) | copy-start | bytes 772
  0.7 5.4 %copy-start.1 = (s32[1,1,64]{2,1,0:T(1,128)S(1)}, s32[1,1,64]{2,1,0:T(1,128)}, u32[]{:S(2)}) copy-start(s32[1,1,64]{2,1,0:T(1,128)} %param.8) | copy-start | bytes 772
  8.8 23.2 %all-to-all-start = ((f32[16,128,128]{2,1,0:T(8,128)}), f32[16,128,128]{2,1,0:T(8,128)S(1)}, u32[]{:S(2)}, u32[]{:S(2)}) async-start(f32[16,128,128]{2,1,0:T(8,128)} %broadcast_in_dim.190), calls=%async_computation | async-start | bytes 2097152 | tf_op jit(solution)/shard_map/all_to_all | solution.py:14
  33.1 10.4 %all-to-all-start.1 = ((f32[16,1,1024]{2,1,0:T(1,128)}), f32[16,1,1024]{2,1,0:T(1,128)S(1)}, u32[]{:S(2)}, u32[]{:S(2)}) async-start(f32[16,1,1024]{2,1,0:T(1,128)} %bitcast.10), calls=%async_computation.1 | async-start | bytes 131072 | tf_op jit(solution)/shard_map/all_to_all | solution.py:31
  60.0 41.7 %all-to-all-start.3 = ((f32[16,128,128]{2,1,0:T(8,128)}), f32[16,128,128]{2,1,0:T(8,128)S(1)}, u32[]{:S(2)}, u32[]{:S(2)}) async-start(f32[16,128,128]{2,1,0:T(8,128)} %broadcast_in_dim.194), calls=%async_computation.3 | async-start | bytes 2097152 | tf_op jit(solution)/shard_map/all_to_all | solution.py:14
  102.7 11.2 %all-to-all-start.4 = ((f32[16,1,1024]{2,1,0:T(1,128)}), f32[16,1,1024]{2,1,0:T(1,128)S(1)}, u32[]{:S(2)}, u32[]{:S(2)}) async-start(f32[16,1,1024]{2,1,0:T(1,128)} %bitcast.13), calls=%async_computation.4 | async-start | bytes 131072 | tf_op jit(solution)/shard_map/all_to_all | solution.py:31
  136.2 20.8 %all-to-all-start.5 = ((f32[16,128,128]{2,1,0:T(8,128)}), f32[16,128,128]{2,1,0:T(8,128)S(1)}, u32[]{:S(2)}, u32[]{:S(2)}) async-start(f32[16,128,128]{2,1,0:T(8,128)} %broadcast_in_dim.196), calls=%async_computation.5 | async-start | bytes 2097152 | tf_op jit(solution)/shard_map/all_to_all | solution.py:14
  184.0 36.1 %all-to-all-start.8 = ((f32[16,128,128]{2,1,0:T(8,128)}), f32[16,128,128]{2,1,0:T(8,128)S(1)}, u32[]{:S(2)}, u32[]{:S(2)}) async-start(f32[16,128,128]{2,1,0:T(8,128)} %broadcast_in_dim.199), calls=%async_computation.8 | async-start | bytes 2097152 | tf_op jit(solution)/shard_map/all_to_all | solution.py:14
  221.1 11.2 %all-to-all-start.9 = ((f32[16,1,1024]{2,1,0:T(1,128)}), f32[16,1,1024]{2,1,0:T(1,128)S(1)}, u32[]{:S(2)}, u32[]{:S(2)}) async-start(f32[16,1,1024]{2,1,0:T(1,128)} %bitcast.20), calls=%async_computation.9 | async-start | bytes 131072 | tf_op jit(solution)/shard_map/all_to_all | solution.py:31
where the time goes:
time: 250 us; the launch traced here: 249 us
  waiting for transfers between devices  94.4 us (38%)
  blocking collectives  58.7 us (23%)
  starting transfers between devices  43.8 us (18%)
  other arithmetic  37.1 us (15%)
  local copies, waits for them, and re-layouts  10.5 us (4%)
  matrix products  3.19 us (1%)
    all_to_all x4, waiting for transfers between devices, copy_for_each(): lax.all_to_all(jnp.broadcast_to(shard[None], (peers, *shard.shape)), axis...  72.3 us
    all_to_all x4, starting transfers between devices, copy_for_each(): lax.all_to_all(jnp.broadcast_to(shard[None], (peers, *shard.shape)), axis...  33 us
    all_gather x2, blocking collectives, finish_target(): return lax.all_gather(piece, 'row', axis=0, tiled=True)  29.7 us
    all_to_all x3, waiting for transfers between devices, sent_and_summed(): parts = lax.all_to_all(cut_along(shard, dim, peers), axis, 0, 0, tiled=True)  22.1 us
    all_to_all x2, blocking collectives, copy_for_each(): lax.all_to_all(jnp.broadcast_to(shard[None], (peers, *shard.shape)), axis...  19.2 us
    reduce_sum x4, other arithmetic, block_stats(): tsum = jnp.where(valid[:, None], jnp.sum(expo, axis=red), 0.0)  13.8 us
    reduce_max x4, other arithmetic, block_stats(): tmax = jnp.where(valid[:, None], jnp.max(scores, axis=red), -jnp.inf)  12.4 us
    all_to_all x3, starting transfers between devices, sent_and_summed(): parts = lax.all_to_all(cut_along(shard, dim, peers), axis, 0, 0, tiled=True)  10.8 us
  transfers between devices with their start and end apart: 7, of which 7 were waited for; matrix products, arithmetic and copies ran while one was open for 7% of the time, Pallas kernels for 0%

commit v1 on v0

v1 whole, which is shorter than its diff:
```python
import jax
import jax.numpy as jnp
import numpy as np
from jax import lax
from jax.experimental import pallas as pl
from jax.experimental.pallas import tpu as pltpu
from jax.sharding import Mesh
from jax.sharding import PartitionSpec as P

ITERS = 2
EPS = 0.1
LN2 = float(np.log(2.0))
UNIT = 1.0 / (EPS * LN2)
BACK = EPS * LN2
NONE = -1.0e30
LANES = 128
WAYS = 4
CHUNK = 8


def lse2(parts):
    top = jnp.max(parts, axis=0)
    return top + jnp.log2(jnp.sum(jnp.exp2(parts - top[None]), axis=0))


def merge_slots(values, seg_ref, count, peak, mass):
    slots = values.shape[0]
    nseg = peak.shape[1] - 8

    def home(s):
        return jnp.where(s < count, seg_ref[s], nseg)

    peak[...] = jnp.full(peak.shape, NONE, jnp.float32)
    mass[...] = jnp.zeros(mass.shape, jnp.float32)
    for s in range(slots):
        at = (s % WAYS, pl.ds(home(s), 1), slice(None))
        peak[at] = jnp.maximum(peak[at], values[pl.ds(s, 1), :])
    top = peak[0]
    for way in range(1, WAYS):
        top = jnp.maximum(top, peak[way])
    peak[0] = top
    for s in range(slots):
        row = pl.ds(home(s), 1)
        at = (s % WAYS, row, slice(None))
        mass[at] = mass[at] + jnp.exp2(values[pl.ds(s, 1), :] - peak[0, row, :])
    total = mass[0]
    for way in range(1, WAYS):
        total = total + mass[way]
    dense = jnp.maximum(top + jnp.log2(total), NONE)
    return dense[:nseg]


def fetch_all(cost_hbm, cost, sems):
    for k in range(cost.shape[0] // CHUNK):
        at = pl.ds(k * CHUNK, CHUNK)
        pltpu.make_async_copy(cost_hbm.at[at], cost.at[at], sems.at[k]).start()


def fetch_wait(cost_hbm, cost, sems, k):
    at = pl.ds(k * CHUNK, CHUNK)
    pltpu.make_async_copy(cost_hbm.at[at], cost.at[at], sems.at[k]).wait()


def rows_side(rows, cols, count, cost_hbm, cost, sems, pot, values, peak, mass):
    slots = cost.shape[0]
    lane = lax.broadcasted_iota(jnp.int32, (LANES, LANES), 1)

    def one(s, held):
        part = pot[pl.ds(cols[s], 1), :]
        scores = (part - cost[s]) * UNIT
        top = jnp.max(scores, axis=1, keepdims=True)
        total = jnp.sum(jnp.exp2(scores - top), axis=1, keepdims=True)
        return jnp.where(lane == s, top + jnp.log2(total), held)

    def chunk(k, held):
        fetch_wait(cost_hbm, cost, sems, k)
        for i in range(CHUNK):
            held = one(k * CHUNK + i, held)
        return held

    held = lax.fori_loop(0, slots // CHUNK, chunk, jnp.zeros((LANES, LANES), jnp.float32))
    values[...] = held.T[:slots]
    return merge_slots(values, rows, count, peak, mass)


def cols_side(rows, cols, count, cost_hbm, cost, sems, pot, values, peak, mass):
    slots = cost.shape[0]
    eye = lax.broadcasted_iota(jnp.int32, (LANES, LANES), 1) == lax.broadcasted_iota(
        jnp.int32, (LANES, LANES), 0
    )

    def one(s):
        part = pot[pl.ds(rows[s], 1), :]
        upright = jnp.sum(jnp.where(eye, part, 0.0), axis=1, keepdims=True)
        scores = (upright - cost[s]) * UNIT
        top = jnp.max(scores, axis=0, keepdims=True)
        total = jnp.sum(jnp.exp2(scores - top), axis=0, keepdims=True)
        values[pl.ds(s, 1), :] = top + jnp.log2(total)

    def chunk(k, carry):
        fetch_wait(cost_hbm, cost, sems, k)
        for i in range(CHUNK):
            one(k * CHUNK + i)
        return carry

    lax.fori_loop(0, slots // CHUNK, chunk, 0)
    return merge_slots(values, cols, count, peak, mass)


def first_rows_kernel(rows, cols, count, cost_hbm, pot_in, out, cost, sems, values, peak, mass):
    fetch_all(cost_hbm, cost, sems)
    out[...] = rows_side(
        rows, cols, count[0, 0], cost_hbm, cost, sems, pot_in, values, peak, mass
    )


def rows_kernel(
    rows, cols, count, core, cost_hbm, mine, other, logmass, out, cost, sems, values, peak, mass, pot
):
    fetch_all(cost_hbm, cost, sems)
    half = mine.shape[0]
    at = pl.multiple_of(core[0] * half, half)
    away = pl.multiple_of((1 - core[0]) * half, half)
    pot[pl.ds(at, half), :] = EPS * logmass[pl.ds(at, half), :] - BACK * mine[...]
    pot[pl.ds(away, half), :] = EPS * logmass[pl.ds(away, half), :] - BACK * other[...]
    out[...] = rows_side(
        rows, cols, count[0, 0], cost_hbm, cost, sems, pot, values, peak, mass
    )


def cols_kernel(
    rows, cols, count, core, cost_hbm, parts, logmass, pot, keep, send, cost, sems, values, peak, mass, dense
):
    fetch_all(cost_hbm, cost, sems)
    pot[...] = EPS * logmass[...] - BACK * lse2(parts[...])
    dense[...] = cols_side(
        rows, cols, count[0, 0], cost_hbm, cost, sems, pot, values, peak, mass
    )
    half = keep.shape[0]
    keep[...] = dense[pl.ds(pl.multiple_of(core[0] * half, half), half), :]
    send[...] = dense[pl.ds(pl.multiple_of((1 - core[0]) * half, half), half), :]


def call(kernel, name, smem, hbm, vmem, outs, nseg, extra):
    slots = hbm.shape[0]
    smem_spec = pl.BlockSpec(memory_space=pltpu.SMEM)
    vmem_spec = pl.BlockSpec(memory_space=pltpu.VMEM)
    single = len(outs) == 1
    return pl.pallas_call(
        kernel,
        name=name,
        out_shape=outs[0] if single else outs,
        in_specs=[smem_spec] * len(smem) + [pl.BlockSpec(memory_space=pl.ANY)] + [vmem_spec] * len(vmem),
        out_specs=vmem_spec if single else tuple(vmem_spec for _ in outs),
        scratch_shapes=[
            pltpu.VMEM(hbm.shape, jnp.float32),
            pltpu.SemaphoreType.DMA((slots // CHUNK,)),
            pltpu.VMEM((slots, LANES), jnp.float32),
            pltpu.VMEM((WAYS, nseg + 8, LANES), jnp.float32),
            pltpu.VMEM((WAYS, nseg + 8, LANES), jnp.float32),
            *extra,
        ],
        compiler_params=pltpu.CompilerParams(vmem_limit_bytes=24 << 20),
    )(*smem, hbm, *vmem)


def to_all(value, axes, peers):
    copies = jnp.broadcast_to(value[None], (peers, *value.shape))
    return lax.all_to_all(copies, axes, 0, 0, tiled=True)


def local(
    cost_tiles, tile_rows, tile_cols, tile_count, source_logmass, target_logmass, target_init
):
    cost = cost_tiles.reshape(cost_tiles.shape[2:])
    rows = tile_rows.reshape(-1)
    cols = tile_cols.reshape(-1)
    count = tile_count.reshape(1, 1)
    srcmass = source_logmass.reshape(-1, LANES)
    tgtmass = target_logmass.reshape(-1, LANES)
    nsrc, ntgt = srcmass.shape[0], tgtmass.shape[0]
    ncol = lax.axis_size("col")
    nz = lax.axis_size("z")
    core = lax.axis_index("core")
    core1 = core.reshape(1).astype(jnp.int32)
    swap = [(0, 1), (1, 0)]

    def f32(*shape):
        return jax.ShapeDtypeStruct(shape, jnp.float32)

    mine = other = None
    for step in range(ITERS):
        if step == 0:
            dense = call(
                first_rows_kernel, "first_rows", (rows, cols, count), cost,
                (target_init.reshape(-1, LANES),), (f32(nsrc, LANES),), nsrc, (),
            )
        else:
            dense = call(
                rows_kernel, "rows_half", (rows, cols, count, core1), cost,
                (mine, other, tgtmass), (f32(nsrc, LANES),), nsrc,
                (pltpu.VMEM((ntgt, LANES), jnp.float32),),
            )
        parts = to_all(dense, "col", ncol).reshape(ncol, nsrc, LANES)
        source, keep, send = call(
            cols_kernel, "cols_half", (rows, cols, count, core1), cost,
            (parts, srcmass), (f32(nsrc, LANES), f32(ntgt // 2, LANES), f32(ntgt // 2, LANES)),
            ntgt, (pltpu.VMEM((ntgt, LANES), jnp.float32),),
        )
        got = lax.ppermute(send, "core", swap)
        top = jnp.maximum(keep, got)
        chip = top + jnp.log2(1.0 + jnp.exp2(-jnp.abs(keep - got)))
        mine = lse2(to_all(chip, "z", nz).reshape(nz, ntgt // 2, LANES))
        other = lax.ppermute(mine, "core", swap)
    first = jnp.where(core == 0, mine, other)
    second = jnp.where(core == 0, other, mine)
    target = EPS * tgtmass - BACK * jnp.concatenate([first, second], axis=0)
    return (source.reshape(-1), target.reshape(-1))


def solution(mesh):
    nrow, ncol = mesh.devices.shape
    cores = 2
    finer = Mesh(mesh.devices.reshape(nrow // cores, cores, ncol), ("z", "core", "col"))
    row = ("z", "core")
    return jax.shard_map(
        local,
        mesh=finer,
        in_specs=(
            P(row, "col", None, None, None),
            P(row, "col", None),
            P(row, "col", None),
            P(row, "col"),
            P(row),
            P("col"),
            P("col"),
        ),
        out_specs=(P(row), P("col")),
        check_vma=False,
    )
```

time: 250 us -> 121 us (0.48)
  waiting for transfers between devices: 94.4 us -> 19.1 us
  other arithmetic: 37.1 us -> 0.87 us
  starting transfers between devices: 43.8 us -> 15.2 us
  Pallas kernels: 0 us -> 21.2 us
  blocking collectives: 58.7 us -> 52.7 us
  matrix products: 3.19 us -> 0 us
    all_to_all x7 -> x1, waiting for transfers between devices: 94.4 us -> 15.7 us  [to_all(): return lax.all_to_all(copies, axes, 0, 0, tiled=True)]
    all_to_all x7 -> x1, starting transfers between devices: 43.8 us -> 7.7 us  [to_all(): return lax.all_to_all(copies, axes, 0, 0, tiled=True)]
    all_gather x2 -> x0, blocking collectives: 29.7 us -> none  [finish_target(): return lax.all_gather(piece, 'row', axis=0, tiled=True)]
    all_to_all x3, blocking collectives: 29 us -> 52.7 us  [to_all(): return lax.all_to_all(copies, axes, 0, 0, tiled=True)]
    pallas_call x0 -> x4, Pallas kernels: none -> 21.2 us  [call(): pl.pallas_call(kernel, name=name, out_shape=outs[0] if single else outs,...]
    reduce_max x12 -> x2, other arithmetic: 19 us -> 0.04 us  [lse2(): top = jnp.max(parts, axis=0)]
    reduce_sum x8 -> x2, other arithmetic: 14 us -> 0.11 us  [lse2(): return top + jnp.log2(jnp.sum(jnp.exp2(parts - top[None]), axis=0))]
    ppermute x0 -> x4, starting transfers between devices: none -> 7.54 us  [the longest x2 5.26 us: local(): got = lax.ppermute(send, 'core', swap)]
  transfers between devices with their start and end apart: 7 -> 5, of which waited for: 7 -> 5; matrix products, arithmetic and copies ran while one was open for 7% -> 0% of each run, Pallas kernels for 0% -> 0%
where the time goes in v1:
time: 121 us; the launch traced here: 120 us
  blocking collectives  52.7 us (44%)
  Pallas kernels  21.2 us (18%)
  waiting for transfers between devices  19.1 us (16%)
  starting transfers between devices  15.2 us (13%)
  local copies, waits for them, and re-layouts  9.92 us (8%)
  between operations  1.45 us (1%)
    all_to_all x3, blocking collectives, to_all(): return lax.all_to_all(copies, axes, 0, 0, tiled=True)  52.7 us
    pallas_call x4, Pallas kernels, call(): pl.pallas_call(kernel, name=name, out_shape=outs[0] if single else outs,...  21.2 us
    all_to_all x1, waiting for transfers between devices, to_all(): return lax.all_to_all(copies, axes, 0, 0, tiled=True)  15.7 us
    unnamed x20, local copies, waits for them, and re-layouts  8.72 us
    all_to_all x1, starting transfers between devices, to_all(): return lax.all_to_all(copies, axes, 0, 0, tiled=True)  7.7 us
    ppermute x2, starting transfers between devices, local(): got = lax.ppermute(send, 'core', swap)  5.26 us
  transfers between devices with their start and end apart: 5, of which 5 were waited for; matrix products, arithmetic and copies ran while one was open for 0% of the time, Pallas kernels for 0%

profile of v1, /device:TPU:1, one launch (start us, length us, event | category | flops | bytes accessed | tf_op | source)
XLA Modules:
  0.0 120.5 jit_solution(14336807065742108224)
XLA Ops:
  0.6 0.0 copy-start.7
  0.6 0.0 copy-start.9
  1.3 0.0 copy-start
  1.3 2.2 %copy-done = f32[1,1,64,128,128]{4,3,2,1,0:T(8,128)S(1)} copy-done((f32[1,1,64,128,128]{4,3,2,1,0:T(8,128)S(1)}, f32[1,1,64,128,128]{4,3,2,1,0:T(8,128)}, u32[]{:S(2)}) %copy-start) | copy-done | bytes 4194328
  3.5 0.8 copy-done.5
  4.3 0.7 copy-done.6
  5.0 0.7 copy-done.8
  5.7 6.1 %first_rows.1 = f32[128,128]{1,0:T(8,128)S(1)} custom-call(s32[64]{0:T(128)S(1)} %bitcast.20, s32[64]{0:T(128)S(1)} %bitcast.24, s32[1,1]{1,0:T(1,128)S(6)} %copy.9.count, f32[64,128,128]{2,1,0:T(8,128)S(1)} %bitcast.12, f32[128,128]{1,0:T(8,128)S(1)} %bitcast.19), custom_call_target="tpu_custom_call" | custom-call | tf_op jit(solution)/shard_map/first_rows/pallas_call | solution.py:149
  11.7 1.1 broadcast_in_dim.8
  12.8 7.7 %all-to-all-start = ((f32[16,128,128]{2,1,0:T(8,128)}), f32[16,128,128]{2,1,0:T(8,128)S(1)}, u32[]{:S(2)}, u32[]{:S(2)}) async-start(f32[16,128,128]{2,1,0:T(8,128)} %broadcast_in_dim.8), calls=%async_computation | async-start | bytes 2097152 | tf_op jit(solution)/shard_map/all_to_all | solution.py:169
  20.5 15.7 %all-to-all-done.parts = f32[16,128,128]{2,1,0:T(8,128)S(1)} async-done(((f32[16,128,128]{2,1,0:T(8,128)}), f32[16,128,128]{2,1,0:T(8,128)S(1)}, u32[]{:S(2)}, u32[]{:S(2)}) %all-to-all-start) | async-done | bytes 1048608 | tf_op jit(solution)/shard_map/all_to_all | solution.py:169
  36.2 0.0 copy-start.1
  36.2 2.2 %copy-done.1 = f32[1,1,64,128,128]{4,3,2,1,0:T(8,128)S(1)} copy-done((f32[1,1,64,128,128]{4,3,2,1,0:T(8,128)S(1)}, f32[1,1,64,128,128]{4,3,2,1,0:T(8,128)}, u32[]{:S(2)}) %copy-start.1) | copy-done | bytes 4194328
  38.4 4.5 %cols_half.2 = (f32[128,128]{1,0:T(8,128)}, f32[64,128]{1,0:T(8,128)S(1)}, f32[64,128]{1,0:T(8,128)S(1)}) custom-call(s32[64]{0:T(128)S(1)} %bitcast.21, s32[64]{0:T(128)S(1)} %bitcast.25, s32[1,1]{1,0:T(1,128)S(6)} %copy.9.count, s32[1]{0:T(128)} %bitcast.2.core, f32[64,128,128]{2,1,0:T(8,128)S(1)} %bitcast.13, f32[16,128,128]{2,1,0:T(8,128)S(1)} %all-to-all-done.parts, ...), custom_call_target="tpu_custom_call" | custom-call | tf_op jit(solution)/shard_map/cols_half/pallas_call | solution.py:149
  42.9 3.1 %collective-permute-start = (f32[64,128]{1,0:T(8,128)S(1)}, f32[64,128]{1,0:T(8,128)S(1)}, u32[]{:S(2)}, u32[]{:S(2)}) collective-permute-start(f32[64,128]{1,0:T(8,128)S(1)} %get-tuple-element.8), channel_id=1, source_target_pairs={{0,16},{16,0},{1,17},{17,1},{2,18},{18,2},{3,19},{19,3},{4,20},{20... | collective-permute-start | bytes 98312 | tf_op jit(solution)/shard_map/ppermute | solution.py:210
  46.0 0.9 collective-permute-done
  47.0 19.2 %all_to_all.20 = f32[8,64,128]{2,1,0:T(8,128)S(1)} all-to-all(f32[8,64,128]{2,1,0:T(8,128)S(1)} %broadcast_in_dim.9), channel_id=1, replica_groups=mesh['z'=8,'core'=2,'col'=16] {'z'}, dimensions={0} | all-to-all | bytes 524288 | tf_op jit(solution)/shard_map/all_to_all | solution.py:169
  66.2 0.1 exponential_reduce_fusion.1
  66.3 1.7 %collective-permute-start.1 = (f32[64,128]{1,0:T(8,128)S(1)}, f32[64,128]{1,0:T(8,128)S(1)}, u32[]{:S(2)}, u32[]{:S(2)}) collective-permute-start(f32[64,128]{1,0:T(8,128)S(1)} %multiply_add_fusion.2.mine), channel_id=1, source_target_pairs={{0,16},{16,0},{1,17},{17,1},{2,18},{18,2},{3,19},{19,3},{4,20},{20... | collective-permute-start | bytes 98312 | tf_op jit(solution)/shard_map/ppermute | solution.py:214
  68.0 0.9 collective-permute-done.1.other
  68.8 2.2 %copy-done.2 = f32[1,1,64,128,128]{4,3,2,1,0:T(8,128)S(1)} copy-done((f32[1,1,64,128,128]{4,3,2,1,0:T(8,128)S(1)}, f32[1,1,64,128,128]{4,3,2,1,0:T(8,128)}, u32[]{:S(2)}) %copy-start.2) | copy-done | bytes 4194328
  71.0 6.1 %rows_half.1 = f32[128,128]{1,0:T(8,128)S(1)} custom-call(s32[64]{0:T(128)S(1)} %bitcast.22, s32[64]{0:T(128)S(1)} %bitcast.26, s32[1,1]{1,0:T(1,128)S(6)} %copy.9.count, s32[1]{0:T(128)} %bitcast.2.core, f32[64,128,128]{2,1,0:T(8,128)S(1)} %bitcast.14, f32[64,128]{1,0:T(8,128)S(1)} %multiply_add_fusion.2.mine, f32[64,128]{1,0:T(8,128)S(1)} %collective-permute-done.1.other, ...), custom_call_target="tpu_custom_call" | custom-call | tf_op jit(solution)/shard_map/rows_half/pallas_call | solution.py:149
  77.1 0.1 broadcast_in_dim.10
  77.2 18.8 %all_to_all.21.parts = f32[16,128,128]{2,1,0:T(8,128)S(1)} all-to-all(f32[16,128,128]{2,1,0:T(8,128)S(1)} %broadcast_in_dim.10), channel_id=1, replica_groups=mesh['z'=8,'core'=2,'col'=16] {'col'}, dimensions={0} | all-to-all | bytes 2097152 | tf_op jit(solution)/shard_map/all_to_all | solution.py:169
  96.0 4.5 %cols_half.3 = (f32[128,128]{1,0:T(8,128)}, f32[64,128]{1,0:T(8,128)S(1)}, f32[64,128]{1,0:T(8,128)S(1)}) custom-call(s32[64]{0:T(128)S(1)} %bitcast.23, s32[64]{0:T(128)S(1)} %bitcast.27, s32[1,1]{1,0:T(1,128)S(6)} %copy.9.count, s32[1]{0:T(128)} %bitcast.2.core, f32[64,128,128]{2,1,0:T(8,128)S(1)} %bitcast.15, f32[16,128,128]{2,1,0:T(8,128)S(1)} %all_to_all.21.parts, ...), custom_call_target="tpu_custom_call" | custom-call | tf_op jit(solution)/shard_map/cols_half/pallas_call | solution.py:149
  100.5 2.1 %collective-permute-start.2 = (f32[64,128]{1,0:T(8,128)S(1)}, f32[64,128]{1,0:T(8,128)S(1)}, u32[]{:S(2)}, u32[]{:S(2)}) collective-permute-start(f32[64,128]{1,0:T(8,128)S(1)} %get-tuple-element.11), channel_id=1, source_target_pairs={{0,16},{16,0},{1,17},{17,1},{2,18},{18,2},{3,19},{19,3},{4,20},{20... | collective-permute-start | bytes 98312 | tf_op jit(solution)/shard_map/ppermute | solution.py:210
  102.6 0.9 collective-permute-done.2
  103.6 14.8 %all_to_all.22 = f32[8,64,128]{2,1,0:T(8,128)S(1)} all-to-all(f32[8,64,128]{2,1,0:T(8,128)S(1)} %broadcast_in_dim.11), channel_id=1, replica_groups=mesh['z'=8,'core'=2,'col'=16] {'z'}, dimensions={0} | all-to-all | bytes 524288 | tf_op jit(solution)/shard_map/all_to_all | solution.py:169
  118.3 0.1 exponential_reduce_fusion
  118.4 0.6 collective-permute-start.3
  119.0 0.9 collective-permute-done.3
  119.9 0.6 fusion.1
  (19 shorter events, 0.2 us)
Async XLA Ops:
  0.6 35.6 %copy-start.7 = (s32[1,1,64]{2,1,0:T(1,128)S(1)}, s32[1,1,64]{2,1,0:T(1,128)}, u32[]{:S(2)}) copy-start(s32[1,1,64]{2,1,0:T(1,128)} %param.8) | copy-start | bytes 772
  0.6 35.5 %copy-start.9 = (s32[1,1,64]{2,1,0:T(1,128)S(1)}, s32[1,1,64]{2,1,0:T(1,128)}, u32[]{:S(2)}) copy-start(s32[1,1,64]{2,1,0:T(1,128)} %param.9) | copy-start | bytes 772
  1.3 2.2 %copy-start = (f32[1,1,64,128,128]{4,3,2,1,0:T(8,128)S(1)}, f32[1,1,64,128,128]{4,3,2,1,0:T(8,128)}, u32[]{:S(2)}) copy-start(f32[1,1,64,128,128]{4,3,2,1,0:T(8,128)} %param.7) | copy-start | bytes 12582916
  3.5 0.8 copy-start.5
  4.3 0.7 copy-start.6
  5.0 0.7 copy-start.8
  5.7 30.5 %copy-start.3 = (f32[16384]{0:T(1024)S(1)}, f32[16384]{0:T(1024)}, u32[]{:S(2)}) copy-start(f32[16384]{0:T(1024)} %param.11) | copy-start | bytes 196612
  12.8 56.0 %copy-start.4 = (f32[16384]{0:T(1024)S(1)}, f32[16384]{0:T(1024)}, u32[]{:S(2)}) copy-start(f32[16384]{0:T(1024)} %param.12) | copy-start | bytes 196612
  12.8 23.4 %all-to-all-start = ((f32[16,128,128]{2,1,0:T(8,128)}), f32[16,128,128]{2,1,0:T(8,128)S(1)}, u32[]{:S(2)}, u32[]{:S(2)}) async-start(f32[16,128,128]{2,1,0:T(8,128)} %broadcast_in_dim.8), calls=%async_computation | async-start | bytes 2097152 | tf_op jit(solution)/shard_map/all_to_all | solution.py:169
  36.2 2.2 %copy-start.1 = (f32[1,1,64,128,128]{4,3,2,1,0:T(8,128)S(1)}, f32[1,1,64,128,128]{4,3,2,1,0:T(8,128)}, u32[]{:S(2)}) copy-start(f32[1,1,64,128,128]{4,3,2,1,0:T(8,128)} %param.7) | copy-start | bytes 12582916
  42.9 4.0 %collective-permute-start = (f32[64,128]{1,0:T(8,128)S(1)}, f32[64,128]{1,0:T(8,128)S(1)}, u32[]{:S(2)}, u32[]{:S(2)}) collective-permute-start(f32[64,128]{1,0:T(8,128)S(1)} %get-tuple-element.8), channel_id=1, source_target_pairs={{0,16},{16,0},{1,17},{17,1},{2,18},{18,2},{3,19},{19,3},{4,20},{20... | collective-permute-start | bytes 98312 | tf_op jit(solution)/shard_map/ppermute | solution.py:210
  66.3 2.6 %collective-permute-start.1 = (f32[64,128]{1,0:T(8,128)S(1)}, f32[64,128]{1,0:T(8,128)S(1)}, u32[]{:S(2)}, u32[]{:S(2)}) collective-permute-start(f32[64,128]{1,0:T(8,128)S(1)} %multiply_add_fusion.2.mine), channel_id=1, source_target_pairs={{0,16},{16,0},{1,17},{17,1},{2,18},{18,2},{3,19},{19,3},{4,20},{20... | collective-permute-start | bytes 98312 | tf_op jit(solution)/shard_map/ppermute | solution.py:214
  68.8 2.2 %copy-start.2 = (f32[1,1,64,128,128]{4,3,2,1,0:T(8,128)S(1)}, f32[1,1,64,128,128]{4,3,2,1,0:T(8,128)}, u32[]{:S(2)}) copy-start(f32[1,1,64,128,128]{4,3,2,1,0:T(8,128)} %param.7) | copy-start | bytes 12582916
  100.5 3.0 %collective-permute-start.2 = (f32[64,128]{1,0:T(8,128)S(1)}, f32[64,128]{1,0:T(8,128)S(1)}, u32[]{:S(2)}, u32[]{:S(2)}) collective-permute-start(f32[64,128]{1,0:T(8,128)S(1)} %get-tuple-element.11), channel_id=1, source_target_pairs={{0,16},{16,0},{1,17},{17,1},{2,18},{18,2},{3,19},{19,3},{4,20},{20... | collective-permute-start | bytes 98312 | tf_op jit(solution)/shard_map/ppermute | solution.py:210
  118.4 1.4 %collective-permute-start.3 = (f32[64,128]{1,0:T(8,128)S(1)}, f32[64,128]{1,0:T(8,128)S(1)}, u32[]{:S(2)}, u32[]{:S(2)}) collective-permute-start(f32[64,128]{1,0:T(8,128)S(1)} %multiply_add_fusion), channel_id=1, source_target_pairs={{0,16},{16,0},{1,17},{17,1},{2,18},{18,2},{3,19},{19,3},{4,20},{20... | collective-permute-start | bytes 98312 | tf_op jit(solution)/shard_map/ppermute | solution.py:214

commit v2 on v1

v2 whole, which is shorter than its diff:
```python
import jax
import jax.numpy as jnp
import numpy as np
from jax import lax
from jax.experimental import pallas as pl
from jax.experimental.pallas import tpu as pltpu
from jax.sharding import Mesh
from jax.sharding import PartitionSpec as P

ITERS = 2
EPS = 0.1
LN2 = float(np.log(2.0))
UNIT = 1.0 / (EPS * LN2)
BACK = EPS * LN2
NONE = -1.0e30
LANES = 128
WAYS = 4
CHUNK = 8
LIMIT = 24 << 20


def lse2(parts):
    top = jnp.max(parts, axis=0)
    return top + jnp.log2(jnp.sum(jnp.exp2(parts - top[None]), axis=0))


def merge_slots(values, seg_ref, count, peak, mass):
    slots = values.shape[0]
    nseg = peak.shape[1] - 8

    def home(s):
        return jnp.where(s < count, seg_ref[s], nseg)

    peak[...] = jnp.full(peak.shape, NONE, jnp.float32)
    mass[...] = jnp.zeros(mass.shape, jnp.float32)
    for s in range(slots):
        at = (s % WAYS, pl.ds(home(s), 1), slice(None))
        peak[at] = jnp.maximum(peak[at], values[pl.ds(s, 1), :])
    top = peak[0]
    for way in range(1, WAYS):
        top = jnp.maximum(top, peak[way])
    peak[0] = top
    for s in range(slots):
        row = pl.ds(home(s), 1)
        at = (s % WAYS, row, slice(None))
        mass[at] = mass[at] + jnp.exp2(values[pl.ds(s, 1), :] - peak[0, row, :])
    total = mass[0]
    for way in range(1, WAYS):
        total = total + mass[way]
    dense = jnp.maximum(top + jnp.log2(total), NONE)
    return dense[:nseg]


def one_row_tile(part, tile):
    scores = ((part - tile) * UNIT).T
    top = jnp.max(scores, axis=0, keepdims=True)
    return top + jnp.log2(jnp.sum(jnp.exp2(scores - top), axis=0, keepdims=True))


def one_col_tile(part, tile):
    upright = jnp.broadcast_to(part, tile.shape).T
    scores = (upright - tile) * UNIT
    top = jnp.max(scores, axis=0, keepdims=True)
    return top + jnp.log2(jnp.sum(jnp.exp2(scores - top), axis=0, keepdims=True))


def fetch(cost_in, cost, sems):
    copies = []
    for k in range(cost.shape[0] // CHUNK):
        at = pl.ds(k * CHUNK, CHUNK)
        copies.append(pltpu.make_async_copy(cost_in.at[at], cost.at[at], sems.at[k]))
        copies[-1].start()
    return copies


def tiles(tile_lse, ids, chunks, cost, pot, values):
    for k, chunk in enumerate(chunks):
        chunk.wait()
        for s in range(k * CHUNK, (k + 1) * CHUNK):
            values[pl.ds(s, 1), :] = tile_lse(pot[pl.ds(ids[s], 1), :], cost[s])


def start_all(pairs, sems):
    copies = [pltpu.make_async_copy(src, dst, sems.at[k]) for k, (src, dst) in enumerate(pairs)]
    for copy in copies:
        copy.start()
    return copies


def first_rows_kernel(
    rows_in, cols_in, cost_in, pot_in, count, core, out, cost, rows, cols, pot, sems, cost_sems, values, peak, mass
):
    small = start_all(((cols_in, cols), (pot_in, pot), (rows_in, rows)), sems)
    chunks = fetch(cost_in, cost, cost_sems)
    small[0].wait()
    small[1].wait()
    tiles(one_row_tile, cols, chunks, cost, pot, values)
    small[2].wait()
    out[...] = merge_slots(values, rows, count[0, 0], peak, mass)


def rows_kernel(
    rows_in, cols_in, cost_in, count, core, mine, other, logmass, out, cost, rows, cols, pot, sems, cost_sems, values, peak, mass
):
    small = start_all(((cols_in, cols), (rows_in, rows)), sems)
    chunks = fetch(cost_in, cost, cost_sems)
    half = mine.shape[0]
    at = pl.multiple_of(core[0] * half, half)
    away = pl.multiple_of((1 - core[0]) * half, half)
    pot[pl.ds(at, half), :] = EPS * logmass[pl.ds(at, half), :] - BACK * mine[...]
    pot[pl.ds(away, half), :] = EPS * logmass[pl.ds(away, half), :] - BACK * other[...]
    for copy in small:
        copy.wait()
    tiles(one_row_tile, cols, chunks, cost, pot, values)
    out[...] = merge_slots(values, rows, count[0, 0], peak, mass)


def cols_kernel(
    rows_in, cols_in, cost_in, count, core, parts, logmass, pot, keep, send, cost, rows, cols, dense, sems, cost_sems, values, peak, mass
):
    small = start_all(((rows_in, rows), (cols_in, cols)), sems)
    chunks = fetch(cost_in, cost, cost_sems)
    pot[...] = EPS * logmass[...] - BACK * lse2(parts[...])
    for copy in small:
        copy.wait()
    tiles(one_col_tile, rows, chunks, cost, pot, values)
    dense[...] = merge_slots(values, cols, count[0, 0], peak, mass)
    half = keep.shape[0]
    keep[...] = dense[pl.ds(pl.multiple_of(core[0] * half, half), half), :]
    send[...] = dense[pl.ds(pl.multiple_of((1 - core[0]) * half, half), half), :]


def call(kernel, name, anywhere, smem, vmem, outs, slots, nseg):
    held = pl.BlockSpec(memory_space=pltpu.VMEM)
    specs = [pl.BlockSpec(memory_space=pl.ANY)] * len(anywhere)
    specs += [pl.BlockSpec(memory_space=pltpu.SMEM)] * len(smem) + [held] * len(vmem)
    single = len(outs) == 1
    return pl.pallas_call(
        kernel,
        name=name,
        out_shape=outs[0] if single else outs,
        in_specs=specs,
        out_specs=held if single else tuple(held for _ in outs),
        scratch_shapes=[
            pltpu.VMEM((slots, LANES, LANES), jnp.float32),
            pltpu.SMEM((slots,), jnp.int32),
            pltpu.SMEM((slots,), jnp.int32),
            pltpu.VMEM((nseg, LANES), jnp.float32),
            pltpu.SemaphoreType.DMA((3,)),
            pltpu.SemaphoreType.DMA((slots // CHUNK,)),
            pltpu.VMEM((slots, LANES), jnp.float32),
            pltpu.VMEM((WAYS, nseg + 8, LANES), jnp.float32),
            pltpu.VMEM((WAYS, nseg + 8, LANES), jnp.float32),
        ],
        compiler_params=pltpu.CompilerParams(vmem_limit_bytes=LIMIT),
    )(*[pltpu.with_memory_space_constraint(x, pltpu.HBM) for x in anywhere], *smem, *vmem)


def to_all(value, axes, peers):
    copies = jnp.broadcast_to(value[None], (peers, *value.shape))
    return lax.all_to_all(copies, axes, 0, 0, tiled=True)


def local(
    cost_tiles, tile_rows, tile_cols, tile_count, source_logmass, target_logmass, target_init
):
    cost = cost_tiles.reshape(cost_tiles.shape[2:])
    rows = tile_rows.reshape(-1)
    cols = tile_cols.reshape(-1)
    count = tile_count.reshape(1, 1)
    srcmass = source_logmass.reshape(-1, LANES)
    tgtmass = target_logmass.reshape(-1, LANES)
    nsrc, ntgt = srcmass.shape[0], tgtmass.shape[0]
    ncol = lax.axis_size("col")
    nz = lax.axis_size("z")
    core = lax.axis_index("core")
    core1 = core.reshape(1).astype(jnp.int32)
    swap = [(0, 1), (1, 0)]

    def f32(*shape):
        return jax.ShapeDtypeStruct(shape, jnp.float32)

    mine = other = None
    slots = cost.shape[0]
    tiled = (rows, cols, cost)
    full, half = f32(nsrc, LANES), f32(ntgt // 2, LANES)
    for step in range(ITERS):
        if step == 0:
            dense = call(
                first_rows_kernel, "first_rows", (*tiled, target_init.reshape(-1, LANES)), (count, core1), (),
                (pltpu.VMEM((nsrc, LANES), jnp.float32),), slots, nsrc,
            )
        else:
            dense = call(
                rows_kernel, "rows_half", tiled, (count, core1), (mine, other, tgtmass), (full,), slots, nsrc
            )
        parts = to_all(dense, "col", ncol).reshape(ncol, nsrc, LANES)
        source, keep, send = call(
            cols_kernel, "cols_half", tiled, (count, core1), (parts, srcmass), (full, half, half), slots, ntgt
        )
        got = lax.ppermute(send, "core", swap)
        top = jnp.maximum(keep, got)
        chip = top + jnp.log2(1.0 + jnp.exp2(-jnp.abs(keep - got)))
        mine = lse2(to_all(chip, "z", nz).reshape(nz, ntgt // 2, LANES))
        other = lax.ppermute(mine, "core", swap)
    first = jnp.where(core == 0, mine, other)
    second = jnp.where(core == 0, other, mine)
    target = EPS * tgtmass - BACK * jnp.concatenate([first, second], axis=0)
    return (source.reshape(-1), target.reshape(-1))


def solution(mesh):
    nrow, ncol = mesh.devices.shape
    cores = 2
    finer = Mesh(mesh.devices.reshape(nrow // cores, cores, ncol), ("z", "core", "col"))
    row = ("z", "core")
    return jax.shard_map(
        local,
        mesh=finer,
        in_specs=(
            P(row, "col", None, None, None),
            P(row, "col", None),
            P(row, "col", None),
            P(row, "col"),
            P(row),
            P("col"),
            P("col"),
        ),
        out_specs=(P(row), P("col")),
        check_vma=False,
    )
```

time: 121 us -> 106 us (0.88)
  blocking collectives: 52.7 us -> 76.8 us
  waiting for transfers between devices: 19.1 us -> 3.44 us
  local copies, waits for them, and re-layouts: 9.92 us -> 0.24 us
  starting transfers between devices: 15.2 us -> 6.37 us
  Pallas kernels: 21.2 us -> 16.8 us
    all_to_all x3 -> x4, blocking collectives: 52.7 us -> 76.8 us  [to_all(): return lax.all_to_all(copies, axes, 0, 0, tiled=True)]
    all_to_all x1 -> x0, waiting for transfers between devices: 15.7 us -> none  [to_all(): return lax.all_to_all(copies, axes, 0, 0, tiled=True)]
    unnamed x20 -> x4, local copies, waits for them, and re-layouts: 8.72 us -> 0.01 us
    all_to_all x1 -> x0, starting transfers between devices: 7.7 us -> none  [to_all(): return lax.all_to_all(copies, axes, 0, 0, tiled=True)]
    pallas_call x4, Pallas kernels: 21.2 us -> 16.8 us  [call(): pl.pallas_call(kernel, name=name, out_shape=outs[0] if single else outs,...]
  transfers between devices with their start and end apart: 5 -> 4, of which waited for: 5 -> 4; matrix products, arithmetic and copies ran while one was open for 0% -> 0% of each run, Pallas kernels for 0% -> 0%
where the time goes in v2:
time: 106 us
  blocking collectives  76.8 us (72%)
  Pallas kernels  16.8 us (16%)
  starting transfers between devices  6.37 us (6%)
  waiting for transfers between devices  3.44 us (3%)
  between operations  1.44 us (1%)
    all_to_all x4, blocking collectives, to_all(): return lax.all_to_all(copies, axes, 0, 0, tiled=True)  76.8 us
    pallas_call x4, Pallas kernels, call(): pl.pallas_call(kernel, name=name, out_shape=outs[0] if single else outs,...  16.8 us
    ppermute x2, starting transfers between devices, local(): got = lax.ppermute(send, 'core', swap)  4.09 us
    ppermute x2, starting transfers between devices, local(): other = lax.ppermute(mine, 'core', swap)  2.27 us
  transfers between devices with their start and end apart: 4, of which 4 were waited for; matrix products, arithmetic and copies ran while one was open for 0% of the time, Pallas kernels for 0%

profile of v2, /device:TPU:1, one launch (start us, length us, event | category | flops | bytes accessed | tf_op | source)
XLA Modules:
  0.0 105.9 jit_solution(17703154689495697957)
XLA Ops:
  0.6 0.0 copy-start
  1.3 4.6 %first_rows.1 = f32[128,128]{1,0:T(8,128)S(1)} custom-call(s32[64]{0:T(128)} %bitcast.20, s32[64]{0:T(128)} %bitcast.24, f32[64,128,128]{2,1,0:T(8,128)} %bitcast.15, f32[128,128]{1,0:T(8,128)} %bitcast.19, s32[1,1]{1,0:T(1,128)S(6)} %copy.9.count, s32[1]{0:T(128)} %bitcast.3.core), custom_call_target="tpu_custom_call" | custom-call | tf_op jit(solution)/shard_map/first_rows/pallas_call | solution.py:138
  5.9 0.1 broadcast_in_dim.8
  6.0 0.0 copy-start.1
  6.1 23.4 %all_to_all.20.parts = f32[16,128,128]{2,1,0:T(8,128)S(1)} all-to-all(f32[16,128,128]{2,1,0:T(8,128)S(1)} %broadcast_in_dim.8), channel_id=1, replica_groups=mesh['z'=8,'core'=2,'col'=16] {'col'}, dimensions={0} | all-to-all | bytes 2097152 | tf_op jit(solution)/shard_map/all_to_all | solution.py:161
  29.5 0.0 copy-done
  29.5 4.2 %cols_half.2 = (f32[128,128]{1,0:T(8,128)}, f32[64,128]{1,0:T(8,128)S(1)}, f32[64,128]{1,0:T(8,128)S(1)}) custom-call(s32[64]{0:T(128)} %bitcast.21, s32[64]{0:T(128)} %bitcast.25, f32[64,128,128]{2,1,0:T(8,128)} %bitcast.16, s32[1,1]{1,0:T(1,128)S(6)} %copy.9.count, s32[1]{0:T(128)} %bitcast.3.core, f32[16,128,128]{2,1,0:T(8,128)S(1)} %all_to_all.20.parts, ...), custom_call_target="tpu_custom_call" | custom-call | tf_op jit(solution)/shard_map/cols_half/pallas_call | solution.py:138
  33.8 1.9 %collective-permute-start = (f32[64,128]{1,0:T(8,128)S(1)}, f32[64,128]{1,0:T(8,128)S(1)}, u32[]{:S(2)}, u32[]{:S(2)}) collective-permute-start(f32[64,128]{1,0:T(8,128)S(1)} %get-tuple-element.8), channel_id=1, source_target_pairs={{0,16},{16,0},{1,17},{17,1},{2,18},{18,2},{3,19},{19,3},{4,20},{20... | collective-permute-start | bytes 98312 | tf_op jit(solution)/shard_map/ppermute | solution.py:201
  35.7 0.9 collective-permute-done
  36.6 19.2 %all_to_all.21 = f32[8,64,128]{2,1,0:T(8,128)S(1)} all-to-all(f32[8,64,128]{2,1,0:T(8,128)S(1)} %broadcast_in_dim.9), channel_id=1, replica_groups=mesh['z'=8,'core'=2,'col'=16] {'z'}, dimensions={0} | all-to-all | bytes 524288 | tf_op jit(solution)/shard_map/all_to_all | solution.py:161
  55.9 0.1 exponential_reduce_fusion.1
  55.9 1.7 %collective-permute-start.1 = (f32[64,128]{1,0:T(8,128)S(1)}, f32[64,128]{1,0:T(8,128)S(1)}, u32[]{:S(2)}, u32[]{:S(2)}) collective-permute-start(f32[64,128]{1,0:T(8,128)S(1)} %multiply_add_fusion.2.mine), channel_id=1, source_target_pairs={{0,16},{16,0},{1,17},{17,1},{2,18},{18,2},{3,19},{19,3},{4,20},{20... | collective-permute-start | bytes 98312 | tf_op jit(solution)/shard_map/ppermute | solution.py:205
  57.6 0.9 collective-permute-done.1.other
  58.5 0.0 copy-done.1
  58.5 3.6 %rows_half.1 = f32[128,128]{1,0:T(8,128)S(1)} custom-call(s32[64]{0:T(128)} %bitcast.22, s32[64]{0:T(128)} %bitcast.26, f32[64,128,128]{2,1,0:T(8,128)} %bitcast.17, s32[1,1]{1,0:T(1,128)S(6)} %copy.9.count, s32[1]{0:T(128)} %bitcast.3.core, f32[64,128]{1,0:T(8,128)S(1)} %multiply_add_fusion.2.mine, f32[64,128]{1,0:T(8,128)S(1)} %collective-permute-done.1.other, ...), custom_call_target="tpu_custom_call" | custom-call | tf_op jit(solution)/shard_map/rows_half/pallas_call | solution.py:138
  62.2 0.1 broadcast_in_dim.10
  62.3 19.4 %all_to_all.22.parts = f32[16,128,128]{2,1,0:T(8,128)S(1)} all-to-all(f32[16,128,128]{2,1,0:T(8,128)S(1)} %broadcast_in_dim.10), channel_id=1, replica_groups=mesh['z'=8,'core'=2,'col'=16] {'col'}, dimensions={0} | all-to-all | bytes 2097152 | tf_op jit(solution)/shard_map/all_to_all | solution.py:161
  81.6 4.2 %cols_half.3 = (f32[128,128]{1,0:T(8,128)}, f32[64,128]{1,0:T(8,128)S(1)}, f32[64,128]{1,0:T(8,128)S(1)}) custom-call(s32[64]{0:T(128)} %bitcast.23, s32[64]{0:T(128)} %bitcast.27, f32[64,128,128]{2,1,0:T(8,128)} %bitcast.18, s32[1,1]{1,0:T(1,128)S(6)} %copy.9.count, s32[1]{0:T(128)} %bitcast.3.core, f32[16,128,128]{2,1,0:T(8,128)S(1)} %all_to_all.22.parts, ...), custom_call_target="tpu_custom_call" | custom-call | tf_op jit(solution)/shard_map/cols_half/pallas_call | solution.py:138
  85.9 2.1 %collective-permute-start.2 = (f32[64,128]{1,0:T(8,128)S(1)}, f32[64,128]{1,0:T(8,128)S(1)}, u32[]{:S(2)}, u32[]{:S(2)}) collective-permute-start(f32[64,128]{1,0:T(8,128)S(1)} %get-tuple-element.11), channel_id=1, source_target_pairs={{0,16},{16,0},{1,17},{17,1},{2,18},{18,2},{3,19},{19,3},{4,20},{20... | collective-permute-start | bytes 98312 | tf_op jit(solution)/shard_map/ppermute | solution.py:201
  88.0 0.9 collective-permute-done.2
  88.9 14.8 %all_to_all.23 = f32[8,64,128]{2,1,0:T(8,128)S(1)} all-to-all(f32[8,64,128]{2,1,0:T(8,128)S(1)} %broadcast_in_dim.11), channel_id=1, replica_groups=mesh['z'=8,'core'=2,'col'=16] {'z'}, dimensions={0} | all-to-all | bytes 524288 | tf_op jit(solution)/shard_map/all_to_all | solution.py:161
  103.7 0.1 exponential_reduce_fusion
  103.8 0.6 collective-permute-start.3
  104.4 0.9 collective-permute-done.3
  105.2 0.6 fusion.1
  (9 shorter events, 0.2 us)
Async XLA Ops:
  0.6 28.9 %copy-start = (f32[16384]{0:T(1024)S(1)}, f32[16384]{0:T(1024)}, u32[]{:S(2)}) copy-start(f32[16384]{0:T(1024)} %param.11) | copy-start | bytes 196612
  6.0 52.5 %copy-start.1 = (f32[16384]{0:T(1024)S(1)}, f32[16384]{0:T(1024)}, u32[]{:S(2)}) copy-start(f32[16384]{0:T(1024)} %param.12) | copy-start | bytes 196612
  33.8 2.8 %collective-permute-start = (f32[64,128]{1,0:T(8,128)S(1)}, f32[64,128]{1,0:T(8,128)S(1)}, u32[]{:S(2)}, u32[]{:S(2)}) collective-permute-start(f32[64,128]{1,0:T(8,128)S(1)} %get-tuple-element.8), channel_id=1, source_target_pairs={{0,16},{16,0},{1,17},{17,1},{2,18},{18,2},{3,19},{19,3},{4,20},{20... | collective-permute-start | bytes 98312 | tf_op jit(solution)/shard_map/ppermute | solution.py:201
  55.9 2.6 %collective-permute-start.1 = (f32[64,128]{1,0:T(8,128)S(1)}, f32[64,128]{1,0:T(8,128)S(1)}, u32[]{:S(2)}, u32[]{:S(2)}) collective-permute-start(f32[64,128]{1,0:T(8,128)S(1)} %multiply_add_fusion.2.mine), channel_id=1, source_target_pairs={{0,16},{16,0},{1,17},{17,1},{2,18},{18,2},{3,19},{19,3},{4,20},{20... | collective-permute-start | bytes 98312 | tf_op jit(solution)/shard_map/ppermute | solution.py:205
  85.9 3.0 %collective-permute-start.2 = (f32[64,128]{1,0:T(8,128)S(1)}, f32[64,128]{1,0:T(8,128)S(1)}, u32[]{:S(2)}, u32[]{:S(2)}) collective-permute-start(f32[64,128]{1,0:T(8,128)S(1)} %get-tuple-element.11), channel_id=1, source_target_pairs={{0,16},{16,0},{1,17},{17,1},{2,18},{18,2},{3,19},{19,3},{4,20},{20... | collective-permute-start | bytes 98312 | tf_op jit(solution)/shard_map/ppermute | solution.py:201
  103.8 1.4 %collective-permute-start.3 = (f32[64,128]{1,0:T(8,128)S(1)}, f32[64,128]{1,0:T(8,128)S(1)}, u32[]{:S(2)}, u32[]{:S(2)}) collective-permute-start(f32[64,128]{1,0:T(8,128)S(1)} %multiply_add_fusion), channel_id=1, source_target_pairs={{0,16},{16,0},{1,17},{17,1},{2,18},{18,2},{3,19},{19,3},{4,20},{20... | collective-permute-start | bytes 98312 | tf_op jit(solution)/shard_map/ppermute | solution.py:205

commit v3 on v2

v3 whole, which is shorter than its diff:
```python
import jax
import jax.numpy as jnp
import numpy as np
from jax import lax
from jax.experimental import pallas as pl
from jax.experimental.pallas import tpu as pltpu
from jax.sharding import Mesh
from jax.sharding import PartitionSpec as P

ITERS = 2
EPS = 0.1
LN2 = float(np.log(2.0))
UNIT = 1.0 / (EPS * LN2)
BACK = EPS * LN2
NONE = -1.0e30
LANES = 128
CHUNK = 8
LIMIT = 24 << 20


def pieces(x):
    high = x.astype(jnp.bfloat16)
    rest = x - high.astype(jnp.float32)
    middle = rest.astype(jnp.bfloat16)
    low = (rest - middle.astype(jnp.float32)).astype(jnp.bfloat16)
    return high, middle, low


def note_ids(ids, count, upright, across):
    slots = ids.shape[0]
    for s in range(slots):
        one = jnp.full((1, LANES), jnp.where(s < count, ids[s], -1), jnp.int32)
        upright[pl.ds(s, 1), :] = one
        upright[pl.ds(slots + s, 1), :] = one
    across[...] = upright[...].T


def merged(values, ids, count, upright, across, out):
    slots = values.shape[0]
    mine = upright[:slots, :]
    top = jnp.full((slots, LANES), NONE, jnp.float32)
    for s in range(slots):
        same = mine == jnp.where(s < count, ids[s], -1)
        top = jnp.maximum(top, jnp.where(same, values[pl.ds(s, 1), :], NONE))
    same = jnp.where(mine == across[:slots, :], 1.0, 0.0).astype(jnp.bfloat16)
    high, middle, _ = pieces(jnp.exp2(values[...] - top))
    mass = jnp.dot(same, jnp.concatenate([high, middle], axis=0), preferred_element_type=jnp.float32)
    out[:slots, :] = top + jnp.log2(mass)
    above = lax.broadcasted_iota(jnp.int32, (slots, LANES), 0)
    lane = lax.broadcasted_iota(jnp.int32, (slots, LANES), 1)
    earlier = above < jnp.where(lane < slots, lane, lane - slots)
    again = jnp.max(jnp.where(earlier & (mine == across[:slots, :]), 1.0, 0.0), axis=0, keepdims=True)
    named = jnp.where(again > 0.0, -1.0, across[:1, :].astype(jnp.float32))
    out[slots:, :] = jnp.broadcast_to(named, (out.shape[0] - slots, LANES))


def spread(parts, dense):
    peers = parts.shape[0]
    slots = LANES // 2
    block = lax.broadcasted_iota(jnp.int32, (LANES, LANES), 0).astype(jnp.float32)
    ones = jnp.ones((slots, LANES), jnp.bfloat16)
    none = jnp.zeros((slots, LANES), jnp.bfloat16)
    hits = jnp.concatenate([ones, none, none, none], axis=0)
    top = jnp.full((LANES, LANES), NONE, jnp.float32)
    for d in range(peers):
        pick = jnp.where(block == parts[d, slots : slots + 1, :], 1.0, 0.0).astype(jnp.bfloat16)
        high, middle, low = pieces(parts[d, :slots, :])
        cut = jnp.concatenate([high, middle, low, none], axis=0)
        both = jnp.dot(
            jnp.concatenate([pick, pick], axis=1),
            jnp.concatenate([cut, hits], axis=1),
            preferred_element_type=jnp.float32,
        )
        value = jnp.where(both[:, LANES:] > 0.5, both[:, :LANES], NONE)
        dense[d] = value
        top = jnp.maximum(top, value)
    total = jnp.zeros((LANES, LANES), jnp.float32)
    for d in range(peers):
        total = total + jnp.exp2(dense[d] - top)
    return jnp.maximum(top + jnp.log2(total), NONE)


def one_row_tile(part, tile):
    scores = ((part - tile) * UNIT).T
    top = jnp.max(scores, axis=0, keepdims=True)
    return top + jnp.log2(jnp.sum(jnp.exp2(scores - top), axis=0, keepdims=True))


def one_col_tile(part, tile):
    upright = jnp.broadcast_to(part, tile.shape).T
    scores = (upright - tile) * UNIT
    top = jnp.max(scores, axis=0, keepdims=True)
    return top + jnp.log2(jnp.sum(jnp.exp2(scores - top), axis=0, keepdims=True))


def fetch(cost_in, cost, sems):
    copies = []
    for k in range(cost.shape[0] // CHUNK):
        at = pl.ds(k * CHUNK, CHUNK)
        copies.append(pltpu.make_async_copy(cost_in.at[at], cost.at[at], sems.at[k]))
        copies[-1].start()
    return copies


def tiles(tile_lse, ids, chunks, cost, pot, values):
    for k, chunk in enumerate(chunks):
        chunk.wait()
        for s in range(k * CHUNK, (k + 1) * CHUNK):
            values[pl.ds(s, 1), :] = tile_lse(pot[pl.ds(ids[s], 1), :], cost[s])


def start_all(pairs, sems):
    copies = [pltpu.make_async_copy(src, dst, sems.at[k]) for k, (src, dst) in enumerate(pairs)]
    for copy in copies:
        copy.start()
    return copies


def source_side(rows, cols, chunks, small, count, cost, pot, values, upright, across, out):
    for copy in small:
        copy.wait()
    note_ids(rows, count, upright, across)
    tiles(one_row_tile, cols, chunks, cost, pot, values)
    merged(values, rows, count, upright, across, out)


def first_rows_kernel(
    rows_in, cols_in, cost_in, pot_in, count, out, cost, rows, cols, pot, sems, cost_sems, values, upright, across
):
    small = start_all(((cols_in, cols), (pot_in, pot), (rows_in, rows)), sems)
    chunks = fetch(cost_in, cost, cost_sems)
    source_side(rows, cols, chunks, small, count[0, 0], cost, pot, values, upright, across, out)


def rows_kernel(
    rows_in, cols_in, cost_in, count, mine, other, logmass, out, cost, rows, cols, pot, sems, cost_sems, values, upright, across
):
    small = start_all(((cols_in, cols), (rows_in, rows)), sems)
    chunks = fetch(cost_in, cost, cost_sems)
    pot[...] = EPS * logmass[...] - BACK * pair_lse2(mine[...], other[...])
    source_side(rows, cols, chunks, small, count[0, 0], cost, pot, values, upright, across, out)


def cols_kernel(
    rows_in, cols_in, cost_in, count, parts, logmass, pot, out, cost, rows, cols, spare, sems, cost_sems, values, upright, across, dense
):
    small = start_all(((rows_in, rows), (cols_in, cols)), sems)
    chunks = fetch(cost_in, cost, cost_sems)
    pot[...] = EPS * logmass[...] - BACK * spread(parts, dense)
    for copy in small:
        copy.wait()
    note_ids(cols, count[0, 0], upright, across)
    tiles(one_col_tile, rows, chunks, cost, pot, values)
    merged(values, cols, count[0, 0], upright, across, out)


def spread_kernel(parts, out, dense):
    out[...] = spread(parts, dense)


def pair_lse2(a, b):
    return jnp.maximum(a, b) + jnp.log2(1.0 + jnp.exp2(-jnp.abs(a - b)))


def call(kernel, name, anywhere, smem, vmem, outs, slots, extra):
    held = pl.BlockSpec(memory_space=pltpu.VMEM)
    specs = [pl.BlockSpec(memory_space=pl.ANY)] * len(anywhere)
    specs += [pl.BlockSpec(memory_space=pltpu.SMEM)] * len(smem) + [held] * len(vmem)
    single = len(outs) == 1
    scratch = []
    if anywhere:
        scratch = [
            pltpu.VMEM((slots, LANES, LANES), jnp.float32),
            pltpu.SMEM((slots,), jnp.int32),
            pltpu.SMEM((slots,), jnp.int32),
            pltpu.VMEM((LANES, LANES), jnp.float32),
            pltpu.SemaphoreType.DMA((3,)),
            pltpu.SemaphoreType.DMA((slots // CHUNK,)),
            pltpu.VMEM((slots, LANES), jnp.float32),
            pltpu.VMEM((LANES, LANES), jnp.int32),
            pltpu.VMEM((LANES, LANES), jnp.int32),
        ]
    return pl.pallas_call(
        kernel,
        name=name,
        out_shape=outs[0] if single else outs,
        in_specs=specs,
        out_specs=held if single else tuple(held for _ in outs),
        scratch_shapes=scratch + list(extra),
        compiler_params=pltpu.CompilerParams(vmem_limit_bytes=LIMIT),
    )(*[pltpu.with_memory_space_constraint(x, pltpu.HBM) for x in anywhere], *smem, *vmem)


def to_all(value, axes, peers):
    copies = jnp.broadcast_to(value[None], (peers, *value.shape))
    return lax.all_to_all(copies, axes, 0, 0, tiled=True)


def local(
    cost_tiles, tile_rows, tile_cols, tile_count, source_logmass, target_logmass, target_init
):
    cost = cost_tiles.reshape(cost_tiles.shape[2:])
    rows = tile_rows.reshape(-1)
    cols = tile_cols.reshape(-1)
    count = tile_count.reshape(1, 1)
    srcmass = source_logmass.reshape(-1, LANES)
    tgtmass = target_logmass.reshape(-1, LANES)
    ncol = lax.axis_size("col")
    nz = lax.axis_size("z")
    swap = [(0, 1), (1, 0)]
    slots = cost.shape[0]
    tiled = (rows, cols, cost)

    def f32(*shape):
        return jax.ShapeDtypeStruct(shape, jnp.float32)

    full, sent = f32(LANES, LANES), f32(slots + 8, LANES)
    for step in range(ITERS):
        if step == 0:
            listed = call(
                first_rows_kernel, "first_rows", (*tiled, target_init.reshape(-1, LANES)), (count,), (),
                (sent,), slots, (),
            )
        else:
            listed = call(
                rows_kernel, "rows_half", tiled, (count,), (mine, other, tgtmass), (sent,), slots, ()
            )
        parts = to_all(listed, "col", ncol).reshape(ncol, slots + 8, LANES)
        source, listed = call(
            cols_kernel, "cols_half", tiled, (count,), (parts, srcmass), (full, sent), slots,
            (pltpu.VMEM((ncol, LANES, LANES), jnp.float32),),
        )
        parts = to_all(listed, "z", nz).reshape(nz, slots + 8, LANES)
        mine = call(
            spread_kernel, "spread", (), (), (parts,), (full,), slots,
            (pltpu.VMEM((nz, LANES, LANES), jnp.float32),),
        )
        other = lax.ppermute(mine, "core", swap)
    target = EPS * tgtmass - BACK * pair_lse2(mine, other)
    return (source.reshape(-1), target.reshape(-1))


def solution(mesh):
    nrow, ncol = mesh.devices.shape
    cores = 2
    finer = Mesh(mesh.devices.reshape(nrow // cores, cores, ncol), ("z", "core", "col"))
    row = ("z", "core")
    return jax.shard_map(
        local,
        mesh=finer,
        in_specs=(
            P(row, "col", None, None, None),
            P(row, "col", None),
            P(row, "col", None),
            P(row, "col"),
            P(row),
            P("col"),
            P("col"),
        ),
        out_specs=(P(row), P("col")),
        check_vma=False,
    )
```

time: 106 us -> 91.8 us (0.87)
  blocking collectives: 76.8 us -> 63.9 us
  waiting for transfers between devices: 3.44 us -> 1.8 us
    all_to_all x4, blocking collectives: 76.8 us -> 63.9 us  [to_all(): return lax.all_to_all(copies, axes, 0, 0, tiled=True)]
    ppermute x2, starting transfers between devices: 2.27 us -> 6.91 us  [local(): other = lax.ppermute(mine, 'core', swap)]
    ppermute x2 -> x0, starting transfers between devices: 4.09 us -> none  [local(): got = lax.ppermute(send, 'core', swap)]
    ppermute x2 -> x0, waiting for transfers between devices: 1.72 us -> none  [local(): got = lax.ppermute(send, 'core', swap)]
    pallas_call x4 -> x6, Pallas kernels: 16.8 us -> 16.6 us  [call(): pl.pallas_call(kernel, name=name, out_shape=outs[0] if single else outs,...]
  transfers between devices with their start and end apart: 4 -> 2, of which waited for: 4 -> 2; matrix products, arithmetic and copies ran while one was open for 0% -> 0% of each run, Pallas kernels for 0% -> 0%
where the time goes in v3:
time: 91.8 us; the launch traced here: 91.4 us
  blocking collectives  63.9 us (70%)
  Pallas kernels  16.6 us (18%)
  starting transfers between devices  6.91 us (8%)
  waiting for transfers between devices  1.8 us (2%)
  between operations  1.4 us (2%)
    all_to_all x4, blocking collectives, to_all(): return lax.all_to_all(copies, axes, 0, 0, tiled=True)  63.9 us
    pallas_call x6, Pallas kernels, call(): pl.pallas_call(kernel, name=name, out_shape=outs[0] if single else outs,...  16.6 us
    ppermute x2, starting transfers between devices, local(): other = lax.ppermute(mine, 'core', swap)  6.91 us
  transfers between devices with their start and end apart: 2, of which 2 were waited for; matrix products, arithmetic and copies ran while one was open for 0% of the time, Pallas kernels for 0%

profile of v3, /device:TPU:1, one launch (start us, length us, event | category | flops | bytes accessed | tf_op | source)
XLA Modules:
  0.0 91.4 jit_solution(8755838811239773119)
XLA Ops:
  0.6 0.0 copy-start
  1.3 4.4 %first_rows.1 = f32[72,128]{1,0:T(8,128)S(1)} custom-call(s32[64]{0:T(128)} %bitcast.18, s32[64]{0:T(128)} %bitcast.22, f32[64,128,128]{2,1,0:T(8,128)} %bitcast.13, f32[128,128]{1,0:T(8,128)} %bitcast.17, s32[1,1]{1,0:T(1,128)S(6)} %copy.9.count), custom_call_target="tpu_custom_call" | custom-call | tf_op jit(solution)/shard_map/first_rows/pallas_call | solution.py:183
  5.8 0.0 copy-start.1
  5.8 18.4 %all_to_all.20.parts = f32[16,72,128]{2,1,0:T(8,128)S(1)} all-to-all(f32[16,72,128]{2,1,0:T(8,128)S(1)} %broadcast_in_dim.8), channel_id=1, replica_groups=mesh['z'=8,'core'=2,'col'=16] {'col'}, dimensions={0} | all-to-all | bytes 1179648 | tf_op jit(solution)/shard_map/all_to_all | solution.py:196
  24.3 0.0 copy-done
  24.3 4.0 %cols_half.2 = (f32[128,128]{1,0:T(8,128)}, f32[72,128]{1,0:T(8,128)S(1)}) custom-call(s32[64]{0:T(128)} %bitcast.19, s32[64]{0:T(128)} %bitcast.23, f32[64,128,128]{2,1,0:T(8,128)} %bitcast.14, s32[1,1]{1,0:T(1,128)S(6)} %copy.9.count, f32[16,72,128]{2,1,0:T(8,128)S(1)} %all_to_all.20.parts, f32[128,128]{1,0:T(8,128)S(1)} %bitcast.10), custom_call_target="tpu_custom_call" | custom-call | tf_op jit(solution)/shard_map/cols_half/pallas_call | solution.py:183
  28.3 17.8 %all_to_all.21.parts = f32[8,72,128]{2,1,0:T(8,128)S(1)} all-to-all(f32[8,72,128]{2,1,0:T(8,128)S(1)} %broadcast_in_dim.9), channel_id=1, replica_groups=mesh['z'=8,'core'=2,'col'=16] {'z'}, dimensions={0} | all-to-all | bytes 589824 | tf_op jit(solution)/shard_map/all_to_all | solution.py:196
  46.1 0.4 spread.2.mine
  46.5 3.7 %collective-permute-start = (f32[128,128]{1,0:T(8,128)S(1)}, f32[128,128]{1,0:T(8,128)S(1)}, u32[]{:S(2)}, u32[]{:S(2)}) collective-permute-start(f32[128,128]{1,0:T(8,128)S(1)} %spread.2.mine), channel_id=1, source_target_pairs={{0,16},{16,0},{1,17},{17,1},{2,18},{18,2},{3,19},{19,3},{4,20},{20... | collective-permute-start | bytes 196616 | tf_op jit(solution)/shard_map/ppermute | solution.py:238
  50.2 0.9 collective-permute-done.other
  51.1 0.0 copy-done.1
  51.1 3.5 %rows_half.1 = f32[72,128]{1,0:T(8,128)S(1)} custom-call(s32[64]{0:T(128)} %bitcast.20, s32[64]{0:T(128)} %bitcast.24, f32[64,128,128]{2,1,0:T(8,128)} %bitcast.15, s32[1,1]{1,0:T(1,128)S(6)} %copy.9.count, f32[128,128]{1,0:T(8,128)S(1)} %spread.2.mine, f32[128,128]{1,0:T(8,128)S(1)} %collective-permute-done.other, f32[128,128]{1,0:T(8,128)S(1)} %bitcast.12), custom_call_target="tpu_custom_call" | custom-call | tf_op jit(solution)/shard_map/rows_half/pallas_call | solution.py:183
  54.7 14.8 %all_to_all.22.parts = f32[16,72,128]{2,1,0:T(8,128)S(1)} all-to-all(f32[16,72,128]{2,1,0:T(8,128)S(1)} %broadcast_in_dim.10), channel_id=1, replica_groups=mesh['z'=8,'core'=2,'col'=16] {'col'}, dimensions={0} | all-to-all | bytes 1179648 | tf_op jit(solution)/shard_map/all_to_all | solution.py:196
  69.5 4.0 %cols_half.3 = (f32[128,128]{1,0:T(8,128)}, f32[72,128]{1,0:T(8,128)S(1)}) custom-call(s32[64]{0:T(128)} %bitcast.21, s32[64]{0:T(128)} %bitcast.25, f32[64,128,128]{2,1,0:T(8,128)} %bitcast.16, s32[1,1]{1,0:T(1,128)S(6)} %copy.9.count, f32[16,72,128]{2,1,0:T(8,128)S(1)} %all_to_all.22.parts, f32[128,128]{1,0:T(8,128)S(1)} %bitcast.11), custom_call_target="tpu_custom_call" | custom-call | tf_op jit(solution)/shard_map/cols_half/pallas_call | solution.py:183
  73.5 12.8 %all_to_all.23.parts = f32[8,72,128]{2,1,0:T(8,128)S(1)} all-to-all(f32[8,72,128]{2,1,0:T(8,128)S(1)} %broadcast_in_dim.11), channel_id=1, replica_groups=mesh['z'=8,'core'=2,'col'=16] {'z'}, dimensions={0} | all-to-all | bytes 589824 | tf_op jit(solution)/shard_map/all_to_all | solution.py:196
  86.3 0.4 spread.3
  86.7 3.2 %collective-permute-start.1 = (f32[128,128]{1,0:T(8,128)S(1)}, f32[128,128]{1,0:T(8,128)S(1)}, u32[]{:S(2)}, u32[]{:S(2)}) collective-permute-start(f32[128,128]{1,0:T(8,128)S(1)} %spread.3), channel_id=1, source_target_pairs={{0,16},{16,0},{1,17},{17,1},{2,18},{18,2},{3,19},{19,3},{4,20},{20... | collective-permute-start | bytes 196616 | tf_op jit(solution)/shard_map/ppermute | solution.py:238
  89.9 0.9 collective-permute-done.1
  90.8 0.7 subtract_bitcast_fusion
  (4 shorter events, 0.1 us)
Async XLA Ops:
  0.6 23.6 %copy-start = (f32[16384]{0:T(1024)S(1)}, f32[16384]{0:T(1024)}, u32[]{:S(2)}) copy-start(f32[16384]{0:T(1024)} %param.11) | copy-start | bytes 196612
  5.8 45.4 %copy-start.1 = (f32[16384]{0:T(1024)S(1)}, f32[16384]{0:T(1024)}, u32[]{:S(2)}) copy-start(f32[16384]{0:T(1024)} %param.12) | copy-start | bytes 196612
  46.5 4.6 %collective-permute-start = (f32[128,128]{1,0:T(8,128)S(1)}, f32[128,128]{1,0:T(8,128)S(1)}, u32[]{:S(2)}, u32[]{:S(2)}) collective-permute-start(f32[128,128]{1,0:T(8,128)S(1)} %spread.2.mine), channel_id=1, source_target_pairs={{0,16},{16,0},{1,17},{17,1},{2,18},{18,2},{3,19},{19,3},{4,20},{20... | collective-permute-start | bytes 196616 | tf_op jit(solution)/shard_map/ppermute | solution.py:238
  86.7 4.1 %collective-permute-start.1 = (f32[128,128]{1,0:T(8,128)S(1)}, f32[128,128]{1,0:T(8,128)S(1)}, u32[]{:S(2)}, u32[]{:S(2)}) collective-permute-start(f32[128,128]{1,0:T(8,128)S(1)} %spread.3), channel_id=1, source_target_pairs={{0,16},{16,0},{1,17},{17,1},{2,18},{18,2},{3,19},{19,3},{4,20},{20... | collective-permute-start | bytes 196616 | tf_op jit(solution)/shard_map/ppermute | solution.py:238

commit v4 on v3

v4 whole, which is shorter than its diff:
```python
import jax
import jax.numpy as jnp
import numpy as np
from jax import lax
from jax.experimental import pallas as pl
from jax.experimental.pallas import tpu as pltpu
from jax.sharding import Mesh
from jax.sharding import PartitionSpec as P

ITERS = 2
EPS = 0.1
LN2 = float(np.log(2.0))
UNIT = 1.0 / (EPS * LN2)
BACK = EPS * LN2
NONE = -1.0e30
LANES = 128
CHUNK = 8
LIMIT = 24 << 20


def pieces(x):
    high = x.astype(jnp.bfloat16)
    rest = x - high.astype(jnp.float32)
    middle = rest.astype(jnp.bfloat16)
    low = (rest - middle.astype(jnp.float32)).astype(jnp.bfloat16)
    return high, middle, low


def note_ids(ids, count, upright, same, named, scratch):
    slots = ids.shape[0]
    for s in range(slots):
        one = jnp.full((1, LANES), jnp.where(s < count, ids[s], -1), jnp.int32)
        scratch[pl.ds(s, 1), :] = one
        scratch[pl.ds(slots + s, 1), :] = one
    upright[...] = scratch[:slots, :]
    across = scratch[...].T[:slots, :]
    equal = upright[...] == across
    same[...] = jnp.where(equal, 1.0, 0.0)
    above = lax.broadcasted_iota(jnp.int32, (slots, LANES), 0)
    lane = lax.broadcasted_iota(jnp.int32, (slots, LANES), 1)
    earlier = above < jnp.where(lane < slots, lane, lane - slots)
    again = jnp.max(jnp.where(earlier & equal, 1.0, 0.0), axis=0, keepdims=True)
    once = jnp.where(again > 0.0, -1.0, across[:1, :].astype(jnp.float32))
    named[...] = jnp.broadcast_to(once, named.shape)


def gathered(pot, upright):
    block = lax.broadcasted_iota(jnp.int32, upright.shape, 1)
    pick = jnp.where(block == upright[...], 1.0, 0.0).astype(jnp.bfloat16)
    return jnp.dot(
        jnp.concatenate([pick, pick, pick], axis=1),
        jnp.concatenate(pieces(pot), axis=0),
        preferred_element_type=jnp.float32,
    )


def merged(values, upright, same, named, out):
    slots = values.shape[0]
    mine = upright[...]
    top = jnp.full((slots, LANES), NONE, jnp.float32)
    for s in range(slots):
        hit = mine == upright[pl.ds(s, 1), :]
        top = jnp.maximum(top, jnp.where(hit, values[pl.ds(s, 1), :], NONE))
    high, middle, _ = pieces(jnp.exp2(values[...] - top))
    mass = jnp.dot(
        same[...].astype(jnp.bfloat16),
        jnp.concatenate([high, middle], axis=0),
        preferred_element_type=jnp.float32,
    )
    out[:slots, :] = top + jnp.log2(mass)
    if out.shape[0] > slots:
        out[slots:, :] = named[...]


def spread(parts, names, dense):
    peers = parts.shape[0]
    slots = LANES // 2
    block = lax.broadcasted_iota(jnp.int32, (LANES, LANES), 0).astype(jnp.float32)
    ones = jnp.ones((slots, LANES), jnp.bfloat16)
    none = jnp.zeros((slots, LANES), jnp.bfloat16)
    hits = jnp.concatenate([ones, none, none, none], axis=0)
    top = jnp.full((LANES, LANES), NONE, jnp.float32)
    for d in range(peers):
        pick = jnp.where(block == names[d, slots : slots + 1, :], 1.0, 0.0).astype(jnp.bfloat16)
        high, middle, low = pieces(parts[d, :slots, :])
        cut = jnp.concatenate([high, middle, low, none], axis=0)
        both = jnp.dot(
            jnp.concatenate([pick, pick], axis=1),
            jnp.concatenate([cut, hits], axis=1),
            preferred_element_type=jnp.float32,
        )
        value = jnp.where(both[:, LANES:] > 0.5, both[:, :LANES], NONE)
        dense[d] = value
        top = jnp.maximum(top, value)
    total = jnp.zeros((LANES, LANES), jnp.float32)
    for d in range(peers):
        total = total + jnp.exp2(dense[d] - top)
    return jnp.maximum(top + jnp.log2(total), NONE)


def one_row_tile(part, tile):
    scores = ((part - tile) * UNIT).T
    top = jnp.max(scores, axis=0, keepdims=True)
    return top + jnp.log2(jnp.sum(jnp.exp2(scores - top), axis=0, keepdims=True))


def one_col_tile(part, tile):
    upright = jnp.broadcast_to(part, tile.shape).T
    scores = (upright - tile) * UNIT
    top = jnp.max(scores, axis=0, keepdims=True)
    return top + jnp.log2(jnp.sum(jnp.exp2(scores - top), axis=0, keepdims=True))


def tiles(tile_lse, cost, picked, values, chunks=None):
    for k in range(cost.shape[0] // CHUNK):
        if chunks:
            chunks[k].wait()
        for s in range(k * CHUNK, (k + 1) * CHUNK):
            values[pl.ds(s, 1), :] = tile_lse(picked[pl.ds(s, 1), :], cost[s])


def first_rows_kernel(
    rows_in, cols_in, cost_in, pot_in, count,
    out, cost, row_up, row_same, row_named, col_up, col_same, col_named,
    rows, cols, pot, sems, cost_sems, scratch, values, picked,
):
    small = []
    for k, (src, dst) in enumerate(((cols_in, cols), (rows_in, rows), (pot_in, pot))):
        small.append(pltpu.make_async_copy(src, dst, sems.at[k]))
        small[-1].start()
    chunks = []
    for k in range(cost.shape[0] // CHUNK):
        at = pl.ds(k * CHUNK, CHUNK)
        chunks.append(pltpu.make_async_copy(cost_in.at[at], cost.at[at], cost_sems.at[k]))
        chunks[-1].start()
    small[0].wait()
    note_ids(cols, count[0, 0], col_up, col_same, col_named, scratch)
    small[1].wait()
    note_ids(rows, count[0, 0], row_up, row_same, row_named, scratch)
    small[2].wait()
    picked[...] = gathered(pot[...], col_up)
    tiles(one_row_tile, cost, picked, values, chunks)
    merged(values, row_up, row_same, row_named, out)


def rows_kernel(mine, other, logmass, cost, row_up, row_same, row_named, col_up, out, values, picked):
    pot = EPS * logmass[...] - BACK * pair_lse2(mine[...], other[...])
    picked[...] = gathered(pot, col_up)
    tiles(one_row_tile, cost, picked, values)
    merged(values, row_up, row_same, row_named, out)


def cols_kernel(
    parts, names, logmass, cost, row_up, col_up, col_same, col_named, pot, out, values, picked, dense
):
    pot[...] = EPS * logmass[...] - BACK * spread(parts, names, dense)
    picked[...] = gathered(pot[...], row_up)
    tiles(one_col_tile, cost, picked, values)
    merged(values, col_up, col_same, col_named, out)


def spread_kernel(parts, names, out, dense):
    out[...] = spread(parts, names, dense)


def pair_lse2(a, b):
    return jnp.maximum(a, b) + jnp.log2(1.0 + jnp.exp2(-jnp.abs(a - b)))


def call(kernel, name, operands, specs, outs, scratch):
    held = pl.BlockSpec(memory_space=pltpu.VMEM)
    single = len(outs) == 1
    return pl.pallas_call(
        kernel,
        name=name,
        out_shape=outs[0] if single else outs,
        in_specs=[held] * len(operands) if specs is None else specs,
        out_specs=held if single else tuple(held for _ in outs),
        scratch_shapes=scratch,
        compiler_params=pltpu.CompilerParams(vmem_limit_bytes=LIMIT),
    )(*operands)


def to_all(value, axes, peers):
    copies = jnp.broadcast_to(value[None], (peers, *value.shape))
    return lax.all_to_all(copies, axes, 0, 0, tiled=True)


def local(
    cost_tiles, tile_rows, tile_cols, tile_count, source_logmass, target_logmass, target_init
):
    cost = cost_tiles.reshape(cost_tiles.shape[2:])
    rows = tile_rows.reshape(-1)
    cols = tile_cols.reshape(-1)
    count = tile_count.reshape(1, 1)
    srcmass = source_logmass.reshape(-1, LANES)
    tgtmass = target_logmass.reshape(-1, LANES)
    ncol = lax.axis_size("col")
    nz = lax.axis_size("z")
    swap = [(0, 1), (1, 0)]
    slots = cost.shape[0]

    def f32(*shape):
        return pltpu.VMEM(shape, jnp.float32)

    def keep(x):
        return pltpu.with_memory_space_constraint(x, pltpu.VMEM)

    def far(x):
        return pltpu.with_memory_space_constraint(x, pltpu.HBM)

    full, named, values = f32(LANES, LANES), f32(8, LANES), f32(slots, LANES)
    ids = (pltpu.VMEM((slots, LANES), jnp.int32), values, named)
    anywhere = pl.BlockSpec(memory_space=pl.ANY)
    col_names = row_names = None
    for step in range(ITERS):
        sent = f32(slots + 8, LANES) if step == 0 else f32(slots, LANES)
        if step == 0:
            listed, *kept = call(
                first_rows_kernel, "first_rows",
                (far(rows), far(cols), far(cost), far(target_init.reshape(-1, LANES)), count),
                [anywhere] * 4 + [pl.BlockSpec(memory_space=pltpu.SMEM)],
                (sent, f32(*cost.shape), *ids, *ids),
                (
                    pltpu.SMEM((slots,), jnp.int32),
                    pltpu.SMEM((slots,), jnp.int32),
                    full,
                    pltpu.SemaphoreType.DMA((3,)),
                    pltpu.SemaphoreType.DMA((slots // CHUNK,)),
                    pltpu.VMEM((LANES, LANES), jnp.int32),
                    values,
                    values,
                ),
            )
            tiles_held, row_up, row_same, row_named, col_up, col_same, col_named = (keep(x) for x in kept)
        else:
            listed = call(
                rows_kernel, "rows_half",
                (mine, other, tgtmass, tiles_held, row_up, row_same, row_named, col_up),
                None, (sent,), (values, values),
            )
        parts = to_all(listed, "col", ncol).reshape(ncol, -1, LANES)
        col_names = parts if step == 0 else col_names
        source, listed = call(
            cols_kernel, "cols_half",
            (parts, col_names, srcmass, tiles_held, row_up, col_up, col_same, col_named),
            None, (jax.ShapeDtypeStruct((LANES, LANES), jnp.float32), sent),
            (values, values, f32(ncol, LANES, LANES)),
        )
        parts = to_all(listed, "z", nz).reshape(nz, -1, LANES)
        row_names = parts if step == 0 else row_names
        mine = call(
            spread_kernel, "spread", (parts, row_names), None, (full,), (f32(nz, LANES, LANES),)
        )
        other = lax.ppermute(mine, "core", swap)
    target = EPS * tgtmass - BACK * pair_lse2(mine, other)
    return (source.reshape(-1), target.reshape(-1))


def solution(mesh):
    nrow, ncol = mesh.devices.shape
    cores = 2
    finer = Mesh(mesh.devices.reshape(nrow // cores, cores, ncol), ("z", "core", "col"))
    row = ("z", "core")
    return jax.shard_map(
        local,
        mesh=finer,
        in_specs=(
            P(row, "col", None, None, None),
            P(row, "col", None),
            P(row, "col", None),
            P(row, "col"),
            P(row),
            P("col"),
            P("col"),
        ),
        out_specs=(P(row), P("col")),
        check_vma=False,
    )
```

time: 91.8 us -> 85.4 us (0.930)
  Pallas kernels: 16.6 us -> 11.9 us
  blocking collectives: 63.9 us -> 61.7 us
    pallas_call x6, Pallas kernels: 16.6 us -> 11.9 us  [call(): pl.pallas_call(kernel, name=name, out_shape=outs[0] if single else outs,...]
    all_to_all x4, blocking collectives: 63.9 us -> 61.7 us  [to_all(): return lax.all_to_all(copies, axes, 0, 0, tiled=True)]
where the time goes in v4:
time: 85.4 us; the launch traced here: 85.1 us
  blocking collectives  61.7 us (72%)
  Pallas kernels  11.9 us (14%)
  starting transfers between devices  7.44 us (9%)
  waiting for transfers between devices  1.8 us (2%)
  between operations  1.39 us (2%)
    all_to_all x4, blocking collectives, to_all(): return lax.all_to_all(copies, axes, 0, 0, tiled=True)  61.7 us
    pallas_call x6, Pallas kernels, call(): pl.pallas_call(kernel, name=name, out_shape=outs[0] if single else outs,...  11.9 us
    ppermute x2, starting transfers between devices, local(): other = lax.ppermute(mine, 'core', swap)  7.44 us
    ppermute x2, waiting for transfers between devices, local(): other = lax.ppermute(mine, 'core', swap)  1.8 us
  transfers between devices with their start and end apart: 2, of which 2 were waited for; matrix products, arithmetic and copies ran while one was open for 0% of the time, Pallas kernels for 0%

profile of v4, /device:TPU:1, one launch (start us, length us, event | category | flops | bytes accessed | tf_op | source)
XLA Modules:
  0.0 85.1 jit_solution(13985064141208095883)
XLA Ops:
  0.6 0.0 copy-start
  1.3 4.5 %first_rows.1 = (f32[72,128]{1,0:T(8,128)S(1)}, f32[64,128,128]{2,1,0:T(8,128)S(1)}, s32[64,128]{1,0:T(8,128)S(1)}, f32[64,128]{1,0:T(8,128)S(1)}, f32[8,128]{1,...) custom-call(s32[64]{0:T(128)} %bitcast.15, s32[64]{0:T(128)} %bitcast.16, ...), custom_call_target="tpu_custom_call" | custom-call | tf_op jit(solution)/shard_map/first_rows/pallas_call | solution.py:173
  5.9 0.0 copy-start.1
  5.9 18.6 %all_to_all.20.parts.names = f32[16,72,128]{2,1,0:T(8,128)S(1)} all-to-all(f32[16,72,128]{2,1,0:T(8,128)S(1)} %broadcast_in_dim.8), channel_id=1, replica_groups=mesh['z'=8,'core'=2,'col'=16] {'col'}, dimensions={0} | all-to-all | bytes 1179648 | tf_op jit(solution)/shard_map/all_to_all | solution.py:186
  24.5 0.0 copy-done
  24.5 2.8 %cols_half.2 = (f32[128,128]{1,0:T(8,128)}, f32[72,128]{1,0:T(8,128)S(1)}) custom-call(f32[16,72,128]{2,1,0:T(8,128)S(1)} %all_to_all.20.parts.names, f32[16,72,128]{2,1,0:T(8,128)S(1)} %all_to_all.20.parts.names, f32[128,128]{1,0:T(8,128)S(1)} %bitcast.10, f32[64,128,128]{2,1,0:T(8,128)S(1)} %get-tuple-element.14.cost, ...), custom_call_target="tpu_custom_call" | custom-call | tf_op jit(solution)/shard_map/cols_half/pallas_call | solution.py:173
  27.3 17.9 %all_to_all.21.parts.names = f32[8,72,128]{2,1,0:T(8,128)S(1)} all-to-all(f32[8,72,128]{2,1,0:T(8,128)S(1)} %broadcast_in_dim.9), channel_id=1, replica_groups=mesh['z'=8,'core'=2,'col'=16] {'z'}, dimensions={0} | all-to-all | bytes 589824 | tf_op jit(solution)/shard_map/all_to_all | solution.py:186
  45.1 0.4 spread.2.mine
  45.5 3.7 %collective-permute-start = (f32[128,128]{1,0:T(8,128)S(1)}, f32[128,128]{1,0:T(8,128)S(1)}, u32[]{:S(2)}, u32[]{:S(2)}) collective-permute-start(f32[128,128]{1,0:T(8,128)S(1)} %spread.2.mine), channel_id=1, source_target_pairs={{0,16},{16,0},{1,17},{17,1},{2,18},{18,2},{3,19},{19,3},{4,20},{20... | collective-permute-start | bytes 196616 | tf_op jit(solution)/shard_map/ppermute | solution.py:255
  49.2 0.9 %collective-permute-done.other = f32[128,128]{1,0:T(8,128)S(1)} collective-permute-done((f32[128,128]{1,0:T(8,128)S(1)}, f32[128,128]{1,0:T(8,128)S(1)}, u32[]{:S(2)}, u32[]{:S(2)}) %collective-permute-start) | collective-permute-done | bytes 65568 | tf_op jit(solution)/shard_map/ppermute | solution.py:255
  50.1 0.0 copy-done.1
  50.1 1.7 %rows_half.1 = f32[64,128]{1,0:T(8,128)S(1)} custom-call(f32[128,128]{1,0:T(8,128)S(1)} %spread.2.mine, f32[128,128]{1,0:T(8,128)S(1)} %collective-permute-done.other, f32[128,128]{1,0:T(8,128)S(1)} %bitcast.12, f32[64,128,128]{2,1,0:T(8,128)S(1)} %get-tuple-element.14.cost, s32[64,128]{1,0:T(8,128)S(1)} %get-tuple-element.15.row_up, ...), custom_call_target="tpu_custom_call" | custom-call | tf_op jit(solution)/shard_map/rows_half/pallas_call | solution.py:173
  51.9 13.7 %all_to_all.22.parts = f32[16,64,128]{2,1,0:T(8,128)S(1)} all-to-all(f32[16,64,128]{2,1,0:T(8,128)S(1)} %broadcast_in_dim.10), channel_id=1, replica_groups=mesh['z'=8,'core'=2,'col'=16] {'col'}, dimensions={0} | all-to-all | bytes 1048576 | tf_op jit(solution)/shard_map/all_to_all | solution.py:186
  65.5 2.3 %cols_half.3 = (f32[128,128]{1,0:T(8,128)}, f32[64,128]{1,0:T(8,128)S(1)}) custom-call(f32[16,64,128]{2,1,0:T(8,128)S(1)} %all_to_all.22.parts, f32[16,72,128]{2,1,0:T(8,128)S(1)} %all_to_all.20.parts.names, f32[128,128]{1,0:T(8,128)S(1)} %bitcast.11, f32[64,128,128]{2,1,0:T(8,128)S(1)} %get-tuple-element.14.cost, s32[64,128]{1,0:T(8,128)S(1)} %get-tuple-element.15.row_up, ...), custom_call_target="tpu_custom_call" | custom-call | tf_op jit(solution)/shard_map/cols_half/pallas_call | solution.py:173
  67.8 11.6 %all_to_all.23.parts = f32[8,64,128]{2,1,0:T(8,128)S(1)} all-to-all(f32[8,64,128]{2,1,0:T(8,128)S(1)} %broadcast_in_dim.11), channel_id=1, replica_groups=mesh['z'=8,'core'=2,'col'=16] {'z'}, dimensions={0} | all-to-all | bytes 524288 | tf_op jit(solution)/shard_map/all_to_all | solution.py:186
  79.5 0.4 spread.3
  79.8 3.7 %collective-permute-start.1 = (f32[128,128]{1,0:T(8,128)S(1)}, f32[128,128]{1,0:T(8,128)S(1)}, u32[]{:S(2)}, u32[]{:S(2)}) collective-permute-start(f32[128,128]{1,0:T(8,128)S(1)} %spread.3), channel_id=1, source_target_pairs={{0,16},{16,0},{1,17},{17,1},{2,18},{18,2},{3,19},{19,3},{4,20},{20... | collective-permute-start | bytes 196616 | tf_op jit(solution)/shard_map/ppermute | solution.py:255
  83.5 0.9 %collective-permute-done.1 = f32[128,128]{1,0:T(8,128)S(1)} collective-permute-done((f32[128,128]{1,0:T(8,128)S(1)}, f32[128,128]{1,0:T(8,128)S(1)}, u32[]{:S(2)}, u32[]{:S(2)}) %collective-permute-start.1) | collective-permute-done | bytes 65568 | tf_op jit(solution)/shard_map/ppermute | solution.py:255
  84.4 0.7 subtract_bitcast_fusion
  (4 shorter events, 0.1 us)
Async XLA Ops:
  0.6 23.9 %copy-start = (f32[16384]{0:T(1024)S(1)}, f32[16384]{0:T(1024)}, u32[]{:S(2)}) copy-start(f32[16384]{0:T(1024)} %param.11) | copy-start | bytes 196612
  5.9 44.2 %copy-start.1 = (f32[16384]{0:T(1024)S(1)}, f32[16384]{0:T(1024)}, u32[]{:S(2)}) copy-start(f32[16384]{0:T(1024)} %param.12) | copy-start | bytes 196612
  45.5 4.6 %collective-permute-start = (f32[128,128]{1,0:T(8,128)S(1)}, f32[128,128]{1,0:T(8,128)S(1)}, u32[]{:S(2)}, u32[]{:S(2)}) collective-permute-start(f32[128,128]{1,0:T(8,128)S(1)} %spread.2.mine), channel_id=1, source_target_pairs={{0,16},{16,0},{1,17},{17,1},{2,18},{18,2},{3,19},{19,3},{4,20},{20... | collective-permute-start | bytes 196616 | tf_op jit(solution)/shard_map/ppermute | solution.py:255
  79.8 4.6 %collective-permute-start.1 = (f32[128,128]{1,0:T(8,128)S(1)}, f32[128,128]{1,0:T(8,128)S(1)}, u32[]{:S(2)}, u32[]{:S(2)}) collective-permute-start(f32[128,128]{1,0:T(8,128)S(1)} %spread.3), channel_id=1, source_target_pairs={{0,16},{16,0},{1,17},{17,1},{2,18},{18,2},{3,19},{19,3},{4,20},{20... | collective-permute-start | bytes 196616 | tf_op jit(solution)/shard_map/ppermute | solution.py:255

commit v5 on v4

--- a/solution.py
+++ b/solution.py
@@ -14,7 +14,10 @@
 BACK = EPS * LN2
 NONE = -1.0e30
 LANES = 128
-CHUNK = 8
+SLOTS = 64
+RING = 4
+CHUNK = 16
+AHEAD = 2
 LIMIT = 24 << 20
 
 
@@ -57,6 +60,7 @@
 def merged(values, upright, same, named, out):
     slots = values.shape[0]
     mine = upright[...]
+    values[...] = jnp.where(mine >= 0, values[...], 0.0)
     top = jnp.full((slots, LANES), NONE, jnp.float32)
     for s in range(slots):
         hit = mine == upright[pl.ds(s, 1), :]
@@ -72,28 +76,30 @@
         out[slots:, :] = named[...]
 
 
+def placed(rows, ids):
+    block = lax.broadcasted_iota(jnp.int32, (LANES, LANES), 0).astype(jnp.float32)
+    ones = jnp.ones((SLOTS, LANES), jnp.bfloat16)
+    none = jnp.zeros((SLOTS, LANES), jnp.bfloat16)
+    pick = jnp.where(block == ids, 1.0, 0.0).astype(jnp.bfloat16)
+    both = jnp.dot(
+        jnp.concatenate([pick, pick], axis=1),
+        jnp.concatenate(
+            [jnp.concatenate([*pieces(rows), none], axis=0), jnp.concatenate([ones, none, none, none], axis=0)],
+            axis=1,
+        ),
+        preferred_element_type=jnp.float32,
+    )
+    return jnp.where(both[:, LANES:] > 0.5, both[:, :LANES], NONE)
+
+
 def spread(parts, names, dense):
-    peers = parts.shape[0]
-    slots = LANES // 2
-    block = lax.broadcasted_iota(jnp.int32, (LANES, LANES), 0).astype(jnp.float32)
-    ones = jnp.ones((slots, LANES), jnp.bfloat16)
-    none = jnp.zeros((slots, LANES), jnp.bfloat16)
-    hits = jnp.concatenate([ones, none, none, none], axis=0)
     top = jnp.full((LANES, LANES), NONE, jnp.float32)
-    for d in range(peers):
-        pick = jnp.where(block == names[d, slots : slots + 1, :], 1.0, 0.0).astype(jnp.bfloat16)
-        high, middle, low = pieces(parts[d, :slots, :])
-        cut = jnp.concatenate([high, middle, low, none], axis=0)
-        both = jnp.dot(
-            jnp.concatenate([pick, pick], axis=1),
-            jnp.concatenate([cut, hits], axis=1),
-            preferred_element_type=jnp.float32,
-        )
-        value = jnp.where(both[:, LANES:] > 0.5, both[:, :LANES], NONE)
+    for d in range(parts.shape[0]):
+        value = placed(parts[d, :SLOTS, :], names[d, SLOTS : SLOTS + 1, :])
         dense[d] = value
         top = jnp.maximum(top, value)
     total = jnp.zeros((LANES, LANES), jnp.float32)
-    for d in range(peers):
+    for d in range(parts.shape[0]):
         total = total + jnp.exp2(dense[d] - top)
     return jnp.maximum(top + jnp.log2(total), NONE)
 
@@ -111,19 +117,17 @@
     return top + jnp.log2(jnp.sum(jnp.exp2(scores - top), axis=0, keepdims=True))
 
 
-def tiles(tile_lse, cost, picked, values, chunks=None):
-    for k in range(cost.shape[0] // CHUNK):
-        if chunks:
-            chunks[k].wait()
-        for s in range(k * CHUNK, (k + 1) * CHUNK):
-            values[pl.ds(s, 1), :] = tile_lse(picked[pl.ds(s, 1), :], cost[s])
+def tiles(tile_lse, cost, picked, values):
+    for s in range(cost.shape[0]):
+        values[pl.ds(s, 1), :] = tile_lse(picked[pl.ds(s, 1), :], cost[s])
 
 
 def first_rows_kernel(
-    rows_in, cols_in, cost_in, pot_in, count,
+    rows_in, cols_in, cost_in, pot_in, count_in,
     out, cost, row_up, row_same, row_named, col_up, col_same, col_named,
     rows, cols, pot, sems, cost_sems, scratch, values, picked,
 ):
+    count = count_in[0, 0]
     small = []
     for k, (src, dst) in enumerate(((cols_in, cols), (rows_in, rows), (pot_in, pot))):
         small.append(pltpu.make_async_copy(src, dst, sems.at[k]))
@@ -132,14 +136,24 @@
     for k in range(cost.shape[0] // CHUNK):
         at = pl.ds(k * CHUNK, CHUNK)
         chunks.append(pltpu.make_async_copy(cost_in.at[at], cost.at[at], cost_sems.at[k]))
-        chunks[-1].start()
-    small[0].wait()
-    note_ids(cols, count[0, 0], col_up, col_same, col_named, scratch)
-    small[1].wait()
-    note_ids(rows, count[0, 0], row_up, row_same, row_named, scratch)
-    small[2].wait()
+        if k < AHEAD:
+            pl.when(count > k * CHUNK)(chunks[k].start)
+    values[...] = jnp.zeros(values.shape, jnp.float32)
+    for copy in small:
+        copy.wait()
+    note_ids(cols, count, col_up, col_same, col_named, scratch)
     picked[...] = gathered(pot[...], col_up)
-    tiles(one_row_tile, cost, picked, values, chunks)
+    note_ids(rows, count, row_up, row_same, row_named, scratch)
+    for k, chunk in enumerate(chunks):
+
+        @pl.when(count > k * CHUNK)
+        def _():
+            chunk.wait()
+            if k + AHEAD < len(chunks):
+                pl.when(count > (k + AHEAD) * CHUNK)(chunks[k + AHEAD].start)
+            for s in range(k * CHUNK, (k + 1) * CHUNK):
+                values[pl.ds(s, 1), :] = one_row_tile(picked[pl.ds(s, 1), :], cost[s])
+
     merged(values, row_up, row_same, row_named, out)
 
 
@@ -151,12 +165,23 @@
 
 
 def cols_kernel(
-    parts, names, logmass, cost, row_up, col_up, col_same, col_named, pot, out, values, picked, dense
+    one, two, three, four, logmass, cost, row_up, col_up, col_same, col_named, pot, out, values, picked
 ):
-    pot[...] = EPS * logmass[...] - BACK * spread(parts, names, dense)
+    pot[...] = EPS * logmass[...] - BACK * ring_lse2([x[...] for x in (one, two, three, four)])
     picked[...] = gathered(pot[...], row_up)
     tiles(one_col_tile, cost, picked, values)
     merged(values, col_up, col_same, col_named, out)
+
+
+def ring_lse2(parts):
+    top = jnp.maximum(jnp.maximum(parts[0], parts[2]), jnp.maximum(parts[1], parts[3]))
+    own, after, across, before = (jnp.exp2(part - top) for part in parts)
+    return jnp.maximum(top + jnp.log2((own + across) + (after + before)), NONE)
+
+
+def ring_kernel(*refs):
+    parts, names, out = refs[:4], refs[4:8], refs[8]
+    out[...] = ring_lse2([placed(part[:SLOTS, :], name[SLOTS : SLOTS + 1, :]) for part, name in zip(parts, names)])
 
 
 def spread_kernel(parts, names, out, dense):
@@ -181,6 +206,22 @@
     )(*operands)
 
 
+def ring(value, nz, stage):
+    got = {0: value}
+    for hop in (2, 1, 3):
+        pairs = []
+        for z in range(nz):
+            for core in range(2):
+                for x in range(RING):
+                    for y in range(RING):
+                        along_x = core == stage
+                        to = ((x + hop) % RING, y) if along_x else (x, (y + hop) % RING)
+                        row = (z * 2 + core) * RING
+                        pairs.append(((row + x) * RING + y, (row + to[0]) * RING + to[1]))
+        got[hop] = lax.ppermute(value, ("z", "core", "col"), pairs)
+    return [got[hop] for hop in range(RING)]
+
+
 def to_all(value, axes, peers):
     copies = jnp.broadcast_to(value[None], (peers, *value.shape))
     return lax.all_to_all(copies, axes, 0, 0, tiled=True)
@@ -195,7 +236,6 @@
     count = tile_count.reshape(1, 1)
     srcmass = source_logmass.reshape(-1, LANES)
     tgtmass = target_logmass.reshape(-1, LANES)
-    ncol = lax.axis_size("col")
     nz = lax.axis_size("z")
     swap = [(0, 1), (1, 0)]
     slots = cost.shape[0]
@@ -239,13 +279,14 @@
                 (mine, other, tgtmass, tiles_held, row_up, row_same, row_named, col_up),
                 None, (sent,), (values, values),
             )
-        parts = to_all(listed, "col", ncol).reshape(ncol, -1, LANES)
+        parts = ring(listed, nz, 0)
         col_names = parts if step == 0 else col_names
+        part = call(ring_kernel, "ring", (*parts, *col_names), None, (full,), ())
         source, listed = call(
             cols_kernel, "cols_half",
-            (parts, col_names, srcmass, tiles_held, row_up, col_up, col_same, col_named),
+            (*ring(part, nz, 1), srcmass, tiles_held, row_up, col_up, col_same, col_named),
             None, (jax.ShapeDtypeStruct((LANES, LANES), jnp.float32), sent),
-            (values, values, f32(ncol, LANES, LANES)),
+            (values, values),
         )
         parts = to_all(listed, "z", nz).reshape(nz, -1, LANES)
         row_names = parts if step == 0 else row_names

time: 85.4 us -> 80.9 us (0.947)
  blocking collectives: 61.7 us -> 28.8 us
  waiting for transfers between devices: 1.8 us -> 17.7 us
  starting transfers between devices: 7.44 us -> 21.6 us
  Pallas kernels: 11.9 us -> 10.4 us
    all_to_all x4 -> x2, blocking collectives: 61.7 us -> 28.8 us  [to_all(): return lax.all_to_all(copies, axes, 0, 0, tiled=True)]
    ppermute x0 -> x12, waiting for transfers between devices: none -> 15.8 us  [ring(): got[hop] = lax.ppermute(value, ('z', 'core', 'col'), pairs)]
    ppermute x0 -> x12, starting transfers between devices: none -> 11.5 us  [ring(): got[hop] = lax.ppermute(value, ('z', 'core', 'col'), pairs)]
    ppermute x2, starting transfers between devices: 7.44 us -> 10.1 us  [local(): other = lax.ppermute(mine, 'core', swap)]
    pallas_call x6 -> x8, Pallas kernels: 11.9 us -> 10.4 us  [call(): pl.pallas_call(kernel, name=name, out_shape=outs[0] if single else outs,...]
  transfers between devices with their start and end apart: 2 -> 14, of which waited for: 2 -> 13; matrix products, arithmetic and copies ran while one was open for 0% -> 0% of each run, Pallas kernels for 0% -> 0%
where the time goes in v5:
time: 80.9 us; the launch traced here: 80.6 us
  blocking collectives  28.8 us (36%)
  starting transfers between devices  21.6 us (27%)
  waiting for transfers between devices  17.7 us (22%)
  Pallas kernels  10.4 us (13%)
  between operations  1.4 us (2%)
    all_to_all x2, blocking collectives, to_all(): return lax.all_to_all(copies, axes, 0, 0, tiled=True)  28.8 us
    ppermute x12, waiting for transfers between devices, ring(): got[hop] = lax.ppermute(value, ('z', 'core', 'col'), pairs)  15.8 us
    ppermute x12, starting transfers between devices, ring(): got[hop] = lax.ppermute(value, ('z', 'core', 'col'), pairs)  11.5 us
    pallas_call x8, Pallas kernels, call(): pl.pallas_call(kernel, name=name, out_shape=outs[0] if single else outs,...  10.4 us
    ppermute x2, starting transfers between devices, local(): other = lax.ppermute(mine, 'core', swap)  10.1 us
    ppermute x2, waiting for transfers between devices, local(): other = lax.ppermute(mine, 'core', swap)  1.8 us
  transfers between devices with their start and end apart: 14, of which 13 were waited for; matrix products, arithmetic and copies ran while one was open for 0% of the time, Pallas kernels for 0%

profile of v5, /device:TPU:1, one launch (start us, length us, event | category | flops | bytes accessed | tf_op | source)
XLA Modules:
  0.0 80.6 jit_solution(16544633634038949996)
XLA Ops:
  1.3 3.5 %first_rows.1 = (f32[72,128]{1,0:T(8,128)S(1)}, f32[64,128,128]{2,1,0:T(8,128)S(1)}, s32[64,128]{1,0:T(8,128)S(1)}, f32[64,128]{1,0:T(8,128)S(1)}, f32[8,128]{1,...) custom-call(s32[64]{0:T(128)} %bitcast.15, s32[64]{0:T(128)} %bitcast.16, ...), custom_call_target="tpu_custom_call" | custom-call | tf_op jit(solution)/shard_map/first_rows/pallas_call | solution.py:198
  4.8 2.8 %collective-permute-start.2 = (f32[72,128]{1,0:T(8,128)S(1)}, f32[72,128]{1,0:T(8,128)S(1)}, u32[]{:S(2)}, u32[]{:S(2)}) collective-permute-start(f32[72,128]{1,0:T(8,128)S(1)} %get-tuple-element.13.refs_0_.refs_4_), channel_id=1, source_target_pairs={{0,12},{1,13},{2,14},{3,15},{4,0},{5,1},{6,2},{7,3},{8,4},{9,5},{1... | collective-permute-start | bytes 110600 | tf_op jit(solution)/shard_map/ppermute | solution.py:221
  7.6 1.2 %collective-permute-start.1 = (f32[72,128]{1,0:T(8,128)S(1)}, f32[72,128]{1,0:T(8,128)S(1)}, u32[]{:S(2)}, u32[]{:S(2)}) collective-permute-start(f32[72,128]{1,0:T(8,128)S(1)} %get-tuple-element.13.refs_0_.refs_4_), channel_id=1, source_target_pairs={{0,8},{1,9},{2,10},{3,11},{4,12},{5,13},{6,14},{7,15},{8,0},{9,1},... | collective-permute-start | bytes 110600 | tf_op jit(solution)/shard_map/ppermute | solution.py:221
  8.8 3.1 %collective-permute-done.1.refs_2_.refs_6_ = f32[72,128]{1,0:T(8,128)S(1)} collective-permute-done((f32[72,128]{1,0:T(8,128)S(1)}, f32[72,128]{1,0:T(8,128)S(1)}, u32[]{:S(2)}, u32[]{:S(2)}) %collective-permute-start.1) | collective-permute-done | bytes 36896 | tf_op jit(solution)/shard_map/ppermute | solution.py:221
  11.9 1.1 %collective-permute-done.refs_1_.refs_5_ = f32[72,128]{1,0:T(8,128)S(1)} collective-permute-done((f32[72,128]{1,0:T(8,128)S(1)}, f32[72,128]{1,0:T(8,128)S(1)}, u32[]{:S(2)}, u32[]{:S(2)}) %collective-permute-start) | collective-permute-done | bytes 36896 | tf_op jit(solution)/shard_map/ppermute | solution.py:221
  13.2 2.8 %collective-permute-start.5 = (f32[128,128]{1,0:T(8,128)S(1)}, f32[128,128]{1,0:T(8,128)S(1)}, u32[]{:S(2)}, u32[]{:S(2)}) collective-permute-start(f32[128,128]{1,0:T(8,128)S(1)} %ring.2.one), channel_id=1, source_target_pairs={{0,3},{1,0},{2,1},{3,2},{4,7},{5,4},{6,5},{7,6},{8,11},{9,8},{10,9... | collective-permute-start | bytes 196616 | tf_op jit(solution)/shard_map/ppermute | solution.py:221
  16.2 0.5 collective-permute-start.3
  16.6 0.7 collective-permute-done.5.four
  17.3 3.4 %collective-permute-done.4.three = f32[128,128]{1,0:T(8,128)S(1)} collective-permute-done((f32[128,128]{1,0:T(8,128)S(1)}, f32[128,128]{1,0:T(8,128)S(1)}, u32[]{:S(2)}, u32[]{:S(2)}) %collective-permute-start.4) | collective-permute-done | bytes 65568 | tf_op jit(solution)/shard_map/ppermute | solution.py:221
  20.7 0.5 collective-permute-done.3.two
  21.2 2.2 %cols_half.2 = (f32[128,128]{1,0:T(8,128)}, f32[72,128]{1,0:T(8,128)S(1)}) custom-call(f32[128,128]{1,0:T(8,128)S(1)} %ring.2.one, f32[128,128]{1,0:T(8,128)S(1)} %collective-permute-done.3.two, f32[128,128]{1,0:T(8,128)S(1)} %collective-permute-done.4.three, f32[128,128]{1,0:T(8,128)S(1)} %collective-permute-done.5.four, f32[128,128]{1,0:T(8,128)S(1)} %bitcast.10, ...), custom_call_target="tpu_custom_call" | custom-call | tf_op jit(solution)/shard_map/cols_half/pallas_call | solution.py:198
  23.5 17.0 %all_to_all.10.parts.names = f32[8,72,128]{2,1,0:T(8,128)S(1)} all-to-all(f32[8,72,128]{2,1,0:T(8,128)S(1)} %broadcast_in_dim.4), channel_id=1, replica_groups=mesh['z'=8,'core'=2,'col'=16] {'z'}, dimensions={0} | all-to-all | bytes 589824 | tf_op jit(solution)/shard_map/all_to_all | solution.py:227
  40.5 0.4 spread.2.mine
  40.8 5.5 %collective-permute-start.6 = (f32[128,128]{1,0:T(8,128)S(1)}, f32[128,128]{1,0:T(8,128)S(1)}, u32[]{:S(2)}, u32[]{:S(2)}) collective-permute-start(f32[128,128]{1,0:T(8,128)S(1)} %spread.2.mine), channel_id=1, source_target_pairs={{0,16},{16,0},{1,17},{17,1},{2,18},{18,2},{3,19},{19,3},{4,20},{20... | collective-permute-start | bytes 196616 | tf_op jit(solution)/shard_map/ppermute | solution.py:296
  46.3 0.9 %collective-permute-done.6.other = f32[128,128]{1,0:T(8,128)S(1)} collective-permute-done((f32[128,128]{1,0:T(8,128)S(1)}, f32[128,128]{1,0:T(8,128)S(1)}, u32[]{:S(2)}, u32[]{:S(2)}) %collective-permute-start.6) | collective-permute-done | bytes 65568 | tf_op jit(solution)/shard_map/ppermute | solution.py:296
  47.2 1.7 %rows_half.1.refs_0_ = f32[64,128]{1,0:T(8,128)S(1)} custom-call(f32[128,128]{1,0:T(8,128)S(1)} %spread.2.mine, f32[128,128]{1,0:T(8,128)S(1)} %collective-permute-done.6.other, f32[128,128]{1,0:T(8,128)S(1)} %bitcast.12, f32[64,128,128]{2,1,0:T(8,128)S(1)} %get-tuple-element.14.cost, s32[64,128]{1,0:T(8,128)S(1)} %get-tuple-element.15.row_up, ...), custom_call_target="tpu_custom_call" | custom-call | tf_op jit(solution)/shard_map/rows_half/pallas_call | solution.py:198
  48.9 0.4 collective-permute-start.9
  49.3 1.0 %collective-permute-start.8 = (f32[64,128]{1,0:T(8,128)S(1)}, f32[64,128]{1,0:T(8,128)S(1)}, u32[]{:S(2)}, u32[]{:S(2)}) collective-permute-start(f32[64,128]{1,0:T(8,128)S(1)} %rows_half.1.refs_0_), channel_id=1, source_target_pairs={{0,8},{1,9},{2,10},{3,11},{4,12},{5,13},{6,14},{7,15},{8,0},{9,1},... | collective-permute-start | bytes 98312 | tf_op jit(solution)/shard_map/ppermute | solution.py:221
  50.2 0.7 collective-permute-start.7
  50.9 0.9 %collective-permute-done.9.refs_3_ = f32[64,128]{1,0:T(8,128)S(1)} collective-permute-done((f32[64,128]{1,0:T(8,128)S(1)}, f32[64,128]{1,0:T(8,128)S(1)}, u32[]{:S(2)}, u32[]{:S(2)}) %collective-permute-start.9) | collective-permute-done | bytes 32800 | tf_op jit(solution)/shard_map/ppermute | solution.py:221
  51.8 1.8 %collective-permute-done.8.refs_2_ = f32[64,128]{1,0:T(8,128)S(1)} collective-permute-done((f32[64,128]{1,0:T(8,128)S(1)}, f32[64,128]{1,0:T(8,128)S(1)}, u32[]{:S(2)}, u32[]{:S(2)}) %collective-permute-start.8) | collective-permute-done | bytes 32800 | tf_op jit(solution)/shard_map/ppermute | solution.py:221
  53.6 1.0 %collective-permute-done.7.refs_1_ = f32[64,128]{1,0:T(8,128)S(1)} collective-permute-done((f32[64,128]{1,0:T(8,128)S(1)}, f32[64,128]{1,0:T(8,128)S(1)}, u32[]{:S(2)}, u32[]{:S(2)}) %collective-permute-start.7) | collective-permute-done | bytes 32800 | tf_op jit(solution)/shard_map/ppermute | solution.py:221
  54.9 1.3 %collective-permute-start.11 = (f32[128,128]{1,0:T(8,128)S(1)}, f32[128,128]{1,0:T(8,128)S(1)}, u32[]{:S(2)}, u32[]{:S(2)}) collective-permute-start(f32[128,128]{1,0:T(8,128)S(1)} %ring.3.one), channel_id=1, source_target_pairs={{0,2},{1,3},{2,0},{3,1},{4,6},{5,7},{6,4},{7,5},{8,10},{9,11},{10,... | collective-permute-start | bytes 196616 | tf_op jit(solution)/shard_map/ppermute | solution.py:221
  56.1 0.8 collective-permute-start.10
  56.9 1.1 %collective-permute-done.12.four = f32[128,128]{1,0:T(8,128)S(1)} collective-permute-done((f32[128,128]{1,0:T(8,128)S(1)}, f32[128,128]{1,0:T(8,128)S(1)}, u32[]{:S(2)}, u32[]{:S(2)}) %collective-permute-start.12) | collective-permute-done | bytes 65568 | tf_op jit(solution)/shard_map/ppermute | solution.py:221
  58.0 1.6 %collective-permute-done.11.three = f32[128,128]{1,0:T(8,128)S(1)} collective-permute-done((f32[128,128]{1,0:T(8,128)S(1)}, f32[128,128]{1,0:T(8,128)S(1)}, u32[]{:S(2)}, u32[]{:S(2)}) %collective-permute-start.11) | collective-permute-done | bytes 65568 | tf_op jit(solution)/shard_map/ppermute | solution.py:221
  59.6 0.9 %collective-permute-done.10.two = f32[128,128]{1,0:T(8,128)S(1)} collective-permute-done((f32[128,128]{1,0:T(8,128)S(1)}, f32[128,128]{1,0:T(8,128)S(1)}, u32[]{:S(2)}, u32[]{:S(2)}) %collective-permute-start.10) | collective-permute-done | bytes 65568 | tf_op jit(solution)/shard_map/ppermute | solution.py:221
  60.5 1.8 %cols_half.3 = (f32[128,128]{1,0:T(8,128)}, f32[64,128]{1,0:T(8,128)S(1)}) custom-call(f32[128,128]{1,0:T(8,128)S(1)} %ring.3.one, f32[128,128]{1,0:T(8,128)S(1)} %collective-permute-done.10.two, f32[128,128]{1,0:T(8,128)S(1)} %collective-permute-done.11.three, f32[128,128]{1,0:T(8,128)S(1)} %collective-permute-done.12.four, f32[128,128]{1,0:T(8,128)S(1)} %bitcast.11, ...), custom_call_target="tpu_custom_call" | custom-call | tf_op jit(solution)/shard_map/cols_half/pallas_call | solution.py:198
  62.3 11.8 %all_to_all.11.parts = f32[8,64,128]{2,1,0:T(8,128)S(1)} all-to-all(f32[8,64,128]{2,1,0:T(8,128)S(1)} %broadcast_in_dim.5), channel_id=1, replica_groups=mesh['z'=8,'core'=2,'col'=16] {'z'}, dimensions={0} | all-to-all | bytes 524288 | tf_op jit(solution)/shard_map/all_to_all | solution.py:227
  74.5 4.6 %collective-permute-start.13 = (f32[128,128]{1,0:T(8,128)S(1)}, f32[128,128]{1,0:T(8,128)S(1)}, u32[]{:S(2)}, u32[]{:S(2)}) collective-permute-start(f32[128,128]{1,0:T(8,128)S(1)} %spread.3), channel_id=1, source_target_pairs={{0,16},{16,0},{1,17},{17,1},{2,18},{18,2},{3,19},{19,3},{4,20},{20... | collective-permute-start | bytes 196616 | tf_op jit(solution)/shard_map/ppermute | solution.py:296
  79.1 0.9 %collective-permute-done.13 = f32[128,128]{1,0:T(8,128)S(1)} collective-permute-done((f32[128,128]{1,0:T(8,128)S(1)}, f32[128,128]{1,0:T(8,128)S(1)}, u32[]{:S(2)}, u32[]{:S(2)}) %collective-permute-start.13) | collective-permute-done | bytes 65568 | tf_op jit(solution)/shard_map/ppermute | solution.py:296
  80.0 0.7 subtract_bitcast_fusion
  (13 shorter events, 1.2 us)
Async XLA Ops:
  0.6 20.6 %copy-start = (f32[16384]{0:T(1024)S(1)}, f32[16384]{0:T(1024)}, u32[]{:S(2)}) copy-start(f32[16384]{0:T(1024)} %param.11) | copy-start | bytes 196612
  4.8 42.4 %copy-start.1 = (f32[16384]{0:T(1024)S(1)}, f32[16384]{0:T(1024)}, u32[]{:S(2)}) copy-start(f32[16384]{0:T(1024)} %param.12) | copy-start | bytes 196612
  4.8 4.0 %collective-permute-start.2 = (f32[72,128]{1,0:T(8,128)S(1)}, f32[72,128]{1,0:T(8,128)S(1)}, u32[]{:S(2)}, u32[]{:S(2)}) collective-permute-start(f32[72,128]{1,0:T(8,128)S(1)} %get-tuple-element.13.refs_0_.refs_4_), channel_id=1, source_target_pairs={{0,12},{1,13},{2,14},{3,15},{4,0},{5,1},{6,2},{7,3},{8,4},{9,5},{1... | collective-permute-start | bytes 110600 | tf_op jit(solution)/shard_map/ppermute | solution.py:221
  7.6 4.3 %collective-permute-start.1 = (f32[72,128]{1,0:T(8,128)S(1)}, f32[72,128]{1,0:T(8,128)S(1)}, u32[]{:S(2)}, u32[]{:S(2)}) collective-permute-start(f32[72,128]{1,0:T(8,128)S(1)} %get-tuple-element.13.refs_0_.refs_4_), channel_id=1, source_target_pairs={{0,8},{1,9},{2,10},{3,11},{4,12},{5,13},{6,14},{7,15},{8,0},{9,1},... | collective-permute-start | bytes 110600 | tf_op jit(solution)/shard_map/ppermute | solution.py:221
  8.8 4.1 %collective-permute-start = (f32[72,128]{1,0:T(8,128)S(1)}, f32[72,128]{1,0:T(8,128)S(1)}, u32[]{:S(2)}, u32[]{:S(2)}) collective-permute-start(f32[72,128]{1,0:T(8,128)S(1)} %get-tuple-element.13.refs_0_.refs_4_), channel_id=1, source_target_pairs={{0,4},{1,5},{2,6},{3,7},{4,8},{5,9},{6,10},{7,11},{8,12},{9,13},{1... | collective-permute-start | bytes 110600 | tf_op jit(solution)/shard_map/ppermute | solution.py:221
  13.2 4.1 %collective-permute-start.5 = (f32[128,128]{1,0:T(8,128)S(1)}, f32[128,128]{1,0:T(8,128)S(1)}, u32[]{:S(2)}, u32[]{:S(2)}) collective-permute-start(f32[128,128]{1,0:T(8,128)S(1)} %ring.2.one), channel_id=1, source_target_pairs={{0,3},{1,0},{2,1},{3,2},{4,7},{5,4},{6,5},{7,6},{8,11},{9,8},{10,9... | collective-permute-start | bytes 196616 | tf_op jit(solution)/shard_map/ppermute | solution.py:221
  16.0 4.7 %collective-permute-start.4 = (f32[128,128]{1,0:T(8,128)S(1)}, f32[128,128]{1,0:T(8,128)S(1)}, u32[]{:S(2)}, u32[]{:S(2)}) collective-permute-start(f32[128,128]{1,0:T(8,128)S(1)} %ring.2.one), channel_id=1, source_target_pairs={{0,2},{1,3},{2,0},{3,1},{4,6},{5,7},{6,4},{7,5},{8,10},{9,11},{10,... | collective-permute-start | bytes 196616 | tf_op jit(solution)/shard_map/ppermute | solution.py:221
  16.2 5.0 %collective-permute-start.3 = (f32[128,128]{1,0:T(8,128)S(1)}, f32[128,128]{1,0:T(8,128)S(1)}, u32[]{:S(2)}, u32[]{:S(2)}) collective-permute-start(f32[128,128]{1,0:T(8,128)S(1)} %ring.2.one), channel_id=1, source_target_pairs={{0,1},{1,2},{2,3},{3,0},{4,5},{5,6},{6,7},{7,4},{8,9},{9,10},{10,1... | collective-permute-start | bytes 196616 | tf_op jit(solution)/shard_map/ppermute | solution.py:221
  40.8 6.4 %collective-permute-start.6 = (f32[128,128]{1,0:T(8,128)S(1)}, f32[128,128]{1,0:T(8,128)S(1)}, u32[]{:S(2)}, u32[]{:S(2)}) collective-permute-start(f32[128,128]{1,0:T(8,128)S(1)} %spread.2.mine), channel_id=1, source_target_pairs={{0,16},{16,0},{1,17},{17,1},{2,18},{18,2},{3,19},{19,3},{4,20},{20... | collective-permute-start | bytes 196616 | tf_op jit(solution)/shard_map/ppermute | solution.py:296
  48.9 2.8 %collective-permute-start.9 = (f32[64,128]{1,0:T(8,128)S(1)}, f32[64,128]{1,0:T(8,128)S(1)}, u32[]{:S(2)}, u32[]{:S(2)}) collective-permute-start(f32[64,128]{1,0:T(8,128)S(1)} %rows_half.1.refs_0_), channel_id=1, source_target_pairs={{0,12},{1,13},{2,14},{3,15},{4,0},{5,1},{6,2},{7,3},{8,4},{9,5},{1... | collective-permute-start | bytes 98312 | tf_op jit(solution)/shard_map/ppermute | solution.py:221
  49.3 4.3 %collective-permute-start.8 = (f32[64,128]{1,0:T(8,128)S(1)}, f32[64,128]{1,0:T(8,128)S(1)}, u32[]{:S(2)}, u32[]{:S(2)}) collective-permute-start(f32[64,128]{1,0:T(8,128)S(1)} %rows_half.1.refs_0_), channel_id=1, source_target_pairs={{0,8},{1,9},{2,10},{3,11},{4,12},{5,13},{6,14},{7,15},{8,0},{9,1},... | collective-permute-start | bytes 98312 | tf_op jit(solution)/shard_map/ppermute | solution.py:221
  50.2 4.3 %collective-permute-start.7 = (f32[64,128]{1,0:T(8,128)S(1)}, f32[64,128]{1,0:T(8,128)S(1)}, u32[]{:S(2)}, u32[]{:S(2)}) collective-permute-start(f32[64,128]{1,0:T(8,128)S(1)} %rows_half.1.refs_0_), channel_id=1, source_target_pairs={{0,4},{1,5},{2,6},{3,7},{4,8},{5,9},{6,10},{7,11},{8,12},{9,13},{1... | collective-permute-start | bytes 98312 | tf_op jit(solution)/shard_map/ppermute | solution.py:221
  54.8 3.2 %collective-permute-start.12 = (f32[128,128]{1,0:T(8,128)S(1)}, f32[128,128]{1,0:T(8,128)S(1)}, u32[]{:S(2)}, u32[]{:S(2)}) collective-permute-start(f32[128,128]{1,0:T(8,128)S(1)} %ring.3.one), channel_id=1, source_target_pairs={{0,3},{1,0},{2,1},{3,2},{4,7},{5,4},{6,5},{7,6},{8,11},{9,8},{10,9... | collective-permute-start | bytes 196616 | tf_op jit(solution)/shard_map/ppermute | solution.py:221
  54.9 4.7 %collective-permute-start.11 = (f32[128,128]{1,0:T(8,128)S(1)}, f32[128,128]{1,0:T(8,128)S(1)}, u32[]{:S(2)}, u32[]{:S(2)}) collective-permute-start(f32[128,128]{1,0:T(8,128)S(1)} %ring.3.one), channel_id=1, source_target_pairs={{0,2},{1,3},{2,0},{3,1},{4,6},{5,7},{6,4},{7,5},{8,10},{9,11},{10,... | collective-permute-start | bytes 196616 | tf_op jit(solution)/shard_map/ppermute | solution.py:221
  56.1 4.3 %collective-permute-start.10 = (f32[128,128]{1,0:T(8,128)S(1)}, f32[128,128]{1,0:T(8,128)S(1)}, u32[]{:S(2)}, u32[]{:S(2)}) collective-permute-start(f32[128,128]{1,0:T(8,128)S(1)} %ring.3.one), channel_id=1, source_target_pairs={{0,1},{1,2},{2,3},{3,0},{4,5},{5,6},{6,7},{7,4},{8,9},{9,10},{10,1... | collective-permute-start | bytes 196616 | tf_op jit(solution)/shard_map/ppermute | solution.py:221
  74.5 5.5 %collective-permute-start.13 = (f32[128,128]{1,0:T(8,128)S(1)}, f32[128,128]{1,0:T(8,128)S(1)}, u32[]{:S(2)}, u32[]{:S(2)}) collective-permute-start(f32[128,128]{1,0:T(8,128)S(1)} %spread.3), channel_id=1, source_target_pairs={{0,16},{16,0},{1,17},{17,1},{2,18},{18,2},{3,19},{19,3},{4,20},{20... | collective-permute-start | bytes 196616 | tf_op jit(solution)/shard_map/ppermute | solution.py:296

commit v6 on v5

--- a/solution.py
+++ b/solution.py
@@ -57,7 +57,7 @@
     )
 
 
-def merged(values, upright, same, named, out):
+def merged(values, upright, same, out):
     slots = values.shape[0]
     mine = upright[...]
     values[...] = jnp.where(mine >= 0, values[...], 0.0)
@@ -72,8 +72,6 @@
         preferred_element_type=jnp.float32,
     )
     out[:slots, :] = top + jnp.log2(mass)
-    if out.shape[0] > slots:
-        out[slots:, :] = named[...]
 
 
 def placed(rows, ids):
@@ -104,15 +102,20 @@
     return jnp.maximum(top + jnp.log2(total), NONE)
 
 
+def add_names(named, out):
+    if out.shape[0] > SLOTS:
+        out[SLOTS:, :] = named[...]
+
+
 def one_row_tile(part, tile):
-    scores = ((part - tile) * UNIT).T
+    scores = (part - tile).T
     top = jnp.max(scores, axis=0, keepdims=True)
     return top + jnp.log2(jnp.sum(jnp.exp2(scores - top), axis=0, keepdims=True))
 
 
 def one_col_tile(part, tile):
     upright = jnp.broadcast_to(part, tile.shape).T
-    scores = (upright - tile) * UNIT
+    scores = upright - tile
     top = jnp.max(scores, axis=0, keepdims=True)
     return top + jnp.log2(jnp.sum(jnp.exp2(scores - top), axis=0, keepdims=True))
 
@@ -125,7 +128,7 @@
 def first_rows_kernel(
     rows_in, cols_in, cost_in, pot_in, count_in,
     out, cost, row_up, row_same, row_named, col_up, col_same, col_named,
-    rows, cols, pot, sems, cost_sems, scratch, values, picked,
+    landing, rows, cols, pot, sems, cost_sems, scratch, values, picked,
 ):
     count = count_in[0, 0]
     small = []
@@ -135,15 +138,16 @@
     chunks = []
     for k in range(cost.shape[0] // CHUNK):
         at = pl.ds(k * CHUNK, CHUNK)
-        chunks.append(pltpu.make_async_copy(cost_in.at[at], cost.at[at], cost_sems.at[k]))
+        chunks.append(pltpu.make_async_copy(cost_in.at[at], landing.at[at], cost_sems.at[k]))
         if k < AHEAD:
             pl.when(count > k * CHUNK)(chunks[k].start)
     values[...] = jnp.zeros(values.shape, jnp.float32)
     for copy in small:
         copy.wait()
     note_ids(cols, count, col_up, col_same, col_named, scratch)
-    picked[...] = gathered(pot[...], col_up)
+    picked[...] = gathered(UNIT * pot[...], col_up)
     note_ids(rows, count, row_up, row_same, row_named, scratch)
+    add_names(row_named, out)
     for k, chunk in enumerate(chunks):
 
         @pl.when(count > k * CHUNK)
@@ -152,25 +156,29 @@
             if k + AHEAD < len(chunks):
                 pl.when(count > (k + AHEAD) * CHUNK)(chunks[k + AHEAD].start)
             for s in range(k * CHUNK, (k + 1) * CHUNK):
-                values[pl.ds(s, 1), :] = one_row_tile(picked[pl.ds(s, 1), :], cost[s])
-
-    merged(values, row_up, row_same, row_named, out)
+                tile = UNIT * landing[s]
+                cost[s] = tile
+                values[pl.ds(s, 1), :] = one_row_tile(picked[pl.ds(s, 1), :], tile)
+
+    merged(values, row_up, row_same, out)
 
 
 def rows_kernel(mine, other, logmass, cost, row_up, row_same, row_named, col_up, out, values, picked):
+    add_names(row_named, out)
     pot = EPS * logmass[...] - BACK * pair_lse2(mine[...], other[...])
-    picked[...] = gathered(pot, col_up)
+    picked[...] = gathered(UNIT * pot, col_up)
     tiles(one_row_tile, cost, picked, values)
-    merged(values, row_up, row_same, row_named, out)
+    merged(values, row_up, row_same, out)
 
 
 def cols_kernel(
     one, two, three, four, logmass, cost, row_up, col_up, col_same, col_named, pot, out, values, picked
 ):
+    add_names(col_named, out)
     pot[...] = EPS * logmass[...] - BACK * ring_lse2([x[...] for x in (one, two, three, four)])
-    picked[...] = gathered(pot[...], row_up)
+    picked[...] = gathered(UNIT * pot[...], row_up)
     tiles(one_col_tile, cost, picked, values)
-    merged(values, col_up, col_same, col_named, out)
+    merged(values, col_up, col_same, out)
 
 
 def ring_lse2(parts):
@@ -262,6 +270,7 @@
                 [anywhere] * 4 + [pl.BlockSpec(memory_space=pltpu.SMEM)],
                 (sent, f32(*cost.shape), *ids, *ids),
                 (
+                    f32(*cost.shape),
                     pltpu.SMEM((slots,), jnp.int32),
                     pltpu.SMEM((slots,), jnp.int32),
                     full,

time: 80.9 us -> 80.5 us (level)
  starting transfers between devices: 21.6 us -> 20.4 us
    all_to_all x2, blocking collectives: 28.8 us -> 29.6 us  [to_all(): return lax.all_to_all(copies, axes, 0, 0, tiled=True)]
  transfers between devices with their start and end apart: 14 -> 14, of which waited for: 13 -> 14; matrix products, arithmetic and copies ran while one was open for 0% -> 0% of each run, Pallas kernels for 0% -> 0%
where the time goes in v6:
time: 80.5 us; the launch traced here: 80.3 us
  blocking collectives  29.6 us (37%)
  starting transfers between devices  20.4 us (25%)
  waiting for transfers between devices  17.9 us (22%)
  Pallas kernels  10.2 us (13%)
  between operations  1.42 us (2%)
    all_to_all x2, blocking collectives, to_all(): return lax.all_to_all(copies, axes, 0, 0, tiled=True)  29.6 us
    ppermute x12, waiting for transfers between devices, ring(): got[hop] = lax.ppermute(value, ('z', 'core', 'col'), pairs)  16.1 us
    ppermute x12, starting transfers between devices, ring(): got[hop] = lax.ppermute(value, ('z', 'core', 'col'), pairs)  10.8 us
    pallas_call x8, Pallas kernels, call(): pl.pallas_call(kernel, name=name, out_shape=outs[0] if single else outs,...  10.2 us
    ppermute x2, starting transfers between devices, local(): other = lax.ppermute(mine, 'core', swap)  9.61 us
    ppermute x2, waiting for transfers between devices, local(): other = lax.ppermute(mine, 'core', swap)  1.8 us
  transfers between devices with their start and end apart: 14, of which 14 were waited for; matrix products, arithmetic and copies ran while one was open for 0% of the time, Pallas kernels for 0%

profile of v6, /device:TPU:1, one launch (start us, length us, event | category | flops | bytes accessed | tf_op | source)
XLA Modules:
  0.0 80.3 jit_solution(838240482959914897)
XLA Ops:
  1.3 3.9 %first_rows.1 = (f32[72,128]{1,0:T(8,128)S(1)}, f32[64,128,128]{2,1,0:T(8,128)S(1)}, s32[64,128]{1,0:T(8,128)S(1)}, f32[64,128]{1,0:T(8,128)S(1)}, f32[8,128]{1,...) custom-call(s32[64]{0:T(128)} %bitcast.15, s32[64]{0:T(128)} %bitcast.16, ...), custom_call_target="tpu_custom_call" | custom-call | tf_op jit(solution)/shard_map/first_rows/pallas_call | solution.py:206
  5.3 2.3 %collective-permute-start.2 = (f32[72,128]{1,0:T(8,128)S(1)}, f32[72,128]{1,0:T(8,128)S(1)}, u32[]{:S(2)}, u32[]{:S(2)}) collective-permute-start(f32[72,128]{1,0:T(8,128)S(1)} %get-tuple-element.13.refs_0_.refs_4_), channel_id=1, source_target_pairs={{0,12},{1,13},{2,14},{3,15},{4,0},{5,1},{6,2},{7,3},{8,4},{9,5},{1... | collective-permute-start | bytes 110600 | tf_op jit(solution)/shard_map/ppermute | solution.py:229
  8.3 0.4 collective-permute-done.2.refs_3_.refs_7_
  8.7 3.3 %collective-permute-done.1.refs_2_.refs_6_ = f32[72,128]{1,0:T(8,128)S(1)} collective-permute-done((f32[72,128]{1,0:T(8,128)S(1)}, f32[72,128]{1,0:T(8,128)S(1)}, u32[]{:S(2)}, u32[]{:S(2)}) %collective-permute-start.1) | collective-permute-done | bytes 36896 | tf_op jit(solution)/shard_map/ppermute | solution.py:229
  11.9 0.4 collective-permute-done.refs_1_.refs_5_
  12.6 3.4 %collective-permute-start.5 = (f32[128,128]{1,0:T(8,128)S(1)}, f32[128,128]{1,0:T(8,128)S(1)}, u32[]{:S(2)}, u32[]{:S(2)}) collective-permute-start(f32[128,128]{1,0:T(8,128)S(1)} %ring.2.one), channel_id=1, source_target_pairs={{0,3},{1,0},{2,1},{3,2},{4,7},{5,4},{6,5},{7,6},{8,11},{9,8},{10,9... | collective-permute-start | bytes 196616 | tf_op jit(solution)/shard_map/ppermute | solution.py:229
  16.0 0.7 collective-permute-start.4
  16.7 0.6 collective-permute-done.5.four
  17.3 3.3 %collective-permute-done.4.three = f32[128,128]{1,0:T(8,128)S(1)} collective-permute-done((f32[128,128]{1,0:T(8,128)S(1)}, f32[128,128]{1,0:T(8,128)S(1)}, u32[]{:S(2)}, u32[]{:S(2)}) %collective-permute-start.4) | collective-permute-done | bytes 65568 | tf_op jit(solution)/shard_map/ppermute | solution.py:229
  20.6 0.7 collective-permute-done.3.two
  21.3 1.7 %cols_half.2 = (f32[128,128]{1,0:T(8,128)}, f32[72,128]{1,0:T(8,128)S(1)}) custom-call(f32[128,128]{1,0:T(8,128)S(1)} %ring.2.one, f32[128,128]{1,0:T(8,128)S(1)} %collective-permute-done.3.two, f32[128,128]{1,0:T(8,128)S(1)} %collective-permute-done.4.three, f32[128,128]{1,0:T(8,128)S(1)} %collective-permute-done.5.four, f32[128,128]{1,0:T(8,128)S(1)} %bitcast.10, ...), custom_call_target="tpu_custom_call" | custom-call | tf_op jit(solution)/shard_map/cols_half/pallas_call | solution.py:206
  23.0 17.9 %all_to_all.10.parts.names = f32[8,72,128]{2,1,0:T(8,128)S(1)} all-to-all(f32[8,72,128]{2,1,0:T(8,128)S(1)} %broadcast_in_dim.4), channel_id=1, replica_groups=mesh['z'=8,'core'=2,'col'=16] {'z'}, dimensions={0} | all-to-all | bytes 589824 | tf_op jit(solution)/shard_map/all_to_all | solution.py:235
  40.9 0.4 spread.2.mine
  41.3 5.4 %collective-permute-start.6 = (f32[128,128]{1,0:T(8,128)S(1)}, f32[128,128]{1,0:T(8,128)S(1)}, u32[]{:S(2)}, u32[]{:S(2)}) collective-permute-start(f32[128,128]{1,0:T(8,128)S(1)} %spread.2.mine), channel_id=1, source_target_pairs={{0,16},{16,0},{1,17},{17,1},{2,18},{18,2},{3,19},{19,3},{4,20},{20... | collective-permute-start | bytes 196616 | tf_op jit(solution)/shard_map/ppermute | solution.py:305
  46.7 0.9 %collective-permute-done.6.other = f32[128,128]{1,0:T(8,128)S(1)} collective-permute-done((f32[128,128]{1,0:T(8,128)S(1)}, f32[128,128]{1,0:T(8,128)S(1)}, u32[]{:S(2)}, u32[]{:S(2)}) %collective-permute-start.6) | collective-permute-done | bytes 65568 | tf_op jit(solution)/shard_map/ppermute | solution.py:305
  47.6 1.6 %rows_half.1.refs_0_ = f32[64,128]{1,0:T(8,128)S(1)} custom-call(f32[128,128]{1,0:T(8,128)S(1)} %spread.2.mine, f32[128,128]{1,0:T(8,128)S(1)} %collective-permute-done.6.other, f32[128,128]{1,0:T(8,128)S(1)} %bitcast.12, f32[64,128,128]{2,1,0:T(8,128)S(1)} %get-tuple-element.14.cost, s32[64,128]{1,0:T(8,128)S(1)} %get-tuple-element.15.row_up, ...), custom_call_target="tpu_custom_call" | custom-call | tf_op jit(solution)/shard_map/rows_half/pallas_call | solution.py:206
  49.2 0.4 collective-permute-start.9
  49.6 0.9 %collective-permute-start.8 = (f32[64,128]{1,0:T(8,128)S(1)}, f32[64,128]{1,0:T(8,128)S(1)}, u32[]{:S(2)}, u32[]{:S(2)}) collective-permute-start(f32[64,128]{1,0:T(8,128)S(1)} %rows_half.1.refs_0_), channel_id=1, source_target_pairs={{0,8},{1,9},{2,10},{3,11},{4,12},{5,13},{6,14},{7,15},{8,0},{9,1},... | collective-permute-start | bytes 98312 | tf_op jit(solution)/shard_map/ppermute | solution.py:229
  50.5 0.8 collective-permute-start.7
  51.2 0.9 %collective-permute-done.9.refs_3_ = f32[64,128]{1,0:T(8,128)S(1)} collective-permute-done((f32[64,128]{1,0:T(8,128)S(1)}, f32[64,128]{1,0:T(8,128)S(1)}, u32[]{:S(2)}, u32[]{:S(2)}) %collective-permute-start.9) | collective-permute-done | bytes 32800 | tf_op jit(solution)/shard_map/ppermute | solution.py:229
  52.1 1.8 %collective-permute-done.8.refs_2_ = f32[64,128]{1,0:T(8,128)S(1)} collective-permute-done((f32[64,128]{1,0:T(8,128)S(1)}, f32[64,128]{1,0:T(8,128)S(1)}, u32[]{:S(2)}, u32[]{:S(2)}) %collective-permute-start.8) | collective-permute-done | bytes 32800 | tf_op jit(solution)/shard_map/ppermute | solution.py:229
  53.9 0.9 %collective-permute-done.7.refs_1_ = f32[64,128]{1,0:T(8,128)S(1)} collective-permute-done((f32[64,128]{1,0:T(8,128)S(1)}, f32[64,128]{1,0:T(8,128)S(1)}, u32[]{:S(2)}, u32[]{:S(2)}) %collective-permute-start.7) | collective-permute-done | bytes 32800 | tf_op jit(solution)/shard_map/ppermute | solution.py:229
  55.1 0.8 %collective-permute-start.11 = (f32[128,128]{1,0:T(8,128)S(1)}, f32[128,128]{1,0:T(8,128)S(1)}, u32[]{:S(2)}, u32[]{:S(2)}) collective-permute-start(f32[128,128]{1,0:T(8,128)S(1)} %ring.3.one), channel_id=1, source_target_pairs={{0,2},{1,3},{2,0},{3,1},{4,6},{5,7},{6,4},{7,5},{8,10},{9,11},{10,... | collective-permute-start | bytes 196616 | tf_op jit(solution)/shard_map/ppermute | solution.py:229
  55.9 0.8 collective-permute-start.10
  56.7 1.5 %collective-permute-done.12.four = f32[128,128]{1,0:T(8,128)S(1)} collective-permute-done((f32[128,128]{1,0:T(8,128)S(1)}, f32[128,128]{1,0:T(8,128)S(1)}, u32[]{:S(2)}, u32[]{:S(2)}) %collective-permute-start.12) | collective-permute-done | bytes 65568 | tf_op jit(solution)/shard_map/ppermute | solution.py:229
  58.2 1.6 %collective-permute-done.11.three = f32[128,128]{1,0:T(8,128)S(1)} collective-permute-done((f32[128,128]{1,0:T(8,128)S(1)}, f32[128,128]{1,0:T(8,128)S(1)}, u32[]{:S(2)}, u32[]{:S(2)}) %collective-permute-start.11) | collective-permute-done | bytes 65568 | tf_op jit(solution)/shard_map/ppermute | solution.py:229
  59.8 0.8 collective-permute-done.10.two
  60.6 1.7 %cols_half.3 = (f32[128,128]{1,0:T(8,128)}, f32[64,128]{1,0:T(8,128)S(1)}) custom-call(f32[128,128]{1,0:T(8,128)S(1)} %ring.3.one, f32[128,128]{1,0:T(8,128)S(1)} %collective-permute-done.10.two, f32[128,128]{1,0:T(8,128)S(1)} %collective-permute-done.11.three, f32[128,128]{1,0:T(8,128)S(1)} %collective-permute-done.12.four, f32[128,128]{1,0:T(8,128)S(1)} %bitcast.11, ...), custom_call_target="tpu_custom_call" | custom-call | tf_op jit(solution)/shard_map/cols_half/pallas_call | solution.py:206
  62.3 11.8 %all_to_all.11.parts = f32[8,64,128]{2,1,0:T(8,128)S(1)} all-to-all(f32[8,64,128]{2,1,0:T(8,128)S(1)} %broadcast_in_dim.5), channel_id=1, replica_groups=mesh['z'=8,'core'=2,'col'=16] {'z'}, dimensions={0} | all-to-all | bytes 524288 | tf_op jit(solution)/shard_map/all_to_all | solution.py:235
  74.5 4.2 %collective-permute-start.13 = (f32[128,128]{1,0:T(8,128)S(1)}, f32[128,128]{1,0:T(8,128)S(1)}, u32[]{:S(2)}, u32[]{:S(2)}) collective-permute-start(f32[128,128]{1,0:T(8,128)S(1)} %spread.3), channel_id=1, source_target_pairs={{0,16},{16,0},{1,17},{17,1},{2,18},{18,2},{3,19},{19,3},{4,20},{20... | collective-permute-start | bytes 196616 | tf_op jit(solution)/shard_map/ppermute | solution.py:305
  78.7 0.9 %collective-permute-done.13 = f32[128,128]{1,0:T(8,128)S(1)} collective-permute-done((f32[128,128]{1,0:T(8,128)S(1)}, f32[128,128]{1,0:T(8,128)S(1)}, u32[]{:S(2)}, u32[]{:S(2)}) %collective-permute-start.13) | collective-permute-done | bytes 65568 | tf_op jit(solution)/shard_map/ppermute | solution.py:305
  79.6 0.7 subtract_bitcast_fusion
  (13 shorter events, 1.7 us)
Async XLA Ops:
  0.6 20.7 %copy-start = (f32[16384]{0:T(1024)S(1)}, f32[16384]{0:T(1024)}, u32[]{:S(2)}) copy-start(f32[16384]{0:T(1024)} %param.11) | copy-start | bytes 196612
  5.2 42.3 %copy-start.1 = (f32[16384]{0:T(1024)S(1)}, f32[16384]{0:T(1024)}, u32[]{:S(2)}) copy-start(f32[16384]{0:T(1024)} %param.12) | copy-start | bytes 196612
  5.3 3.4 %collective-permute-start.2 = (f32[72,128]{1,0:T(8,128)S(1)}, f32[72,128]{1,0:T(8,128)S(1)}, u32[]{:S(2)}, u32[]{:S(2)}) collective-permute-start(f32[72,128]{1,0:T(8,128)S(1)} %get-tuple-element.13.refs_0_.refs_4_), channel_id=1, source_target_pairs={{0,12},{1,13},{2,14},{3,15},{4,0},{5,1},{6,2},{7,3},{8,4},{9,5},{1... | collective-permute-start | bytes 110600 | tf_op jit(solution)/shard_map/ppermute | solution.py:229
  7.6 4.3 %collective-permute-start.1 = (f32[72,128]{1,0:T(8,128)S(1)}, f32[72,128]{1,0:T(8,128)S(1)}, u32[]{:S(2)}, u32[]{:S(2)}) collective-permute-start(f32[72,128]{1,0:T(8,128)S(1)} %get-tuple-element.13.refs_0_.refs_4_), channel_id=1, source_target_pairs={{0,8},{1,9},{2,10},{3,11},{4,12},{5,13},{6,14},{7,15},{8,0},{9,1},... | collective-permute-start | bytes 110600 | tf_op jit(solution)/shard_map/ppermute | solution.py:229
  7.9 4.4 %collective-permute-start = (f32[72,128]{1,0:T(8,128)S(1)}, f32[72,128]{1,0:T(8,128)S(1)}, u32[]{:S(2)}, u32[]{:S(2)}) collective-permute-start(f32[72,128]{1,0:T(8,128)S(1)} %get-tuple-element.13.refs_0_.refs_4_), channel_id=1, source_target_pairs={{0,4},{1,5},{2,6},{3,7},{4,8},{5,9},{6,10},{7,11},{8,12},{9,13},{1... | collective-permute-start | bytes 110600 | tf_op jit(solution)/shard_map/ppermute | solution.py:229
  12.6 4.7 %collective-permute-start.5 = (f32[128,128]{1,0:T(8,128)S(1)}, f32[128,128]{1,0:T(8,128)S(1)}, u32[]{:S(2)}, u32[]{:S(2)}) collective-permute-start(f32[128,128]{1,0:T(8,128)S(1)} %ring.2.one), channel_id=1, source_target_pairs={{0,3},{1,0},{2,1},{3,2},{4,7},{5,4},{6,5},{7,6},{8,11},{9,8},{10,9... | collective-permute-start | bytes 196616 | tf_op jit(solution)/shard_map/ppermute | solution.py:229
  16.0 4.6 %collective-permute-start.4 = (f32[128,128]{1,0:T(8,128)S(1)}, f32[128,128]{1,0:T(8,128)S(1)}, u32[]{:S(2)}, u32[]{:S(2)}) collective-permute-start(f32[128,128]{1,0:T(8,128)S(1)} %ring.2.one), channel_id=1, source_target_pairs={{0,2},{1,3},{2,0},{3,1},{4,6},{5,7},{6,4},{7,5},{8,10},{9,11},{10,... | collective-permute-start | bytes 196616 | tf_op jit(solution)/shard_map/ppermute | solution.py:229
  16.7 4.6 %collective-permute-start.3 = (f32[128,128]{1,0:T(8,128)S(1)}, f32[128,128]{1,0:T(8,128)S(1)}, u32[]{:S(2)}, u32[]{:S(2)}) collective-permute-start(f32[128,128]{1,0:T(8,128)S(1)} %ring.2.one), channel_id=1, source_target_pairs={{0,1},{1,2},{2,3},{3,0},{4,5},{5,6},{6,7},{7,4},{8,9},{9,10},{10,1... | collective-permute-start | bytes 196616 | tf_op jit(solution)/shard_map/ppermute | solution.py:229
  41.3 6.3 %collective-permute-start.6 = (f32[128,128]{1,0:T(8,128)S(1)}, f32[128,128]{1,0:T(8,128)S(1)}, u32[]{:S(2)}, u32[]{:S(2)}) collective-permute-start(f32[128,128]{1,0:T(8,128)S(1)} %spread.2.mine), channel_id=1, source_target_pairs={{0,16},{16,0},{1,17},{17,1},{2,18},{18,2},{3,19},{19,3},{4,20},{20... | collective-permute-start | bytes 196616 | tf_op jit(solution)/shard_map/ppermute | solution.py:305
  49.2 2.8 %collective-permute-start.9 = (f32[64,128]{1,0:T(8,128)S(1)}, f32[64,128]{1,0:T(8,128)S(1)}, u32[]{:S(2)}, u32[]{:S(2)}) collective-permute-start(f32[64,128]{1,0:T(8,128)S(1)} %rows_half.1.refs_0_), channel_id=1, source_target_pairs={{0,12},{1,13},{2,14},{3,15},{4,0},{5,1},{6,2},{7,3},{8,4},{9,5},{1... | collective-permute-start | bytes 98312 | tf_op jit(solution)/shard_map/ppermute | solution.py:229
  49.6 4.3 %collective-permute-start.8 = (f32[64,128]{1,0:T(8,128)S(1)}, f32[64,128]{1,0:T(8,128)S(1)}, u32[]{:S(2)}, u32[]{:S(2)}) collective-permute-start(f32[64,128]{1,0:T(8,128)S(1)} %rows_half.1.refs_0_), channel_id=1, source_target_pairs={{0,8},{1,9},{2,10},{3,11},{4,12},{5,13},{6,14},{7,15},{8,0},{9,1},... | collective-permute-start | bytes 98312 | tf_op jit(solution)/shard_map/ppermute | solution.py:229
  50.5 4.3 %collective-permute-start.7 = (f32[64,128]{1,0:T(8,128)S(1)}, f32[64,128]{1,0:T(8,128)S(1)}, u32[]{:S(2)}, u32[]{:S(2)}) collective-permute-start(f32[64,128]{1,0:T(8,128)S(1)} %rows_half.1.refs_0_), channel_id=1, source_target_pairs={{0,4},{1,5},{2,6},{3,7},{4,8},{5,9},{6,10},{7,11},{8,12},{9,13},{1... | collective-permute-start | bytes 98312 | tf_op jit(solution)/shard_map/ppermute | solution.py:229
  55.0 3.2 %collective-permute-start.12 = (f32[128,128]{1,0:T(8,128)S(1)}, f32[128,128]{1,0:T(8,128)S(1)}, u32[]{:S(2)}, u32[]{:S(2)}) collective-permute-start(f32[128,128]{1,0:T(8,128)S(1)} %ring.3.one), channel_id=1, source_target_pairs={{0,3},{1,0},{2,1},{3,2},{4,7},{5,4},{6,5},{7,6},{8,11},{9,8},{10,9... | collective-permute-start | bytes 196616 | tf_op jit(solution)/shard_map/ppermute | solution.py:229
  55.1 4.7 %collective-permute-start.11 = (f32[128,128]{1,0:T(8,128)S(1)}, f32[128,128]{1,0:T(8,128)S(1)}, u32[]{:S(2)}, u32[]{:S(2)}) collective-permute-start(f32[128,128]{1,0:T(8,128)S(1)} %ring.3.one), channel_id=1, source_target_pairs={{0,2},{1,3},{2,0},{3,1},{4,6},{5,7},{6,4},{7,5},{8,10},{9,11},{10,... | collective-permute-start | bytes 196616 | tf_op jit(solution)/shard_map/ppermute | solution.py:229
  55.9 4.7 %collective-permute-start.10 = (f32[128,128]{1,0:T(8,128)S(1)}, f32[128,128]{1,0:T(8,128)S(1)}, u32[]{:S(2)}, u32[]{:S(2)}) collective-permute-start(f32[128,128]{1,0:T(8,128)S(1)} %ring.3.one), channel_id=1, source_target_pairs={{0,1},{1,2},{2,3},{3,0},{4,5},{5,6},{6,7},{7,4},{8,9},{9,10},{10,1... | collective-permute-start | bytes 196616 | tf_op jit(solution)/shard_map/ppermute | solution.py:229
  74.5 5.1 %collective-permute-start.13 = (f32[128,128]{1,0:T(8,128)S(1)}, f32[128,128]{1,0:T(8,128)S(1)}, u32[]{:S(2)}, u32[]{:S(2)}) collective-permute-start(f32[128,128]{1,0:T(8,128)S(1)} %spread.3), channel_id=1, source_target_pairs={{0,16},{16,0},{1,17},{17,1},{2,18},{18,2},{3,19},{19,3},{4,20},{20... | collective-permute-start | bytes 196616 | tf_op jit(solution)/shard_map/ppermute | solution.py:305

commit v7 on v6

--- a/solution.py
+++ b/solution.py
@@ -214,20 +214,47 @@
     )(*operands)
 
 
-def ring(value, nz, stage):
-    got = {0: value}
-    for hop in (2, 1, 3):
+def exchange(value, nz, routes):
+    got = [value]
+    for route in routes:
         pairs = []
         for z in range(nz):
             for core in range(2):
                 for x in range(RING):
                     for y in range(RING):
-                        along_x = core == stage
-                        to = ((x + hop) % RING, y) if along_x else (x, (y + hop) % RING)
-                        row = (z * 2 + core) * RING
-                        pairs.append(((row + x) * RING + y, (row + to[0]) * RING + to[1]))
-        got[hop] = lax.ppermute(value, ("z", "core", "col"), pairs)
-    return [got[hop] for hop in range(RING)]
+                        to = route(z, core, x, y)
+                        here = ((z * 2 + core) * RING + x) * RING + y
+                        pairs.append((here, ((to[0] * 2 + to[1]) * RING + to[2]) * RING + to[3]))
+        got.append(lax.ppermute(value, ("z", "core", "col"), pairs))
+    return got
+
+
+def ring_routes(stage):
+    def route(hop):
+        def to(z, core, x, y):
+            if core == stage:
+                return z, core, (x + hop) % RING, y
+            return z, core, x, (y + hop) % RING
+
+        return to
+
+    return [route(hop) for hop in (1, 2, 3)]
+
+
+def pair_routes():
+    return [
+        lambda z, core, x, y: (z ^ 1, core, x, y),
+        lambda z, core, x, y: (z, 1 - core, x, y),
+        lambda z, core, x, y: (z ^ 1, 1 - core, x, y),
+    ]
+
+
+def line_routes(nz):
+    return [
+        lambda z, core, x, y: ((z + 2) % nz, core, x, y),
+        lambda z, core, x, y: (((z // 2 + nz // 4) * 2 + 1 - z % 2) % nz, core, x, y),
+        lambda z, core, x, y: ((z - 2) % nz, core, x, y),
+    ]
 
 
 def to_all(value, axes, peers):
@@ -245,7 +272,6 @@
     srcmass = source_logmass.reshape(-1, LANES)
     tgtmass = target_logmass.reshape(-1, LANES)
     nz = lax.axis_size("z")
-    swap = [(0, 1), (1, 0)]
     slots = cost.shape[0]
 
     def f32(*shape):
@@ -260,7 +286,7 @@
     full, named, values = f32(LANES, LANES), f32(8, LANES), f32(slots, LANES)
     ids = (pltpu.VMEM((slots, LANES), jnp.int32), values, named)
     anywhere = pl.BlockSpec(memory_space=pl.ANY)
-    col_names = row_names = None
+    col_names = None
     for step in range(ITERS):
         sent = f32(slots + 8, LANES) if step == 0 else f32(slots, LANES)
         if step == 0:
@@ -288,22 +314,22 @@
                 (mine, other, tgtmass, tiles_held, row_up, row_same, row_named, col_up),
                 None, (sent,), (values, values),
             )
-        parts = ring(listed, nz, 0)
+        parts = exchange(listed, nz, ring_routes(0))
         col_names = parts if step == 0 else col_names
         part = call(ring_kernel, "ring", (*parts, *col_names), None, (full,), ())
         source, listed = call(
             cols_kernel, "cols_half",
-            (*ring(part, nz, 1), srcmass, tiles_held, row_up, col_up, col_same, col_named),
-            None, (jax.ShapeDtypeStruct((LANES, LANES), jnp.float32), sent),
+            (*exchange(part, nz, ring_routes(1)), srcmass, tiles_held, row_up, col_up, col_same, col_named),
+            None, (jax.ShapeDtypeStruct((LANES, LANES), jnp.float32), f32(slots + 8, LANES)),
             (values, values),
         )
-        parts = to_all(listed, "z", nz).reshape(nz, -1, LANES)
-        row_names = parts if step == 0 else row_names
-        mine = call(
-            spread_kernel, "spread", (parts, row_names), None, (full,), (f32(nz, LANES, LANES),)
-        )
-        other = lax.ppermute(mine, "core", swap)
-    target = EPS * tgtmass - BACK * pair_lse2(mine, other)
+        if step < ITERS - 1:
+            parts = to_all(listed, "z", nz).reshape(nz, -1, LANES)
+            mine = call(spread_kernel, "spread", (parts, parts), None, (full,), (f32(nz, LANES, LANES),))
+            other = lax.ppermute(mine, "core", [(0, 1), (1, 0)])
+    parts = exchange(listed, nz, pair_routes())
+    part = call(ring_kernel, "pair", (*parts, *parts), None, (full,), ())
+    target = EPS * tgtmass - BACK * ring_lse2(exchange(part, nz, line_routes(nz)))
     return (source.reshape(-1), target.reshape(-1))
 
 

time: 80.5 us -> 79.6 us (0.989); the launches traced: 80.3 us -> 78 us
  blocking collectives: 29.6 us -> 17.8 us
  starting transfers between devices: 20.4 us -> 25.6 us
  waiting for transfers between devices: 17.9 us -> 22.8 us
    all_to_all x2 -> x1, blocking collectives: 29.6 us -> 17.8 us  [to_all(): return lax.all_to_all(copies, axes, 0, 0, tiled=True)]
    ppermute x14 -> x19, starting transfers between devices: 20.4 us -> 25.6 us  [the longest x18 20.5 us: exchange(): got.append(lax.ppermute(value, ('z', 'core', 'col'), pairs))]
    ppermute x14 -> x19, waiting for transfers between devices: 17.9 us -> 22.8 us  [the longest x18 21.9 us: exchange(): got.append(lax.ppermute(value, ('z', 'core', 'col'), pairs))]
  transfers between devices with their start and end apart: 14 -> 19, of which waited for: 14 -> 17; matrix products, arithmetic and copies ran while one was open for 0% -> 0% of each run, Pallas kernels for 0% -> 0%
where the time goes in v7:
time: 79.6 us; the launch traced here: 78 us
  starting transfers between devices  25.6 us (32%)
  waiting for transfers between devices  22.8 us (29%)
  blocking collectives  17.8 us (22%)
  Pallas kernels  9.65 us (12%)
  between operations  1.41 us (2%)
    ppermute x18, waiting for transfers between devices, exchange(): got.append(lax.ppermute(value, ('z', 'core', 'col'), pairs))  21.9 us
    ppermute x18, starting transfers between devices, exchange(): got.append(lax.ppermute(value, ('z', 'core', 'col'), pairs))  20.5 us
    all_to_all x1, blocking collectives, to_all(): return lax.all_to_all(copies, axes, 0, 0, tiled=True)  17.8 us
    pallas_call x8, Pallas kernels, call(): pl.pallas_call(kernel, name=name, out_shape=outs[0] if single else outs,...  9.65 us
    ppermute x1, starting transfers between devices, local(): other = lax.ppermute(mine, 'core', [(0, 1), (1, 0)])  5.03 us
  transfers between devices with their start and end apart: 19, of which 17 were waited for; matrix products, arithmetic and copies ran while one was open for 0% of the time, Pallas kernels for 0%

profile of v7, /device:TPU:1, one launch (start us, length us, event | category | flops | bytes accessed | tf_op | source)
XLA Modules:
  0.0 78.0 jit_solution(17494669224431060202)
XLA Ops:
  1.3 3.5 %first_rows.1 = (f32[72,128]{1,0:T(8,128)S(1)}, f32[64,128,128]{2,1,0:T(8,128)S(1)}, s32[64,128]{1,0:T(8,128)S(1)}, f32[64,128]{1,0:T(8,128)S(1)}, f32[8,128]{1,...) custom-call(s32[64]{0:T(128)} %bitcast.15, s32[64]{0:T(128)} %bitcast.16, ...), custom_call_target="tpu_custom_call" | custom-call | tf_op jit(solution)/shard_map/first_rows/pallas_call | solution.py:206
  4.8 3.6 %collective-permute-start.2 = (f32[72,128]{1,0:T(8,128)S(1)}, f32[72,128]{1,0:T(8,128)S(1)}, u32[]{:S(2)}, u32[]{:S(2)}) collective-permute-start(f32[72,128]{1,0:T(8,128)S(1)} %get-tuple-element.13.refs_0_.refs_4_), channel_id=1, source_target_pairs={{0,12},{1,13},{2,14},{3,15},{4,0},{5,1},{6,2},{7,3},{8,4},{9,5},{1... | collective-permute-start | bytes 110600 | tf_op jit(solution)/shard_map/ppermute | solution.py:228
  9.5 3.5 %collective-permute-done.1.refs_2_.refs_6_ = f32[72,128]{1,0:T(8,128)S(1)} collective-permute-done((f32[72,128]{1,0:T(8,128)S(1)}, f32[72,128]{1,0:T(8,128)S(1)}, u32[]{:S(2)}, u32[]{:S(2)}) %collective-permute-start.1) | collective-permute-done | bytes 36896 | tf_op jit(solution)/shard_map/ppermute | solution.py:228
  13.4 1.7 %collective-permute-start.5 = (f32[128,128]{1,0:T(8,128)S(1)}, f32[128,128]{1,0:T(8,128)S(1)}, u32[]{:S(2)}, u32[]{:S(2)}) collective-permute-start(f32[128,128]{1,0:T(8,128)S(1)} %ring.2.one), channel_id=1, source_target_pairs={{0,3},{1,0},{2,1},{3,2},{4,7},{5,4},{6,5},{7,6},{8,11},{9,8},{10,9... | collective-permute-start | bytes 196616 | tf_op jit(solution)/shard_map/ppermute | solution.py:228
  15.1 0.9 %collective-permute-start.4 = (f32[128,128]{1,0:T(8,128)S(1)}, f32[128,128]{1,0:T(8,128)S(1)}, u32[]{:S(2)}, u32[]{:S(2)}) collective-permute-start(f32[128,128]{1,0:T(8,128)S(1)} %ring.2.one), channel_id=1, source_target_pairs={{0,2},{1,3},{2,0},{3,1},{4,6},{5,7},{6,4},{7,5},{8,10},{9,11},{10,... | collective-permute-start | bytes 196616 | tf_op jit(solution)/shard_map/ppermute | solution.py:228
  16.0 0.8 collective-permute-start.3
  16.8 3.0 %collective-permute-done.4.three = f32[128,128]{1,0:T(8,128)S(1)} collective-permute-done((f32[128,128]{1,0:T(8,128)S(1)}, f32[128,128]{1,0:T(8,128)S(1)}, u32[]{:S(2)}, u32[]{:S(2)}) %collective-permute-start.4) | collective-permute-done | bytes 65568 | tf_op jit(solution)/shard_map/ppermute | solution.py:228
  19.7 0.7 collective-permute-done.3.two
  20.4 1.7 %cols_half.2 = (f32[128,128]{1,0:T(8,128)}, f32[72,128]{1,0:T(8,128)S(1)}) custom-call(f32[128,128]{1,0:T(8,128)S(1)} %ring.2.one, f32[128,128]{1,0:T(8,128)S(1)} %collective-permute-done.3.two, f32[128,128]{1,0:T(8,128)S(1)} %collective-permute-done.4.three, f32[128,128]{1,0:T(8,128)S(1)} %collective-permute-done.5.four, f32[128,128]{1,0:T(8,128)S(1)} %bitcast.10, ...), custom_call_target="tpu_custom_call" | custom-call | tf_op jit(solution)/shard_map/cols_half/pallas_call | solution.py:206
  22.2 17.8 %all_to_all.5.parts.names = f32[8,72,128]{2,1,0:T(8,128)S(1)} all-to-all(f32[8,72,128]{2,1,0:T(8,128)S(1)} %broadcast_in_dim.2), channel_id=1, replica_groups=mesh['z'=8,'core'=2,'col'=16] {'z'}, dimensions={0} | all-to-all | bytes 589824 | tf_op jit(solution)/shard_map/all_to_all | solution.py:262
  40.3 5.0 %collective-permute-start.6 = (f32[128,128]{1,0:T(8,128)S(1)}, f32[128,128]{1,0:T(8,128)S(1)}, u32[]{:S(2)}, u32[]{:S(2)}) collective-permute-start(f32[128,128]{1,0:T(8,128)S(1)} %spread.1.mine), channel_id=1, source_target_pairs={{0,16},{16,0},{1,17},{17,1},{2,18},{18,2},{3,19},{19,3},{4,20},{20... | collective-permute-start | bytes 196616 | tf_op jit(solution)/shard_map/ppermute | solution.py:329
  45.4 0.9 %collective-permute-done.6.other = f32[128,128]{1,0:T(8,128)S(1)} collective-permute-done((f32[128,128]{1,0:T(8,128)S(1)}, f32[128,128]{1,0:T(8,128)S(1)}, u32[]{:S(2)}, u32[]{:S(2)}) %collective-permute-start.6) | collective-permute-done | bytes 65568 | tf_op jit(solution)/shard_map/ppermute | solution.py:329
  46.3 1.6 %rows_half.1.refs_0_ = f32[64,128]{1,0:T(8,128)S(1)} custom-call(f32[128,128]{1,0:T(8,128)S(1)} %spread.1.mine, f32[128,128]{1,0:T(8,128)S(1)} %collective-permute-done.6.other, f32[128,128]{1,0:T(8,128)S(1)} %bitcast.12, f32[64,128,128]{2,1,0:T(8,128)S(1)} %get-tuple-element.14.cost, s32[64,128]{1,0:T(8,128)S(1)} %get-tuple-element.15.row_up, ...), custom_call_target="tpu_custom_call" | custom-call | tf_op jit(solution)/shard_map/rows_half/pallas_call | solution.py:206
  48.3 1.1 %collective-permute-start.8 = (f32[64,128]{1,0:T(8,128)S(1)}, f32[64,128]{1,0:T(8,128)S(1)}, u32[]{:S(2)}, u32[]{:S(2)}) collective-permute-start(f32[64,128]{1,0:T(8,128)S(1)} %rows_half.1.refs_0_), channel_id=1, source_target_pairs={{0,8},{1,9},{2,10},{3,11},{4,12},{5,13},{6,14},{7,15},{8,0},{9,1},... | collective-permute-start | bytes 98312 | tf_op jit(solution)/shard_map/ppermute | solution.py:228
  49.9 0.9 %collective-permute-done.9.refs_3_ = f32[64,128]{1,0:T(8,128)S(1)} collective-permute-done((f32[64,128]{1,0:T(8,128)S(1)}, f32[64,128]{1,0:T(8,128)S(1)}, u32[]{:S(2)}, u32[]{:S(2)}) %collective-permute-start.9) | collective-permute-done | bytes 32800 | tf_op jit(solution)/shard_map/ppermute | solution.py:228
  50.8 1.8 %collective-permute-done.8.refs_2_ = f32[64,128]{1,0:T(8,128)S(1)} collective-permute-done((f32[64,128]{1,0:T(8,128)S(1)}, f32[64,128]{1,0:T(8,128)S(1)}, u32[]{:S(2)}, u32[]{:S(2)}) %collective-permute-start.8) | collective-permute-done | bytes 32800 | tf_op jit(solution)/shard_map/ppermute | solution.py:228
  52.6 0.8 %collective-permute-done.7.refs_1_ = f32[64,128]{1,0:T(8,128)S(1)} collective-permute-done((f32[64,128]{1,0:T(8,128)S(1)}, f32[64,128]{1,0:T(8,128)S(1)}, u32[]{:S(2)}, u32[]{:S(2)}) %collective-permute-start.7) | collective-permute-done | bytes 32800 | tf_op jit(solution)/shard_map/ppermute | solution.py:228
  54.3 1.2 %collective-permute-start.11 = (f32[128,128]{1,0:T(8,128)S(1)}, f32[128,128]{1,0:T(8,128)S(1)}, u32[]{:S(2)}, u32[]{:S(2)}) collective-permute-start(f32[128,128]{1,0:T(8,128)S(1)} %ring.3.one), channel_id=1, source_target_pairs={{0,2},{1,3},{2,0},{3,1},{4,6},{5,7},{6,4},{7,5},{8,10},{9,11},{10,... | collective-permute-start | bytes 196616 | tf_op jit(solution)/shard_map/ppermute | solution.py:228
  55.4 0.8 collective-permute-start.10
  56.8 2.1 %collective-permute-done.11.three = f32[128,128]{1,0:T(8,128)S(1)} collective-permute-done((f32[128,128]{1,0:T(8,128)S(1)}, f32[128,128]{1,0:T(8,128)S(1)}, u32[]{:S(2)}, u32[]{:S(2)}) %collective-permute-start.11) | collective-permute-done | bytes 65568 | tf_op jit(solution)/shard_map/ppermute | solution.py:228
  58.9 0.9 %collective-permute-done.10.two = f32[128,128]{1,0:T(8,128)S(1)} collective-permute-done((f32[128,128]{1,0:T(8,128)S(1)}, f32[128,128]{1,0:T(8,128)S(1)}, u32[]{:S(2)}, u32[]{:S(2)}) %collective-permute-start.10) | collective-permute-done | bytes 65568 | tf_op jit(solution)/shard_map/ppermute | solution.py:228
  59.7 1.7 %cols_half.3 = (f32[128,128]{1,0:T(8,128)}, f32[72,128]{1,0:T(8,128)S(1)}) custom-call(f32[128,128]{1,0:T(8,128)S(1)} %ring.3.one, f32[128,128]{1,0:T(8,128)S(1)} %collective-permute-done.10.two, f32[128,128]{1,0:T(8,128)S(1)} %collective-permute-done.11.three, f32[128,128]{1,0:T(8,128)S(1)} %collective-permute-done.12.four, f32[128,128]{1,0:T(8,128)S(1)} %bitcast.11, ...), custom_call_target="tpu_custom_call" | custom-call | tf_op jit(solution)/shard_map/cols_half/pallas_call | solution.py:206
  61.5 3.8 %collective-permute-start.15 = (f32[72,128]{1,0:T(8,128)S(1)}, f32[72,128]{1,0:T(8,128)S(1)}, u32[]{:S(2)}, u32[]{:S(2)}) collective-permute-start(f32[72,128]{1,0:T(8,128)S(1)} %get-tuple-element.23.refs_0_.refs_4_), channel_id=1, source_target_pairs={{0,48},{1,49},{2,50},{3,51},{4,52},{5,53},{6,54},{7,55},{8,56},{9,... | collective-permute-start | bytes 110600 | tf_op jit(solution)/shard_map/ppermute | solution.py:228
  65.3 1.2 %collective-permute-start.13 = (f32[72,128]{1,0:T(8,128)S(1)}, f32[72,128]{1,0:T(8,128)S(1)}, u32[]{:S(2)}, u32[]{:S(2)}) collective-permute-start(f32[72,128]{1,0:T(8,128)S(1)} %get-tuple-element.23.refs_0_.refs_4_), channel_id=1, source_target_pairs={{0,32},{1,33},{2,34},{3,35},{4,36},{5,37},{6,38},{7,39},{8,40},{9,... | collective-permute-start | bytes 110600 | tf_op jit(solution)/shard_map/ppermute | solution.py:228
  66.9 1.3 %collective-permute-done.13.refs_1_.refs_5_ = f32[72,128]{1,0:T(8,128)S(1)} collective-permute-done((f32[72,128]{1,0:T(8,128)S(1)}, f32[72,128]{1,0:T(8,128)S(1)}, u32[]{:S(2)}, u32[]{:S(2)}) %collective-permute-start.13) | collective-permute-done | bytes 36896 | tf_op jit(solution)/shard_map/ppermute | solution.py:228
  68.5 0.9 %collective-permute-start.18 = (f32[128,128]{1,0:T(8,128)S(1)}, f32[128,128]{1,0:T(8,128)S(1)}, u32[]{:S(2)}, u32[]{:S(2)}) collective-permute-start(f32[128,128]{1,0:T(8,128)S(1)} %pair.1), channel_id=1, source_target_pairs={{0,192},{1,193},{2,194},{3,195},{4,196},{5,197},{6,198},{7,199},{8... | collective-permute-start | bytes 196616 | tf_op jit(solution)/shard_map/ppermute | solution.py:228
  69.4 1.5 %collective-permute-start.17 = (f32[128,128]{1,0:T(8,128)S(1)}, f32[128,128]{1,0:T(8,128)S(1)}, u32[]{:S(2)}, u32[]{:S(2)}) collective-permute-start(f32[128,128]{1,0:T(8,128)S(1)} %pair.1), channel_id=1, source_target_pairs={{0,64},{1,65},{2,66},{3,67},{4,68},{5,69},{6,70},{7,71},{8,72},{9,... | collective-permute-start | bytes 196616 | tf_op jit(solution)/shard_map/ppermute | solution.py:228
  70.9 0.9 %collective-permute-start.16 = (f32[128,128]{1,0:T(8,128)S(1)}, f32[128,128]{1,0:T(8,128)S(1)}, u32[]{:S(2)}, u32[]{:S(2)}) collective-permute-start(f32[128,128]{1,0:T(8,128)S(1)} %pair.1), channel_id=1, source_target_pairs={{0,160},{1,161},{2,162},{3,163},{4,164},{5,165},{6,166},{7,167},{8... | collective-permute-start | bytes 196616 | tf_op jit(solution)/shard_map/ppermute | solution.py:228
  71.8 0.8 %collective-permute-done.18 = f32[128,128]{1,0:T(8,128)S(1)} collective-permute-done((f32[128,128]{1,0:T(8,128)S(1)}, f32[128,128]{1,0:T(8,128)S(1)}, u32[]{:S(2)}, u32[]{:S(2)}) %collective-permute-start.18) | collective-permute-done | bytes 65568 | tf_op jit(solution)/shard_map/ppermute | solution.py:228
  72.6 2.3 %collective-permute-done.17 = f32[128,128]{1,0:T(8,128)S(1)} collective-permute-done((f32[128,128]{1,0:T(8,128)S(1)}, f32[128,128]{1,0:T(8,128)S(1)}, u32[]{:S(2)}, u32[]{:S(2)}) %collective-permute-start.17) | collective-permute-done | bytes 65568 | tf_op jit(solution)/shard_map/ppermute | solution.py:228
  74.9 2.4 %collective-permute-done.16 = f32[128,128]{1,0:T(8,128)S(1)} collective-permute-done((f32[128,128]{1,0:T(8,128)S(1)}, f32[128,128]{1,0:T(8,128)S(1)}, u32[]{:S(2)}, u32[]{:S(2)}) %collective-permute-start.16) | collective-permute-done | bytes 65568 | tf_op jit(solution)/shard_map/ppermute | solution.py:228
  77.3 0.7 subtract_bitcast_fusion
  (21 shorter events, 4.9 us)
Async XLA Ops:
  0.6 19.8 %copy-start = (f32[16384]{0:T(1024)S(1)}, f32[16384]{0:T(1024)}, u32[]{:S(2)}) copy-start(f32[16384]{0:T(1024)} %param.11) | copy-start | bytes 196612
  4.8 41.5 %copy-start.1 = (f32[16384]{0:T(1024)S(1)}, f32[16384]{0:T(1024)}, u32[]{:S(2)}) copy-start(f32[16384]{0:T(1024)} %param.12) | copy-start | bytes 196612
  4.8 4.7 %collective-permute-start.2 = (f32[72,128]{1,0:T(8,128)S(1)}, f32[72,128]{1,0:T(8,128)S(1)}, u32[]{:S(2)}, u32[]{:S(2)}) collective-permute-start(f32[72,128]{1,0:T(8,128)S(1)} %get-tuple-element.13.refs_0_.refs_4_), channel_id=1, source_target_pairs={{0,12},{1,13},{2,14},{3,15},{4,0},{5,1},{6,2},{7,3},{8,4},{9,5},{1... | collective-permute-start | bytes 110600 | tf_op jit(solution)/shard_map/ppermute | solution.py:228
  8.5 4.6 %collective-permute-start.1 = (f32[72,128]{1,0:T(8,128)S(1)}, f32[72,128]{1,0:T(8,128)S(1)}, u32[]{:S(2)}, u32[]{:S(2)}) collective-permute-start(f32[72,128]{1,0:T(8,128)S(1)} %get-tuple-element.13.refs_0_.refs_4_), channel_id=1, source_target_pairs={{0,8},{1,9},{2,10},{3,11},{4,12},{5,13},{6,14},{7,15},{8,0},{9,1},... | collective-permute-start | bytes 110600 | tf_op jit(solution)/shard_map/ppermute | solution.py:228
  8.5 4.7 %collective-permute-start = (f32[72,128]{1,0:T(8,128)S(1)}, f32[72,128]{1,0:T(8,128)S(1)}, u32[]{:S(2)}, u32[]{:S(2)}) collective-permute-start(f32[72,128]{1,0:T(8,128)S(1)} %get-tuple-element.13.refs_0_.refs_4_), channel_id=1, source_target_pairs={{0,4},{1,5},{2,6},{3,7},{4,8},{5,9},{6,10},{7,11},{8,12},{9,13},{1... | collective-permute-start | bytes 110600 | tf_op jit(solution)/shard_map/ppermute | solution.py:228
  13.4 3.3 %collective-permute-start.5 = (f32[128,128]{1,0:T(8,128)S(1)}, f32[128,128]{1,0:T(8,128)S(1)}, u32[]{:S(2)}, u32[]{:S(2)}) collective-permute-start(f32[128,128]{1,0:T(8,128)S(1)} %ring.2.one), channel_id=1, source_target_pairs={{0,3},{1,0},{2,1},{3,2},{4,7},{5,4},{6,5},{7,6},{8,11},{9,8},{10,9... | collective-permute-start | bytes 196616 | tf_op jit(solution)/shard_map/ppermute | solution.py:228
  15.1 4.6 %collective-permute-start.4 = (f32[128,128]{1,0:T(8,128)S(1)}, f32[128,128]{1,0:T(8,128)S(1)}, u32[]{:S(2)}, u32[]{:S(2)}) collective-permute-start(f32[128,128]{1,0:T(8,128)S(1)} %ring.2.one), channel_id=1, source_target_pairs={{0,2},{1,3},{2,0},{3,1},{4,6},{5,7},{6,4},{7,5},{8,10},{9,11},{10,... | collective-permute-start | bytes 196616 | tf_op jit(solution)/shard_map/ppermute | solution.py:228
  16.0 4.4 %collective-permute-start.3 = (f32[128,128]{1,0:T(8,128)S(1)}, f32[128,128]{1,0:T(8,128)S(1)}, u32[]{:S(2)}, u32[]{:S(2)}) collective-permute-start(f32[128,128]{1,0:T(8,128)S(1)} %ring.2.one), channel_id=1, source_target_pairs={{0,1},{1,2},{2,3},{3,0},{4,5},{5,6},{6,7},{7,4},{8,9},{9,10},{10,1... | collective-permute-start | bytes 196616 | tf_op jit(solution)/shard_map/ppermute | solution.py:228
  40.3 5.9 %collective-permute-start.6 = (f32[128,128]{1,0:T(8,128)S(1)}, f32[128,128]{1,0:T(8,128)S(1)}, u32[]{:S(2)}, u32[]{:S(2)}) collective-permute-start(f32[128,128]{1,0:T(8,128)S(1)} %spread.1.mine), channel_id=1, source_target_pairs={{0,16},{16,0},{1,17},{17,1},{2,18},{18,2},{3,19},{19,3},{4,20},{20... | collective-permute-start | bytes 196616 | tf_op jit(solution)/shard_map/ppermute | solution.py:329
  47.9 2.8 %collective-permute-start.9 = (f32[64,128]{1,0:T(8,128)S(1)}, f32[64,128]{1,0:T(8,128)S(1)}, u32[]{:S(2)}, u32[]{:S(2)}) collective-permute-start(f32[64,128]{1,0:T(8,128)S(1)} %rows_half.1.refs_0_), channel_id=1, source_target_pairs={{0,12},{1,13},{2,14},{3,15},{4,0},{5,1},{6,2},{7,3},{8,4},{9,5},{1... | collective-permute-start | bytes 98312 | tf_op jit(solution)/shard_map/ppermute | solution.py:228
  48.3 4.3 %collective-permute-start.8 = (f32[64,128]{1,0:T(8,128)S(1)}, f32[64,128]{1,0:T(8,128)S(1)}, u32[]{:S(2)}, u32[]{:S(2)}) collective-permute-start(f32[64,128]{1,0:T(8,128)S(1)} %rows_half.1.refs_0_), channel_id=1, source_target_pairs={{0,8},{1,9},{2,10},{3,11},{4,12},{5,13},{6,14},{7,15},{8,0},{9,1},... | collective-permute-start | bytes 98312 | tf_op jit(solution)/shard_map/ppermute | solution.py:228
  49.4 4.0 %collective-permute-start.7 = (f32[64,128]{1,0:T(8,128)S(1)}, f32[64,128]{1,0:T(8,128)S(1)}, u32[]{:S(2)}, u32[]{:S(2)}) collective-permute-start(f32[64,128]{1,0:T(8,128)S(1)} %rows_half.1.refs_0_), channel_id=1, source_target_pairs={{0,4},{1,5},{2,6},{3,7},{4,8},{5,9},{6,10},{7,11},{8,12},{9,13},{1... | collective-permute-start | bytes 98312 | tf_op jit(solution)/shard_map/ppermute | solution.py:228
  53.6 3.2 %collective-permute-start.12 = (f32[128,128]{1,0:T(8,128)S(1)}, f32[128,128]{1,0:T(8,128)S(1)}, u32[]{:S(2)}, u32[]{:S(2)}) collective-permute-start(f32[128,128]{1,0:T(8,128)S(1)} %ring.3.one), channel_id=1, source_target_pairs={{0,3},{1,0},{2,1},{3,2},{4,7},{5,4},{6,5},{7,6},{8,11},{9,8},{10,9... | collective-permute-start | bytes 196616 | tf_op jit(solution)/shard_map/ppermute | solution.py:228
  54.3 4.6 %collective-permute-start.11 = (f32[128,128]{1,0:T(8,128)S(1)}, f32[128,128]{1,0:T(8,128)S(1)}, u32[]{:S(2)}, u32[]{:S(2)}) collective-permute-start(f32[128,128]{1,0:T(8,128)S(1)} %ring.3.one), channel_id=1, source_target_pairs={{0,2},{1,3},{2,0},{3,1},{4,6},{5,7},{6,4},{7,5},{8,10},{9,11},{10,... | collective-permute-start | bytes 196616 | tf_op jit(solution)/shard_map/ppermute | solution.py:228
  55.4 4.3 %collective-permute-start.10 = (f32[128,128]{1,0:T(8,128)S(1)}, f32[128,128]{1,0:T(8,128)S(1)}, u32[]{:S(2)}, u32[]{:S(2)}) collective-permute-start(f32[128,128]{1,0:T(8,128)S(1)} %ring.3.one), channel_id=1, source_target_pairs={{0,1},{1,2},{2,3},{3,0},{4,5},{5,6},{6,7},{7,4},{8,9},{9,10},{10,1... | collective-permute-start | bytes 196616 | tf_op jit(solution)/shard_map/ppermute | solution.py:228
  61.5 5.5 %collective-permute-start.15 = (f32[72,128]{1,0:T(8,128)S(1)}, f32[72,128]{1,0:T(8,128)S(1)}, u32[]{:S(2)}, u32[]{:S(2)}) collective-permute-start(f32[72,128]{1,0:T(8,128)S(1)} %get-tuple-element.23.refs_0_.refs_4_), channel_id=1, source_target_pairs={{0,48},{1,49},{2,50},{3,51},{4,52},{5,53},{6,54},{7,55},{8,56},{9,... | collective-permute-start | bytes 110600 | tf_op jit(solution)/shard_map/ppermute | solution.py:228
  65.3 1.6 %collective-permute-start.14 = (f32[72,128]{1,0:T(8,128)S(1)}, f32[72,128]{1,0:T(8,128)S(1)}, u32[]{:S(2)}, u32[]{:S(2)}) collective-permute-start(f32[72,128]{1,0:T(8,128)S(1)} %get-tuple-element.23.refs_0_.refs_4_), channel_id=1, source_target_pairs={{0,16},{1,17},{2,18},{3,19},{4,20},{5,21},{6,22},{7,23},{8,24},{9,... | collective-permute-start | bytes 110600 | tf_op jit(solution)/shard_map/ppermute | solution.py:228
  65.3 3.0 %collective-permute-start.13 = (f32[72,128]{1,0:T(8,128)S(1)}, f32[72,128]{1,0:T(8,128)S(1)}, u32[]{:S(2)}, u32[]{:S(2)}) collective-permute-start(f32[72,128]{1,0:T(8,128)S(1)} %get-tuple-element.23.refs_0_.refs_4_), channel_id=1, source_target_pairs={{0,32},{1,33},{2,34},{3,35},{4,36},{5,37},{6,38},{7,39},{8,40},{9,... | collective-permute-start | bytes 110600 | tf_op jit(solution)/shard_map/ppermute | solution.py:228
  68.5 4.1 %collective-permute-start.18 = (f32[128,128]{1,0:T(8,128)S(1)}, f32[128,128]{1,0:T(8,128)S(1)}, u32[]{:S(2)}, u32[]{:S(2)}) collective-permute-start(f32[128,128]{1,0:T(8,128)S(1)} %pair.1), channel_id=1, source_target_pairs={{0,192},{1,193},{2,194},{3,195},{4,196},{5,197},{6,198},{7,199},{8... | collective-permute-start | bytes 196616 | tf_op jit(solution)/shard_map/ppermute | solution.py:228
  69.4 5.4 %collective-permute-start.17 = (f32[128,128]{1,0:T(8,128)S(1)}, f32[128,128]{1,0:T(8,128)S(1)}, u32[]{:S(2)}, u32[]{:S(2)}) collective-permute-start(f32[128,128]{1,0:T(8,128)S(1)} %pair.1), channel_id=1, source_target_pairs={{0,64},{1,65},{2,66},{3,67},{4,68},{5,69},{6,70},{7,71},{8,72},{9,... | collective-permute-start | bytes 196616 | tf_op jit(solution)/shard_map/ppermute | solution.py:228
  70.9 6.3 %collective-permute-start.16 = (f32[128,128]{1,0:T(8,128)S(1)}, f32[128,128]{1,0:T(8,128)S(1)}, u32[]{:S(2)}, u32[]{:S(2)}) collective-permute-start(f32[128,128]{1,0:T(8,128)S(1)} %pair.1), channel_id=1, source_target_pairs={{0,160},{1,161},{2,162},{3,163},{4,164},{5,165},{6,166},{7,167},{8... | collective-permute-start | bytes 196616 | tf_op jit(solution)/shard_map/ppermute | solution.py:228

commit v8 on v7

--- a/solution.py
+++ b/solution.py
@@ -243,8 +243,8 @@
 
 def pair_routes():
     return [
+        lambda z, core, x, y: (z, 1 - core, x, y),
         lambda z, core, x, y: (z ^ 1, core, x, y),
-        lambda z, core, x, y: (z, 1 - core, x, y),
         lambda z, core, x, y: (z ^ 1, 1 - core, x, y),
     ]
 

time: 79.6 us -> 78.5 us (0.986); the launches traced: 78 us -> 77.9 us
  waiting for transfers between devices: 22.8 us -> 23.8 us
  Pallas kernels: 9.65 us -> 8.78 us
    ppermute x18, waiting for transfers between devices: 21.9 us -> 22.9 us  [exchange(): got.append(lax.ppermute(value, ('z', 'core', 'col'), pairs))]
    pallas_call x8, Pallas kernels: 9.65 us -> 8.78 us  [call(): pl.pallas_call(kernel, name=name, out_shape=outs[0] if single else outs,...]
where the time goes in v8:
time: 78.5 us; the launch traced here: 77.9 us
  starting transfers between devices  25.6 us (33%)
  waiting for transfers between devices  23.8 us (30%)
  blocking collectives  17.5 us (22%)
  Pallas kernels  8.78 us (11%)
  between operations  1.41 us (2%)
    ppermute x18, waiting for transfers between devices, exchange(): got.append(lax.ppermute(value, ('z', 'core', 'col'), pairs))  22.9 us
    ppermute x18, starting transfers between devices, exchange(): got.append(lax.ppermute(value, ('z', 'core', 'col'), pairs))  21.2 us
    all_to_all x1, blocking collectives, to_all(): return lax.all_to_all(copies, axes, 0, 0, tiled=True)  17.5 us
    pallas_call x8, Pallas kernels, call(): pl.pallas_call(kernel, name=name, out_shape=outs[0] if single else outs,...  8.78 us
    ppermute x1, starting transfers between devices, local(): other = lax.ppermute(mine, 'core', [(0, 1), (1, 0)])  4.35 us
  transfers between devices with their start and end apart: 19, of which 17 were waited for; matrix products, arithmetic and copies ran while one was open for 0% of the time, Pallas kernels for 0%

profile of v8, /device:TPU:1, one launch (start us, length us, event | category | flops | bytes accessed | tf_op | source)
XLA Modules:
  0.0 77.9 jit_solution(4012221629876971123)
XLA Ops:
  1.3 2.6 %first_rows.1 = (f32[72,128]{1,0:T(8,128)S(1)}, f32[64,128,128]{2,1,0:T(8,128)S(1)}, s32[64,128]{1,0:T(8,128)S(1)}, f32[64,128]{1,0:T(8,128)S(1)}, f32[8,128]{1,...) custom-call(s32[64]{0:T(128)} %bitcast.15, s32[64]{0:T(128)} %bitcast.16, ...), custom_call_target="tpu_custom_call" | custom-call | tf_op jit(solution)/shard_map/first_rows/pallas_call | solution.py:206
  4.0 3.6 %collective-permute-start.2 = (f32[72,128]{1,0:T(8,128)S(1)}, f32[72,128]{1,0:T(8,128)S(1)}, u32[]{:S(2)}, u32[]{:S(2)}) collective-permute-start(f32[72,128]{1,0:T(8,128)S(1)} %get-tuple-element.13.refs_0_.refs_4_), channel_id=1, source_target_pairs={{0,12},{1,13},{2,14},{3,15},{4,0},{5,1},{6,2},{7,3},{8,4},{9,5},{1... | collective-permute-start | bytes 110600 | tf_op jit(solution)/shard_map/ppermute | solution.py:228
  7.9 0.8 collective-permute-start
  8.7 3.4 %collective-permute-done.1.refs_2_.refs_6_ = f32[72,128]{1,0:T(8,128)S(1)} collective-permute-done((f32[72,128]{1,0:T(8,128)S(1)}, f32[72,128]{1,0:T(8,128)S(1)}, u32[]{:S(2)}, u32[]{:S(2)}) %collective-permute-start.1) | collective-permute-done | bytes 36896 | tf_op jit(solution)/shard_map/ppermute | solution.py:228
  12.5 3.6 %collective-permute-start.5 = (f32[128,128]{1,0:T(8,128)S(1)}, f32[128,128]{1,0:T(8,128)S(1)}, u32[]{:S(2)}, u32[]{:S(2)}) collective-permute-start(f32[128,128]{1,0:T(8,128)S(1)} %ring.2.one), channel_id=1, source_target_pairs={{0,3},{1,0},{2,1},{3,2},{4,7},{5,4},{6,5},{7,6},{8,11},{9,8},{10,9... | collective-permute-start | bytes 196616 | tf_op jit(solution)/shard_map/ppermute | solution.py:228
  16.1 0.6 collective-permute-start.4
  16.8 0.7 collective-permute-done.5.four
  17.5 3.3 %collective-permute-done.4.three = f32[128,128]{1,0:T(8,128)S(1)} collective-permute-done((f32[128,128]{1,0:T(8,128)S(1)}, f32[128,128]{1,0:T(8,128)S(1)}, u32[]{:S(2)}, u32[]{:S(2)}) %collective-permute-start.4) | collective-permute-done | bytes 65568 | tf_op jit(solution)/shard_map/ppermute | solution.py:228
  20.8 0.7 collective-permute-done.3.two
  21.4 1.7 %cols_half.2 = (f32[128,128]{1,0:T(8,128)}, f32[72,128]{1,0:T(8,128)S(1)}) custom-call(f32[128,128]{1,0:T(8,128)S(1)} %ring.2.one, f32[128,128]{1,0:T(8,128)S(1)} %collective-permute-done.3.two, f32[128,128]{1,0:T(8,128)S(1)} %collective-permute-done.4.three, f32[128,128]{1,0:T(8,128)S(1)} %collective-permute-done.5.four, f32[128,128]{1,0:T(8,128)S(1)} %bitcast.10, ...), custom_call_target="tpu_custom_call" | custom-call | tf_op jit(solution)/shard_map/cols_half/pallas_call | solution.py:206
  23.2 17.5 %all_to_all.5.parts.names = f32[8,72,128]{2,1,0:T(8,128)S(1)} all-to-all(f32[8,72,128]{2,1,0:T(8,128)S(1)} %broadcast_in_dim.2), channel_id=1, replica_groups=mesh['z'=8,'core'=2,'col'=16] {'z'}, dimensions={0} | all-to-all | bytes 589824 | tf_op jit(solution)/shard_map/all_to_all | solution.py:262
  41.1 4.3 %collective-permute-start.6 = (f32[128,128]{1,0:T(8,128)S(1)}, f32[128,128]{1,0:T(8,128)S(1)}, u32[]{:S(2)}, u32[]{:S(2)}) collective-permute-start(f32[128,128]{1,0:T(8,128)S(1)} %spread.1.mine), channel_id=1, source_target_pairs={{0,16},{16,0},{1,17},{17,1},{2,18},{18,2},{3,19},{19,3},{4,20},{20... | collective-permute-start | bytes 196616 | tf_op jit(solution)/shard_map/ppermute | solution.py:329
  45.4 0.9 %collective-permute-done.6.other = f32[128,128]{1,0:T(8,128)S(1)} collective-permute-done((f32[128,128]{1,0:T(8,128)S(1)}, f32[128,128]{1,0:T(8,128)S(1)}, u32[]{:S(2)}, u32[]{:S(2)}) %collective-permute-start.6) | collective-permute-done | bytes 65568 | tf_op jit(solution)/shard_map/ppermute | solution.py:329
  46.3 1.6 %rows_half.1.refs_0_ = f32[64,128]{1,0:T(8,128)S(1)} custom-call(f32[128,128]{1,0:T(8,128)S(1)} %spread.1.mine, f32[128,128]{1,0:T(8,128)S(1)} %collective-permute-done.6.other, f32[128,128]{1,0:T(8,128)S(1)} %bitcast.12, f32[64,128,128]{2,1,0:T(8,128)S(1)} %get-tuple-element.14.cost, s32[64,128]{1,0:T(8,128)S(1)} %get-tuple-element.15.row_up, ...), custom_call_target="tpu_custom_call" | custom-call | tf_op jit(solution)/shard_map/rows_half/pallas_call | solution.py:206
  48.5 0.7 collective-permute-start.8
  49.2 0.8 collective-permute-start.7
  50.0 0.8 %collective-permute-done.9.refs_3_ = f32[64,128]{1,0:T(8,128)S(1)} collective-permute-done((f32[64,128]{1,0:T(8,128)S(1)}, f32[64,128]{1,0:T(8,128)S(1)}, u32[]{:S(2)}, u32[]{:S(2)}) %collective-permute-start.9) | collective-permute-done | bytes 32800 | tf_op jit(solution)/shard_map/ppermute | solution.py:228
  50.8 2.0 %collective-permute-done.8.refs_2_ = f32[64,128]{1,0:T(8,128)S(1)} collective-permute-done((f32[64,128]{1,0:T(8,128)S(1)}, f32[64,128]{1,0:T(8,128)S(1)}, u32[]{:S(2)}, u32[]{:S(2)}) %collective-permute-start.8) | collective-permute-done | bytes 32800 | tf_op jit(solution)/shard_map/ppermute | solution.py:228
  54.0 1.1 %collective-permute-start.11 = (f32[128,128]{1,0:T(8,128)S(1)}, f32[128,128]{1,0:T(8,128)S(1)}, u32[]{:S(2)}, u32[]{:S(2)}) collective-permute-start(f32[128,128]{1,0:T(8,128)S(1)} %ring.3.one), channel_id=1, source_target_pairs={{0,2},{1,3},{2,0},{3,1},{4,6},{5,7},{6,4},{7,5},{8,10},{9,11},{10,... | collective-permute-start | bytes 196616 | tf_op jit(solution)/shard_map/ppermute | solution.py:228
  55.7 1.0 %collective-permute-done.12.four = f32[128,128]{1,0:T(8,128)S(1)} collective-permute-done((f32[128,128]{1,0:T(8,128)S(1)}, f32[128,128]{1,0:T(8,128)S(1)}, u32[]{:S(2)}, u32[]{:S(2)}) %collective-permute-start.12) | collective-permute-done | bytes 65568 | tf_op jit(solution)/shard_map/ppermute | solution.py:228
  56.7 2.0 %collective-permute-done.11.three = f32[128,128]{1,0:T(8,128)S(1)} collective-permute-done((f32[128,128]{1,0:T(8,128)S(1)}, f32[128,128]{1,0:T(8,128)S(1)}, u32[]{:S(2)}, u32[]{:S(2)}) %collective-permute-start.11) | collective-permute-done | bytes 65568 | tf_op jit(solution)/shard_map/ppermute | solution.py:228
  58.6 0.8 %collective-permute-done.10.two = f32[128,128]{1,0:T(8,128)S(1)} collective-permute-done((f32[128,128]{1,0:T(8,128)S(1)}, f32[128,128]{1,0:T(8,128)S(1)}, u32[]{:S(2)}, u32[]{:S(2)}) %collective-permute-start.10) | collective-permute-done | bytes 65568 | tf_op jit(solution)/shard_map/ppermute | solution.py:228
  59.4 1.7 %cols_half.3 = (f32[128,128]{1,0:T(8,128)}, f32[72,128]{1,0:T(8,128)S(1)}) custom-call(f32[128,128]{1,0:T(8,128)S(1)} %ring.3.one, f32[128,128]{1,0:T(8,128)S(1)} %collective-permute-done.10.two, f32[128,128]{1,0:T(8,128)S(1)} %collective-permute-done.11.three, f32[128,128]{1,0:T(8,128)S(1)} %collective-permute-done.12.four, f32[128,128]{1,0:T(8,128)S(1)} %bitcast.11, ...), custom_call_target="tpu_custom_call" | custom-call | tf_op jit(solution)/shard_map/cols_half/pallas_call | solution.py:206
  61.1 3.8 %collective-permute-start.15 = (f32[72,128]{1,0:T(8,128)S(1)}, f32[72,128]{1,0:T(8,128)S(1)}, u32[]{:S(2)}, u32[]{:S(2)}) collective-permute-start(f32[72,128]{1,0:T(8,128)S(1)} %get-tuple-element.23.refs_0_.refs_4_), channel_id=1, source_target_pairs={{0,48},{1,49},{2,50},{3,51},{4,52},{5,53},{6,54},{7,55},{8,56},{9,... | collective-permute-start | bytes 110600 | tf_op jit(solution)/shard_map/ppermute | solution.py:228
  65.0 1.2 %collective-permute-start.14 = (f32[72,128]{1,0:T(8,128)S(1)}, f32[72,128]{1,0:T(8,128)S(1)}, u32[]{:S(2)}, u32[]{:S(2)}) collective-permute-start(f32[72,128]{1,0:T(8,128)S(1)} %get-tuple-element.23.refs_0_.refs_4_), channel_id=1, source_target_pairs={{0,32},{1,33},{2,34},{3,35},{4,36},{5,37},{6,38},{7,39},{8,40},{9,... | collective-permute-start | bytes 110600 | tf_op jit(solution)/shard_map/ppermute | solution.py:228
  66.6 1.7 %collective-permute-done.14.refs_2_.refs_6_ = f32[72,128]{1,0:T(8,128)S(1)} collective-permute-done((f32[72,128]{1,0:T(8,128)S(1)}, f32[72,128]{1,0:T(8,128)S(1)}, u32[]{:S(2)}, u32[]{:S(2)}) %collective-permute-start.14) | collective-permute-done | bytes 36896 | tf_op jit(solution)/shard_map/ppermute | solution.py:228
  69.1 1.9 %collective-permute-start.17 = (f32[128,128]{1,0:T(8,128)S(1)}, f32[128,128]{1,0:T(8,128)S(1)}, u32[]{:S(2)}, u32[]{:S(2)}) collective-permute-start(f32[128,128]{1,0:T(8,128)S(1)} %pair.1), channel_id=1, source_target_pairs={{0,64},{1,65},{2,66},{3,67},{4,68},{5,69},{6,70},{7,71},{8,72},{9,... | collective-permute-start | bytes 196616 | tf_op jit(solution)/shard_map/ppermute | solution.py:228
  71.0 0.6 collective-permute-start.16
  71.6 2.3 %collective-permute-done.18 = f32[128,128]{1,0:T(8,128)S(1)} collective-permute-done((f32[128,128]{1,0:T(8,128)S(1)}, f32[128,128]{1,0:T(8,128)S(1)}, u32[]{:S(2)}, u32[]{:S(2)}) %collective-permute-start.18) | collective-permute-done | bytes 65568 | tf_op jit(solution)/shard_map/ppermute | solution.py:228
  73.9 0.8 %collective-permute-done.17 = f32[128,128]{1,0:T(8,128)S(1)} collective-permute-done((f32[128,128]{1,0:T(8,128)S(1)}, f32[128,128]{1,0:T(8,128)S(1)}, u32[]{:S(2)}, u32[]{:S(2)}) %collective-permute-start.17) | collective-permute-done | bytes 65568 | tf_op jit(solution)/shard_map/ppermute | solution.py:228
  74.7 2.4 %collective-permute-done.16 = f32[128,128]{1,0:T(8,128)S(1)} collective-permute-done((f32[128,128]{1,0:T(8,128)S(1)}, f32[128,128]{1,0:T(8,128)S(1)}, u32[]{:S(2)}, u32[]{:S(2)}) %collective-permute-start.16) | collective-permute-done | bytes 65568 | tf_op jit(solution)/shard_map/ppermute | solution.py:228
  77.1 0.7 subtract_bitcast_fusion
  (21 shorter events, 4.9 us)
Async XLA Ops:
  0.6 20.8 %copy-start = (f32[16384]{0:T(1024)S(1)}, f32[16384]{0:T(1024)}, u32[]{:S(2)}) copy-start(f32[16384]{0:T(1024)} %param.11) | copy-start | bytes 196612
  4.0 42.4 %copy-start.1 = (f32[16384]{0:T(1024)S(1)}, f32[16384]{0:T(1024)}, u32[]{:S(2)}) copy-start(f32[16384]{0:T(1024)} %param.12) | copy-start | bytes 196612
  4.0 4.7 %collective-permute-start.2 = (f32[72,128]{1,0:T(8,128)S(1)}, f32[72,128]{1,0:T(8,128)S(1)}, u32[]{:S(2)}, u32[]{:S(2)}) collective-permute-start(f32[72,128]{1,0:T(8,128)S(1)} %get-tuple-element.13.refs_0_.refs_4_), channel_id=1, source_target_pairs={{0,12},{1,13},{2,14},{3,15},{4,0},{5,1},{6,2},{7,3},{8,4},{9,5},{1... | collective-permute-start | bytes 110600 | tf_op jit(solution)/shard_map/ppermute | solution.py:228
  7.6 4.4 %collective-permute-start.1 = (f32[72,128]{1,0:T(8,128)S(1)}, f32[72,128]{1,0:T(8,128)S(1)}, u32[]{:S(2)}, u32[]{:S(2)}) collective-permute-start(f32[72,128]{1,0:T(8,128)S(1)} %get-tuple-element.13.refs_0_.refs_4_), channel_id=1, source_target_pairs={{0,8},{1,9},{2,10},{3,11},{4,12},{5,13},{6,14},{7,15},{8,0},{9,1},... | collective-permute-start | bytes 110600 | tf_op jit(solution)/shard_map/ppermute | solution.py:228
  7.9 4.4 %collective-permute-start = (f32[72,128]{1,0:T(8,128)S(1)}, f32[72,128]{1,0:T(8,128)S(1)}, u32[]{:S(2)}, u32[]{:S(2)}) collective-permute-start(f32[72,128]{1,0:T(8,128)S(1)} %get-tuple-element.13.refs_0_.refs_4_), channel_id=1, source_target_pairs={{0,4},{1,5},{2,6},{3,7},{4,8},{5,9},{6,10},{7,11},{8,12},{9,13},{1... | collective-permute-start | bytes 110600 | tf_op jit(solution)/shard_map/ppermute | solution.py:228
  12.5 4.9 %collective-permute-start.5 = (f32[128,128]{1,0:T(8,128)S(1)}, f32[128,128]{1,0:T(8,128)S(1)}, u32[]{:S(2)}, u32[]{:S(2)}) collective-permute-start(f32[128,128]{1,0:T(8,128)S(1)} %ring.2.one), channel_id=1, source_target_pairs={{0,3},{1,0},{2,1},{3,2},{4,7},{5,4},{6,5},{7,6},{8,11},{9,8},{10,9... | collective-permute-start | bytes 196616 | tf_op jit(solution)/shard_map/ppermute | solution.py:228
  16.1 4.7 %collective-permute-start.4 = (f32[128,128]{1,0:T(8,128)S(1)}, f32[128,128]{1,0:T(8,128)S(1)}, u32[]{:S(2)}, u32[]{:S(2)}) collective-permute-start(f32[128,128]{1,0:T(8,128)S(1)} %ring.2.one), channel_id=1, source_target_pairs={{0,2},{1,3},{2,0},{3,1},{4,6},{5,7},{6,4},{7,5},{8,10},{9,11},{10,... | collective-permute-start | bytes 196616 | tf_op jit(solution)/shard_map/ppermute | solution.py:228
  16.7 4.7 %collective-permute-start.3 = (f32[128,128]{1,0:T(8,128)S(1)}, f32[128,128]{1,0:T(8,128)S(1)}, u32[]{:S(2)}, u32[]{:S(2)}) collective-permute-start(f32[128,128]{1,0:T(8,128)S(1)} %ring.2.one), channel_id=1, source_target_pairs={{0,1},{1,2},{2,3},{3,0},{4,5},{5,6},{6,7},{7,4},{8,9},{9,10},{10,1... | collective-permute-start | bytes 196616 | tf_op jit(solution)/shard_map/ppermute | solution.py:228
  41.1 5.3 %collective-permute-start.6 = (f32[128,128]{1,0:T(8,128)S(1)}, f32[128,128]{1,0:T(8,128)S(1)}, u32[]{:S(2)}, u32[]{:S(2)}) collective-permute-start(f32[128,128]{1,0:T(8,128)S(1)} %spread.1.mine), channel_id=1, source_target_pairs={{0,16},{16,0},{1,17},{17,1},{2,18},{18,2},{3,19},{19,3},{4,20},{20... | collective-permute-start | bytes 196616 | tf_op jit(solution)/shard_map/ppermute | solution.py:329
  48.0 2.8 %collective-permute-start.9 = (f32[64,128]{1,0:T(8,128)S(1)}, f32[64,128]{1,0:T(8,128)S(1)}, u32[]{:S(2)}, u32[]{:S(2)}) collective-permute-start(f32[64,128]{1,0:T(8,128)S(1)} %rows_half.1.refs_0_), channel_id=1, source_target_pairs={{0,12},{1,13},{2,14},{3,15},{4,0},{5,1},{6,2},{7,3},{8,4},{9,5},{1... | collective-permute-start | bytes 98312 | tf_op jit(solution)/shard_map/ppermute | solution.py:228
  48.5 4.3 %collective-permute-start.8 = (f32[64,128]{1,0:T(8,128)S(1)}, f32[64,128]{1,0:T(8,128)S(1)}, u32[]{:S(2)}, u32[]{:S(2)}) collective-permute-start(f32[64,128]{1,0:T(8,128)S(1)} %rows_half.1.refs_0_), channel_id=1, source_target_pairs={{0,8},{1,9},{2,10},{3,11},{4,12},{5,13},{6,14},{7,15},{8,0},{9,1},... | collective-permute-start | bytes 98312 | tf_op jit(solution)/shard_map/ppermute | solution.py:228
  49.2 4.0 %collective-permute-start.7 = (f32[64,128]{1,0:T(8,128)S(1)}, f32[64,128]{1,0:T(8,128)S(1)}, u32[]{:S(2)}, u32[]{:S(2)}) collective-permute-start(f32[64,128]{1,0:T(8,128)S(1)} %rows_half.1.refs_0_), channel_id=1, source_target_pairs={{0,4},{1,5},{2,6},{3,7},{4,8},{5,9},{6,10},{7,11},{8,12},{9,13},{1... | collective-permute-start | bytes 98312 | tf_op jit(solution)/shard_map/ppermute | solution.py:228
  53.5 3.2 %collective-permute-start.12 = (f32[128,128]{1,0:T(8,128)S(1)}, f32[128,128]{1,0:T(8,128)S(1)}, u32[]{:S(2)}, u32[]{:S(2)}) collective-permute-start(f32[128,128]{1,0:T(8,128)S(1)} %ring.3.one), channel_id=1, source_target_pairs={{0,3},{1,0},{2,1},{3,2},{4,7},{5,4},{6,5},{7,6},{8,11},{9,8},{10,9... | collective-permute-start | bytes 196616 | tf_op jit(solution)/shard_map/ppermute | solution.py:228
  54.0 4.6 %collective-permute-start.11 = (f32[128,128]{1,0:T(8,128)S(1)}, f32[128,128]{1,0:T(8,128)S(1)}, u32[]{:S(2)}, u32[]{:S(2)}) collective-permute-start(f32[128,128]{1,0:T(8,128)S(1)} %ring.3.one), channel_id=1, source_target_pairs={{0,2},{1,3},{2,0},{3,1},{4,6},{5,7},{6,4},{7,5},{8,10},{9,11},{10,... | collective-permute-start | bytes 196616 | tf_op jit(solution)/shard_map/ppermute | solution.py:228
  55.1 4.3 %collective-permute-start.10 = (f32[128,128]{1,0:T(8,128)S(1)}, f32[128,128]{1,0:T(8,128)S(1)}, u32[]{:S(2)}, u32[]{:S(2)}) collective-permute-start(f32[128,128]{1,0:T(8,128)S(1)} %ring.3.one), channel_id=1, source_target_pairs={{0,1},{1,2},{2,3},{3,0},{4,5},{5,6},{6,7},{7,4},{8,9},{9,10},{10,1... | collective-permute-start | bytes 196616 | tf_op jit(solution)/shard_map/ppermute | solution.py:228
  61.1 5.5 %collective-permute-start.15 = (f32[72,128]{1,0:T(8,128)S(1)}, f32[72,128]{1,0:T(8,128)S(1)}, u32[]{:S(2)}, u32[]{:S(2)}) collective-permute-start(f32[72,128]{1,0:T(8,128)S(1)} %get-tuple-element.23.refs_0_.refs_4_), channel_id=1, source_target_pairs={{0,48},{1,49},{2,50},{3,51},{4,52},{5,53},{6,54},{7,55},{8,56},{9,... | collective-permute-start | bytes 110600 | tf_op jit(solution)/shard_map/ppermute | solution.py:228
  65.0 3.3 %collective-permute-start.14 = (f32[72,128]{1,0:T(8,128)S(1)}, f32[72,128]{1,0:T(8,128)S(1)}, u32[]{:S(2)}, u32[]{:S(2)}) collective-permute-start(f32[72,128]{1,0:T(8,128)S(1)} %get-tuple-element.23.refs_0_.refs_4_), channel_id=1, source_target_pairs={{0,32},{1,33},{2,34},{3,35},{4,36},{5,37},{6,38},{7,39},{8,40},{9,... | collective-permute-start | bytes 110600 | tf_op jit(solution)/shard_map/ppermute | solution.py:228
  66.2 2.1 %collective-permute-start.13 = (f32[72,128]{1,0:T(8,128)S(1)}, f32[72,128]{1,0:T(8,128)S(1)}, u32[]{:S(2)}, u32[]{:S(2)}) collective-permute-start(f32[72,128]{1,0:T(8,128)S(1)} %get-tuple-element.23.refs_0_.refs_4_), channel_id=1, source_target_pairs={{0,16},{1,17},{2,18},{3,19},{4,20},{5,21},{6,22},{7,23},{8,24},{9,... | collective-permute-start | bytes 110600 | tf_op jit(solution)/shard_map/ppermute | solution.py:228
  68.6 5.4 %collective-permute-start.18 = (f32[128,128]{1,0:T(8,128)S(1)}, f32[128,128]{1,0:T(8,128)S(1)}, u32[]{:S(2)}, u32[]{:S(2)}) collective-permute-start(f32[128,128]{1,0:T(8,128)S(1)} %pair.1), channel_id=1, source_target_pairs={{0,192},{1,193},{2,194},{3,195},{4,196},{5,197},{6,198},{7,199},{8... | collective-permute-start | bytes 196616 | tf_op jit(solution)/shard_map/ppermute | solution.py:228
  69.1 5.6 %collective-permute-start.17 = (f32[128,128]{1,0:T(8,128)S(1)}, f32[128,128]{1,0:T(8,128)S(1)}, u32[]{:S(2)}, u32[]{:S(2)}) collective-permute-start(f32[128,128]{1,0:T(8,128)S(1)} %pair.1), channel_id=1, source_target_pairs={{0,64},{1,65},{2,66},{3,67},{4,68},{5,69},{6,70},{7,71},{8,72},{9,... | collective-permute-start | bytes 196616 | tf_op jit(solution)/shard_map/ppermute | solution.py:228
  71.0 6.1 %collective-permute-start.16 = (f32[128,128]{1,0:T(8,128)S(1)}, f32[128,128]{1,0:T(8,128)S(1)}, u32[]{:S(2)}, u32[]{:S(2)}) collective-permute-start(f32[128,128]{1,0:T(8,128)S(1)} %pair.1), channel_id=1, source_target_pairs={{0,160},{1,161},{2,162},{3,163},{4,164},{5,165},{6,166},{7,167},{8... | collective-permute-start | bytes 196616 | tf_op jit(solution)/shard_map/ppermute | solution.py:228
